TPU v7x, 32 devices: a whole 2x2x4 slice. The times are simulated.
32 devices in a mesh: pano: 2 (over y), blk: 8 (over z, x), rows: 2 (over core).
Axes of the slice: x: 2, y: 2, z: 4, core: 2. Of those that a mesh axis runs over, the one named last changes fastest.
Arguments:
- latent: float32 [16, 256, 640], P(('pano', 'rows'), 'blk'), parts along dimension 0, may hold values from -6 to 6
- offset: int32 [2], P('pano'), parts along dimension 0, may hold values from 0 to 31
- counts: int32 [16, 64], P(('pano', 'blk')), parts along dimension 0, may hold values from 1 to 4
- conv_one: bfloat16 [3, 3, 640, 640], P(None, None, None, 'rows'), may hold values from -0.078125 to 0.078125
- conv_two: bfloat16 [3, 3, 640, 640], P(None, None, None, 'rows'), may hold values from -0.078125 to 0.078125
- gain_one: float32 [640], replicated, may hold values from 0.1 to 1.9
- gain_two: float32 [640], replicated, may hold values from 0.1 to 1.9
- time_bias: float32 [640], replicated, may hold values from -6 to 6
Outputs:
- new_latent: float32 [16, 256, 640], P(('pano', 'rows'), 'blk'), parts along dimension 0
There are 2 independent parts, one for each index of `pano`. A program takes and returns all parts, laid end to end along the dimension named above; an argument that names none is the same for every part. Nothing has to cross between parts.
All inputs are finite; a program needn't handle non-finite values.
Results may differ from a plain program's by a relative error of at most 0.0014.
Values may be sent and summed in bfloat16 or wider, within the bound.
No kernel may reach another device: no remote copies, remote signals or barrier semaphores. Data moves between devices by JAX's collectives and lax.ppermute only.
A program may use at most 64 MiB of HBM per device.

v0:
```python
import math

import jax
import jax.numpy as jnp
from jax import lax
from jax.sharding import PartitionSpec as P

GROUPS = 32


def from_behind(value, axis, steps):
    count = lax.axis_size(axis)
    pairs = [(source, (source + steps) % count) for source in range(count)]
    return lax.ppermute(value, axis, pairs)


def nine_taps(framed, weight, height, columns):
    total = jnp.zeros((height * columns, weight.shape[3]), jnp.float32)
    for row_tap in range(3):
        for col_tap in range(3):
            patch = framed[row_tap : row_tap + height, col_tap : col_tap + columns]
            patch = patch.reshape(height * columns, framed.shape[2])
            total = total + jnp.dot(
                patch, weight[row_tap, col_tap], preferred_element_type=jnp.float32
            )
    return total


def group_moments(values, size):
    grouped = values.reshape(values.shape[0], values.shape[1], values.shape[2] // size, size)
    return (jnp.sum(grouped, axis=(0, 1, 3)), jnp.sum(grouped * grouped, axis=(0, 1, 3)))


def normalize(values, summed, squares, count, gain, size):
    grouped = values.reshape(values.shape[0], values.shape[1], values.shape[2] // size, size)
    mean = summed / count
    square = squares / count
    scale = lax.rsqrt(square - mean * mean + 1e-05)
    normed = ((grouped - mean[:, None]) * scale[:, None]).reshape(values.shape) * gain
    return jax.nn.silu(normed).astype(jnp.bfloat16)


def denoise_local(window, conv_one, conv_two, gain_one, gain_two, time_bias):
    whole = lax.all_gather(window, "rows", axis=0, tiled=True)
    height, columns, channels = whole.shape
    half = conv_one.shape[3]
    first = lax.axis_index("rows") * half
    size = channels // GROUPS
    source = whole.astype(jnp.float32)
    summed, squares = group_moments(source, size)
    act_one = normalize(source, summed, squares, height * columns * size, gain_one, size)
    framed = jnp.pad(act_one, ((1, 1), (1, 1), (0, 0)))
    hidden = nine_taps(framed, conv_one, height, columns).reshape(height, columns, half)
    hidden = hidden + lax.dynamic_slice_in_dim(time_bias, first, half)
    summed, squares = group_moments(hidden, size)
    gain_part = lax.dynamic_slice_in_dim(gain_two, first, half)
    act_two = normalize(hidden, summed, squares, height * columns * size, gain_part, size)
    framed_piece = jnp.pad(
        lax.all_gather(act_two, "rows", axis=2, tiled=True), ((1, 1), (1, 1), (0, 0))
    )
    summed_conv = nine_taps(framed_piece, conv_two, height, columns)
    result = lax.dynamic_slice_in_dim(source, first, half, 2) + summed_conv.reshape(
        height, columns, half
    )
    return lax.all_to_all(result, "rows", split_axis=0, concat_axis=2, tiled=True)


def per_device(latent, offset, counts, conv_one, conv_two, gain_one, gain_two, time_bias):
    anchor = offset[0]
    stride = latent.shape[1]
    lowered = latent.astype(jnp.bfloat16)
    after = from_behind(lowered, "blk", -1)
    beyond = from_behind(lowered, "blk", -2)
    strip = jnp.concatenate([lowered, after, beyond], axis=1)
    weights_row = counts[0]
    window = lax.dynamic_slice_in_dim(strip, anchor, 2 * stride, 1)
    prediction = denoise_local(window, conv_one, conv_two, gain_one, gain_two, time_bias)
    weight = weights_row.astype(jnp.float32)
    numer = jnp.zeros((latent.shape[0], 3 * stride, latent.shape[2]), jnp.float32)
    numer = lax.dynamic_update_slice_in_dim(numer, prediction * weight[None, :, None], anchor, 1)
    denom = lax.dynamic_update_slice_in_dim(
        jnp.zeros((3 * stride,), jnp.float32), weight, anchor, 0
    )
    from_one = (
        from_behind(numer[:, stride : 2 * stride].astype(jnp.bfloat16), "blk", 1).astype(
            jnp.float32
        ),
        from_behind(denom[stride : 2 * stride].astype(jnp.bfloat16), "blk", 1).astype(jnp.float32),
    )
    from_two = (
        from_behind(numer[:, 2 * stride :].astype(jnp.bfloat16), "blk", 2).astype(jnp.float32),
        from_behind(denom[2 * stride :].astype(jnp.bfloat16), "blk", 2).astype(jnp.float32),
    )
    total = numer[:, :stride] + from_one[0] + from_two[0]
    weight_sum = denom[:stride] + from_one[1] + from_two[1]
    joined = total / weight_sum[None, :, None]
    return math.sqrt(0.7 / 0.5) * (latent - math.sqrt(0.5) * joined) + math.sqrt(0.3) * joined


def solution(mesh):
    return jax.shard_map(
        per_device,
        mesh=mesh,
        in_specs=(
            P(("pano", "rows"), "blk", None),
            P("pano"),
            P(("pano", "blk"), None),
            P(None, None, None, "rows"),
            P(None, None, None, "rows"),
            P(),
            P(),
            P(),
        ),
        out_specs=P(("pano", "rows"), "blk", None),
        check_vma=False,
    )
```

profile of v0, /device:TPU:2, one launch (start us, length us, event | category | flops | bytes accessed | tf_op | source)
XLA Modules:
  0.0 54.4 jit_solution(9921348887715218666)
XLA Ops:
  0.0 1.0 %convert_element_type.41 = bf16[4,32,640]{2,1,0:T(8,128)(2,1)S(1)} convert(f32[4,32,640]{2,1,0:T(8,128)} %param.8) | non-fusion elementwise | flops 81920 | bytes 491520 | tf_op jit(solution)/shard_map/convert_element_type | solution.py:71
  1.1 4.1 %collective-permute-start.1 = (bf16[4,32,640]{2,1,0:T(8,128)(2,1)S(1)}, bf16[4,32,640]{2,1,0:T(8,128)(2,1)S(1)}, u32[]{:S(2)}, u32[]{:S(2)}) collective-permute-start(bf16[4,32,640]{2,1,0:T(8,128)(2,1)S(1)} %convert_element_type.41), channel_id=1, source_target_pairs={{0,12},{2,14},{4,0},{6,2},{8,4},{10,6},{12,8},{14,10},{1,13},{3,15... | collective-permute-start | bytes 491528 | tf_op jit(solution)/shard_map/ppermute | solution.py:14
  5.9 0.8 %fusion.42 = f32[96]{0:T(128)S(1)} fusion(f32[96]{0:T(128)S(1)} %broadcast_in_dim.5, s32[]{:T(128)S(6)} %select_n.4, s32[1,64]{1,0:T(1,128)} %param.10), kind=kLoop, calls=%fused_computation.93 | loop fusion | flops 64 | bytes 644 | tf_op jit(solution)/shard_map/dynamic_update_slice | solution.py:81
  6.7 2.4 %collective-permute-start.4 = (bf16[32]{0:T(256)(128)(2,1)S(1)}, bf16[32]{0:T(256)(128)(2,1)S(1)}, u32[]{:S(2)}, u32[]{:S(2)}) collective-permute-start(bf16[32]{0:T(256)(128)(2,1)S(1)} %get-tuple-element.27), channel_id=1, source_target_pairs={{0,2},{2,4},{4,6},{6,8},{8,10},{10,12},{12,14},{14,0},{1,3},{3,5},... | collective-permute-start | bytes 200 | tf_op jit(solution)/shard_map/ppermute | solution.py:14
  9.1 0.8 %dynamic_slice.14 = f32[320]{0:T(512)S(1)} dynamic-slice(f32[640]{0:T(1024)} %param.15, s32[]{:T(128)S(6)} %select_n.5), dynamic_slice_sizes={320} | dynamic-slice | bytes 2564 | tf_op jit(solution)/shard_map/dynamic_slice | solution.py:54
  9.9 0.8 %dynamic_slice.15 = f32[320]{0:T(512)S(1)} dynamic-slice(f32[640]{0:T(1024)} %param.14, s32[]{:T(128)S(6)} %select_n.5), dynamic_slice_sizes={320} | dynamic-slice | bytes 2564 | tf_op jit(solution)/shard_map/dynamic_slice | solution.py:56
  10.6 0.7 %convert_bitcast_fusion = f32[64]{0:T(128)S(1)} fusion(s32[1,64]{1,0:T(1,128)} %param.10), kind=kLoop, calls=%fused_computation.88 | loop fusion | flops 64 | bytes 512 | tf_op jit(solution)/shard_map/convert_element_type | solution.py:78
  11.6 2.3 %all_gather.6 = bf16[8,64,640]{2,1,0:T(8,128)(2,1)S(1)} all-gather(bf16[4,64,640]{2,1,0:T(8,128)(2,1)S(1)} %fusion.39), channel_id=1, replica_groups=mesh['pano'=2,'blk'=8,'rows'=2] {'rows'}, dimensions={0}, use_global_device_ids=true | all-gather | bytes 983040 | tf_op jit(solution)/shard_map/all_gather | solution.py:44
  15.4 0.8 %pad_slice_fusion.8 = (bf16[8,64,640]{2,1,0:T(8,128)(2,1)S(1)}, bf16[8,64,640]{2,1,0:T(8,128)(2,1)S(1)}, bf16[8,64,640]{2,1,0:T(8,128)(2,1)S(1)}, bf16[8,64,640]...) fusion(bf16[8,64,640]{2,1,0:T(8,128)(2,1)S(1)} %multiply_conver, ...), kind=kLoop, calls=%fused_computation.26 | loop fusion | bytes 5898240 | tf_op jit(solution)/shard_map/slice | solution.py:21
  16.2 0.8 %copy-done.1 = bf16[3,3,640,320]{2,3,1,0:T(8,128)(2,1)S(1)} copy-done((bf16[3,3,640,320]{2,3,1,0:T(8,128)(2,1)S(1)}, bf16[3,3,640,320]{2,3,1,0:T(8,128)(2,1)}, u32[]{:S(2)}) %copy-start.1) | copy-done | bytes 3686424
  17.5 0.4 convolution_add_fusion.15
  17.9 0.4 convolution_add_fusion.14
  18.4 0.4 convolution_add_fusion.13
  18.9 0.4 convolution_add_fusion.12
  20.7 0.6 %add_reduce_fusion = (f32[320]{0:T(512)S(1)}, f32[320]{0:T(512)S(1)}, f32[512,320]{0,1:T(8,128)S(1)}) fusion(f32[320]{0:T(512)S(1)} %dynamic_slice.14, f32[512,320]{0,1:T(8,128)S(1)} %convolution_add_fusion.9, bf16[512,640]{1,0:T(8,128)(2,1)S(1)} %bitcast.125, bf16[3,3,640,320]{2,3,1,0:T(8,128)(2,1)S(1)} %copy-done.1), kind=kOutput, calls=%fused_computation.38 | convolution fusion | flops 210533760 | bytes 2380288 | tf_op jit(solution)/shard_map/dot_general | solution.py:23
  23.0 2.7 %all_gather.7 = bf16[8,64,640]{1,0,2:T(8,128)(2,1)S(1)} all-gather(bf16[8,64,320]{1,0,2:T(8,128)(2,1)S(1)} %copy.21), channel_id=1, replica_groups=mesh['pano'=2,'blk'=8,'rows'=2] {'rows'}, dimensions={2}, use_global_device_ids=true | all-gather | bytes 983040 | tf_op jit(solution)/shard_map/all_gather | solution.py:59
  25.8 1.2 %copy.22 = bf16[8,64,640]{2,1,0:T(8,128)(2,1)S(1)} copy(bf16[8,64,640]{1,0,2:T(8,128)(2,1)S(1)} %all_gather.7) | data formatting | bytes 1310720 | tf_op jit(solution)/shard_map/all_gather | solution.py:59
  27.0 0.7 %pad_slice_fusion = (bf16[8,64,640]{2,1,0:T(8,128)(2,1)S(1)}, bf16[8,64,640]{2,1,0:T(8,128)(2,1)S(1)}, bf16[8,64,640]{2,1,0:T(8,128)(2,1)S(1)}, bf16[8,64,640]{2...) fusion(bf16[8,64,640]{2,1,0:T(8,128)(2,1)S(1)} %copy.22), kind=kLoop, calls=%fused_computation.18 | loop fusion | bytes 5898240 | tf_op jit(solution)/shard_map/slice | solution.py:21
  27.8 1.3 %copy-done = bf16[3,3,640,320]{2,3,1,0:T(8,128)(2,1)S(1)} copy-done((bf16[3,3,640,320]{2,3,1,0:T(8,128)(2,1)S(1)}, bf16[3,3,640,320]{2,3,1,0:T(8,128)(2,1)}, u32[]{:S(2)}) %copy-start) | copy-done | bytes 3686424
  29.1 0.4 fusion.8
  29.5 0.5 convolution_add_fusion.7
  30.9 0.5 convolution_add_fusion.4
  31.3 0.4 convolution_add_fusion.3
  33.7 4.4 %all_to_all.18 = f32[8,64,320]{2,1,0:T(8,128)S(1)} all-to-all(f32[8,64,320]{2,1,0:T(8,128)S(1)} %dynamic-slice_add_fusion), channel_id=1, replica_groups=mesh['pano'=2,'blk'=8,'rows'=2] {'rows'}, dimensions={0} | all-to-all | bytes 1310720 | tf_op jit(solution)/shard_map/all_to_all | solution.py:65
  38.1 0.6 %copy.25 = f32[4,64,2,320]{3,2,1,0:T(2,128)S(1)} copy(f32[4,64,2,320]{3,1,0,2:T(8,128)S(1)} %bitcast.108) | data formatting | bytes 1310720 | tf_op jit(solution)/shard_map/all_to_all | solution.py:65
  38.7 0.5 all_to_all.16
  39.4 1.2 %dynamic_update_slice.6 = f32[4,96,640]{2,1,0:T(8,128)S(1)} dynamic-update-slice(f32[4,96,640]{2,1,0:T(8,128)S(1)} %broadcast_in_dim.4, f32[4,64,640]{2,1,0:T(8,128)S(1)} %broadcast_multiply_fusion, s32[]{:T(128)} %constant.14.clone.1, s32[]{:T(128)S(6)} %select_n.4, s32[]{:T(128)} %constant.14.clone.1) | dynamic-update-slice | bytes 1310724 | tf_op jit(solution)/shard_map/dynamic_update_slice | solution.py:80
  40.7 1.8 %collective-permute-start.2 = (bf16[4,32,640]{2,1,0:T(8,128)(2,1)S(1)}, bf16[4,32,640]{2,1,0:T(8,128)(2,1)S(1)}, u32[]{:S(2)}, u32[]{:S(2)}) collective-permute-start(bf16[4,32,640]{2,1,0:T(8,128)(2,1)S(1)} %get-tuple-element.25), channel_id=1, source_target_pairs={{0,2},{2,4},{4,6},{6,8},{8,10},{10,12},{12,14},{14,0},{1,3},{3,5},... | collective-permute-start | bytes 491528 | tf_op jit(solution)/shard_map/ppermute | solution.py:14
  42.5 1.6 %collective-permute-start.3 = (bf16[4,32,640]{2,1,0:T(8,128)(2,1)S(1)}, bf16[4,32,640]{2,1,0:T(8,128)(2,1)S(1)}, u32[]{:S(2)}, u32[]{:S(2)}) collective-permute-start(bf16[4,32,640]{2,1,0:T(8,128)(2,1)S(1)} %get-tuple-element.26), channel_id=1, source_target_pairs={{0,4},{2,6},{4,8},{6,10},{8,12},{10,14},{12,0},{14,2},{1,5},{3,7},... | collective-permute-start | bytes 491528 | tf_op jit(solution)/shard_map/ppermute | solution.py:14
  44.1 3.0 %collective-permute-done.2 = bf16[4,32,640]{2,1,0:T(8,128)(2,1)S(1)} collective-permute-done((bf16[4,32,640]{2,1,0:T(8,128)(2,1)S(1)}, bf16[4,32,640]{2,1,0:T(8,128)(2,1)S(1)}, u32[]{:S(2)}, u32[]{:S(2)}) %collective-permute-start.2) | collective-permute-done | bytes 163872 | tf_op jit(solution)/shard_map/ppermute | solution.py:14
  47.1 6.5 %collective-permute-done.3 = bf16[4,32,640]{2,1,0:T(8,128)(2,1)S(1)} collective-permute-done((bf16[4,32,640]{2,1,0:T(8,128)(2,1)S(1)}, bf16[4,32,640]{2,1,0:T(8,128)(2,1)S(1)}, u32[]{:S(2)}, u32[]{:S(2)}) %collective-permute-start.3) | collective-permute-done | bytes 163872 | tf_op jit(solution)/shard_map/ppermute | solution.py:14
  53.6 0.9 %multiply_add_fusion = f32[4,32,640]{2,1,0:T(8,128)} fusion(f32[4,32,640]{2,1,0:T(8,128)S(1)} %copy-done.2, f32[4,96,640]{2,1,0:T(8,128)S(1)} %dynamic_update_slice.6, bf16[4,32,640]{2,1,0:T(8,128)(2,1)S(1)} %collective-permute-done.3, bf16[4,32,640]{2,1,0:T(8,128)(2,1)S(1)} %collective-permute-done.2, f32[32]{0:T(128)S(1)} %convert_add_fusion), kind=kLoop, calls=%fused_computation.85 | loop fusion | flops 819200 | bytes 1310848 | tf_op jit(solution)/shard_map/add | solution.py:97
  (56 shorter events, 8.5 us)
Async XLA Ops:
  0.0 15.0 %copy-start.3 = (f32[640]{0:T(1024)S(1)}, f32[640]{0:T(1024)}, u32[]{:S(2)}) copy-start(f32[640]{0:T(1024)} %param.13) | copy-start | bytes 7684
  1.0 10.3 %collective-permute-start = (bf16[4,32,640]{2,1,0:T(8,128)(2,1)S(1)}, bf16[4,32,640]{2,1,0:T(8,128)(2,1)S(1)}, u32[]{:S(2)}, u32[]{:S(2)}) collective-permute-start(bf16[4,32,640]{2,1,0:T(8,128)(2,1)S(1)} %convert_element_type.41), channel_id=1, source_target_pairs={{0,14},{2,0},{4,2},{6,4},{8,6},{10,8},{12,10},{14,12},{1,15},{3,1}... | collective-permute-start | bytes 491528 | tf_op jit(solution)/shard_map/ppermute | solution.py:14
  1.1 10.2 %collective-permute-start.1 = (bf16[4,32,640]{2,1,0:T(8,128)(2,1)S(1)}, bf16[4,32,640]{2,1,0:T(8,128)(2,1)S(1)}, u32[]{:S(2)}, u32[]{:S(2)}) collective-permute-start(bf16[4,32,640]{2,1,0:T(8,128)(2,1)S(1)} %convert_element_type.41), channel_id=1, source_target_pairs={{0,12},{2,14},{4,0},{6,2},{8,4},{10,6},{12,8},{14,10},{1,13},{3,15... | collective-permute-start | bytes 491528 | tf_op jit(solution)/shard_map/ppermute | solution.py:14
  6.7 37.3 %collective-permute-start.4 = (bf16[32]{0:T(256)(128)(2,1)S(1)}, bf16[32]{0:T(256)(128)(2,1)S(1)}, u32[]{:S(2)}, u32[]{:S(2)}) collective-permute-start(bf16[32]{0:T(256)(128)(2,1)S(1)} %get-tuple-element.27), channel_id=1, source_target_pairs={{0,2},{2,4},{4,6},{6,8},{8,10},{10,12},{12,14},{14,0},{1,3},{3,5},... | collective-permute-start | bytes 200 | tf_op jit(solution)/shard_map/ppermute | solution.py:14
  9.1 35.0 %collective-permute-start.5 = (bf16[32]{0:T(256)(128)(2,1)S(1)}, bf16[32]{0:T(256)(128)(2,1)S(1)}, u32[]{:S(2)}, u32[]{:S(2)}) collective-permute-start(bf16[32]{0:T(256)(128)(2,1)S(1)} %get-tuple-element.28), channel_id=1, source_target_pairs={{0,4},{2,6},{4,8},{6,10},{8,12},{10,14},{12,0},{14,2},{1,5},{3,7},... | collective-permute-start | bytes 200 | tf_op jit(solution)/shard_map/ppermute | solution.py:14
  15.0 2.0 %copy-start.1 = (bf16[3,3,640,320]{2,3,1,0:T(8,128)(2,1)S(1)}, bf16[3,3,640,320]{2,3,1,0:T(8,128)(2,1)}, u32[]{:S(2)}) copy-start(bf16[3,3,640,320]{2,3,1,0:T(8,128)(2,1)} %param.11) | copy-start | bytes 11059204
  27.0 2.0 %copy-start = (bf16[3,3,640,320]{2,3,1,0:T(8,128)(2,1)S(1)}, bf16[3,3,640,320]{2,3,1,0:T(8,128)(2,1)}, u32[]{:S(2)}) copy-start(bf16[3,3,640,320]{2,3,1,0:T(8,128)(2,1)} %param.12) | copy-start | bytes 11059204
  38.7 14.9 %copy-start.2 = (f32[4,32,640]{2,1,0:T(8,128)S(1)}, f32[4,32,640]{2,1,0:T(8,128)}, u32[]{:S(2)}) copy-start(f32[4,32,640]{2,1,0:T(8,128)} %param.8) | copy-start | bytes 983044
  40.7 6.4 %collective-permute-start.2 = (bf16[4,32,640]{2,1,0:T(8,128)(2,1)S(1)}, bf16[4,32,640]{2,1,0:T(8,128)(2,1)S(1)}, u32[]{:S(2)}, u32[]{:S(2)}) collective-permute-start(bf16[4,32,640]{2,1,0:T(8,128)(2,1)S(1)} %get-tuple-element.25), channel_id=1, source_target_pairs={{0,2},{2,4},{4,6},{6,8},{8,10},{10,12},{12,14},{14,0},{1,3},{3,5},... | collective-permute-start | bytes 491528 | tf_op jit(solution)/shard_map/ppermute | solution.py:14
  42.5 11.1 %collective-permute-start.3 = (bf16[4,32,640]{2,1,0:T(8,128)(2,1)S(1)}, bf16[4,32,640]{2,1,0:T(8,128)(2,1)S(1)}, u32[]{:S(2)}, u32[]{:S(2)}) collective-permute-start(bf16[4,32,640]{2,1,0:T(8,128)(2,1)S(1)} %get-tuple-element.26), channel_id=1, source_target_pairs={{0,4},{2,6},{4,8},{6,10},{8,12},{10,14},{12,0},{14,2},{1,5},{3,7},... | collective-permute-start | bytes 491528 | tf_op jit(solution)/shard_map/ppermute | solution.py:14
where the time goes:
time: 54.8 us; the launch traced here: 54.4 us
  local copies, waits for them, and re-layouts  10.9 us (20%)
  starting transfers between devices  9.91 us (18%)
  waiting for transfers between devices  9.52 us (17%)
  blocking collectives  9.38 us (17%)
  matrix products  8.21 us (15%)
  other arithmetic  5.49 us (10%)
  between operations  1.04 us (2%)
    ppermute x6, starting transfers between devices, from_behind(): return lax.ppermute(value, axis, pairs)  9.91 us
    ppermute x6, waiting for transfers between devices, from_behind(): return lax.ppermute(value, axis, pairs)  9.52 us
    dot_general x18, matrix products, nine_taps(): jnp.dot(patch, weight[row_tap, col_tap], preferred_element_type=jnp.float32)  8.21 us
    all_to_all x1, blocking collectives, denoise_local(): lax.all_to_all(result, 'rows', split_axis=0, concat_axis=2, tiled=True)  4.37 us
    all_gather x1, blocking collectives, denoise_local(): lax.all_gather(act_two, 'rows', axis=2, tiled=True)  2.74 us
    all_gather x1, blocking collectives, denoise_local(): whole = lax.all_gather(window, 'rows', axis=0, tiled=True)  2.28 us
    unnamed x8, local copies, waits for them, and re-layouts  2.12 us
    slice x2, local copies, waits for them, and re-layouts, nine_taps(): patch = framed[row_tap:row_tap + height, col_tap:col_tap + columns]  1.52 us
  transfers between devices with their start and end apart: 6, of which 2 were waited for; matrix products, arithmetic and copies ran while one was open for 37% of the time, Pallas kernels for 0%

commit v1 on v0

v1 whole, which is shorter than its diff:
```python
import functools
import math

import jax
import jax.numpy as jnp
from jax import lax
from jax.experimental import pallas as pl
from jax.experimental.pallas import tpu as pltpu
from jax.sharding import PartitionSpec as P

GROUPS = 32
PARAMS = pltpu.CompilerParams(vmem_limit_bytes=20 * 2**20)
VMEM = pl.BlockSpec(memory_space=pltpu.VMEM)
SMEM = pl.BlockSpec(memory_space=pltpu.SMEM)
F32 = jnp.float32
BF16 = jnp.bfloat16


def moved(value, step, flip):
    blocks, cores = lax.axis_size("blk"), lax.axis_size("rows")
    pairs = [
        (b * cores + r, (step(b) % blocks) * cores + (r ^ flip))
        for b in range(blocks)
        for r in range(cores)
    ]
    return lax.ppermute(value, ("blk", "rows"), pairs)


def split3(x):
    high = x.astype(BF16)
    rest = x - high.astype(F32)
    mid = rest.astype(BF16)
    low = (rest - mid.astype(F32)).astype(BF16)
    return [high.astype(F32), mid.astype(F32), low.astype(F32)]


def regroup(first, second, table):
    rows = jnp.concatenate(split3(first) + split3(second) + [jnp.zeros_like(first)] * 2, axis=0)
    out = jnp.dot(rows.astype(BF16), table, preferred_element_type=F32)
    return out[0:1] + out[1:2] + out[2:3], out[3:4] + out[4:5] + out[5:6]


def group_scale(summed, squares, count, size):
    channels, lanes = summed.shape[1], 128
    ch = lax.broadcasted_iota(jnp.int32, (channels, lanes), 0)
    low = lax.broadcasted_iota(jnp.int32, (channels, lanes), 1) * size
    gather = jnp.where((ch >= low) & (ch < low + size), 1.0, 0.0).astype(BF16)
    ch = lax.broadcasted_iota(jnp.int32, (lanes, channels), 1)
    low = lax.broadcasted_iota(jnp.int32, (lanes, channels), 0) * size
    spread = jnp.where((ch >= low) & (ch < low + size), 1.0, 0.0).astype(BF16)
    total, total_sq = regroup(summed, squares, gather)
    mean = total / count
    scale = lax.rsqrt(total_sq / count - mean * mean + 1e-05)
    return regroup(mean, scale, spread)


def silu(u):
    half = 0.5 * u
    return half + half * jnp.tanh(half)


def nine_taps(frame, weight, acc):
    height, columns = frame.shape[0] - 2, frame.shape[1]
    for a in range(3):
        patch = frame[a : a + height].reshape(height * columns, frame.shape[2])
        taps = weight[a].reshape(-1, weight.shape[3])
        part = lax.dot_general(patch, taps, (((1,), (1,)), ((), ())), preferred_element_type=F32)
        if a == 0:
            acc[...] = part
        else:
            acc[...] += part


def joined_taps(acc, row, columns, outs, anchor):
    block = acc[row * columns : (row + 1) * columns]
    col = lax.broadcasted_iota(jnp.int32, (columns, outs), 0)
    left = pltpu.roll(block[:, :outs], 1, 0)
    right = pltpu.roll(block[:, 2 * outs :], columns - 1, 0)
    left = jnp.where(col == anchor, 0.0, left)
    right = jnp.where(col == ((anchor + columns - 1) & (columns - 1)), 0.0, right)
    return block[:, outs : 2 * outs] + left + right


def half_of(ref, outs, core):
    whole = ref[...].reshape(1, -1)
    return jnp.where(core == 0, whole[:, :outs], whole[:, outs:])


def first_kernel(size, anchor_ref, mix, mix_other, full, full_other, w, gain_one, time_bias, gain_two, out, frame, acc, hidden):
    core = lax.axis_index("rows")
    anchor = anchor_ref[0]
    rows, half_cols, channels = mix.shape
    columns, height, outs = 2 * half_cols, 2 * rows, out.shape[2]
    count = height * columns * size
    summed = jnp.zeros((1, channels), F32)
    squares = jnp.zeros((1, channels), F32)
    for ref in (mix, mix_other, full, full_other):
        v = ref[...].astype(F32).reshape(rows * half_cols, channels)
        summed += jnp.sum(v, axis=0, keepdims=True)
        squares += jnp.sum(v * v, axis=0, keepdims=True)
    mean, scale = group_scale(summed, squares, count, size)
    scale = scale * gain_one[...].reshape(1, -1)
    frame[0] = jnp.zeros(frame.shape[1:], BF16)
    frame[height + 1] = jnp.zeros(frame.shape[1:], BF16)
    for ref, mine, col in ((mix, 0, 0), (full, 0, half_cols), (mix_other, 1, 0), (full_other, 1, half_cols)):
        start = 1 + rows * (core ^ mine)
        for row in range(rows):
            v = ref[row].astype(F32)
            frame[start + row, col : col + half_cols] = silu((v - mean) * scale).astype(BF16)
    nine_taps(frame, w, acc)
    bias = half_of(time_bias, outs, core)
    summed = jnp.zeros((1, outs), F32)
    squares = jnp.zeros((1, outs), F32)
    for row in range(height):
        v = joined_taps(acc, row, columns, outs, anchor) + bias
        hidden[row] = v
        summed += jnp.sum(v, axis=0, keepdims=True)
        squares += jnp.sum(v * v, axis=0, keepdims=True)
    mean, scale = group_scale(summed, squares, count, size)
    scale = scale * half_of(gain_two, outs, core)
    for row in range(height):
        out[row] = silu((hidden[row] - mean) * scale).astype(BF16)


def second_kernel(anchor_ref, own, other, w, share, mix_same, mix_cross, full_same, full_cross, frame, acc, result):
    core = lax.axis_index("rows")
    anchor = anchor_ref[0]
    height, columns, outs = own.shape
    rows, half_cols = height // 2, columns // 2
    frame[0] = jnp.zeros(frame.shape[1:], BF16)
    frame[height + 1] = jnp.zeros(frame.shape[1:], BF16)

    @pl.when(core == 0)
    def _():
        for row in range(height):
            frame[1 + row] = jnp.concatenate([own[row], other[row]], axis=1)

    @pl.when(core == 1)
    def _():
        for row in range(height):
            frame[1 + row] = jnp.concatenate([other[row], own[row]], axis=1)

    nine_taps(frame, w, acc)
    part = jnp.broadcast_to(share[:, :1], (columns, outs))
    for row in range(height):
        result[row] = joined_taps(acc, row, columns, outs, anchor) * part
    for out, flip, col in (
        (mix_same, 0, 0),
        (mix_cross, 1, 0),
        (full_same, 0, half_cols),
        (full_cross, 1, half_cols),
    ):
        start = rows * (core ^ flip)
        for row in range(rows):
            out[row] = result[start + row, col : col + half_cols].astype(BF16)


def last_kernel(anchor_ref, latent, lowered, mix_own, mix_core, mix_same, mix_cross, full_same, full_cross, out):
    core = lax.axis_index("rows")
    odd = lax.axis_index("blk") & 1
    anchor = anchor_ref[0]
    rows, cols, outs = mix_own.shape
    col = lax.broadcasted_iota(jnp.int32, (cols, outs), 0)
    keep = (col >= anchor) ^ (odd == 1)
    own_scale = math.sqrt(0.7 / 0.5)
    join_scale = math.sqrt(0.3) - math.sqrt(0.7 / 0.5) * math.sqrt(0.5)
    for row in range(rows):
        same = jnp.where(keep, mix_own[row].astype(F32), mix_same[row].astype(F32)) + full_same[row].astype(F32)
        cross = jnp.where(keep, mix_core[row].astype(F32), mix_cross[row].astype(F32)) + full_cross[row].astype(F32)
        base = own_scale * latent[row] + join_scale * lowered[row].astype(F32)

        @pl.when(core == 0)
        def _():
            out[row] = base + join_scale * jnp.concatenate([same, cross], axis=1)

        @pl.when(core == 1)
        def _():
            out[row] = base + join_scale * jnp.concatenate([cross, same], axis=1)


def per_device(latent, offset, counts, conv_one, conv_two, gain_one, gain_two, time_bias):
    rows, stride, channels = latent.shape
    outs = conv_one.shape[3]
    size = channels // GROUPS
    height, columns = 2 * rows, 2 * stride
    odd = (lax.axis_index("blk") & 1) == 1
    first = lax.axis_index("rows") * outs
    anchor = offset[0]

    def computes(w):
        return w + 2 * (w % 2)

    lowered = latent.astype(BF16)
    full = moved(lowered, lambda b: b ^ 1, 0)
    beyond = moved(lowered, lambda b: b + 2 if b % 2 else b - 2, 0)
    row = counts[0].astype(F32)
    mine = moved(row, computes, 0)
    behind = moved(row, lambda w: computes(w + 1), 0)
    ahead = moved(row, lambda w: computes(w - 1), 0)
    share = mine / (mine + jnp.concatenate([behind[stride:], ahead[:stride]]))
    spot = lax.broadcasted_iota(jnp.int32, (columns, columns), 0) - anchor
    spot = jnp.where(spot < 0, spot + columns, spot)
    picked = spot == lax.broadcasted_iota(jnp.int32, (columns, columns), 1)
    share = jnp.sum(jnp.where(picked, share[None, :], 0.0), axis=1)
    share = jnp.broadcast_to(share[:, None], (columns, 128))
    full_other = moved(full, lambda b: b, 1)
    col = lax.broadcasted_iota(jnp.int32, lowered.shape, 1)
    mix = jnp.where((col >= anchor) ^ odd, lowered, beyond)
    mix_other = moved(mix, lambda b: b, 1)

    w_one = jnp.swapaxes(conv_one, 2, 3)
    w_two = jnp.swapaxes(conv_two, 2, 3)
    frame = pltpu.VMEM((height + 2, columns, channels), BF16)
    acc = pltpu.VMEM((height * columns, 3 * outs), F32)
    result = pltpu.VMEM((height, columns, outs), F32)
    own = pl.pallas_call(
        functools.partial(first_kernel, size),
        out_shape=jax.ShapeDtypeStruct((height, columns, outs), BF16),
        in_specs=[SMEM] + [VMEM] * 8,
        out_specs=VMEM,
        scratch_shapes=[frame, acc, result],
        compiler_params=PARAMS,
    )(offset, mix, mix_other, full, full_other, w_one, gain_one, time_bias, gain_two)
    other = moved(own, lambda b: b, 1)
    piece = jax.ShapeDtypeStruct((rows, stride, outs), BF16)
    mix_same, mix_cross, full_same, full_cross = pl.pallas_call(
        second_kernel,
        out_shape=(piece,) * 4,
        in_specs=[SMEM] + [VMEM] * 4,
        out_specs=(VMEM,) * 4,
        scratch_shapes=[frame, acc, result],
        compiler_params=PARAMS,
    )(offset, own, other, w_two, share)

    def aside(b):
        return b - 2 if b % 2 else b + 2

    got_full_same = moved(full_same, lambda b: b ^ 1, 0)
    got_full_cross = moved(full_cross, lambda b: b ^ 1, 1)
    got_mix_same = moved(mix_same, aside, 0)
    got_mix_cross = moved(mix_cross, aside, 1)
    got_core = moved(mix_cross, lambda b: b, 1)
    return pl.pallas_call(
        last_kernel,
        out_shape=jax.ShapeDtypeStruct(latent.shape, F32),
        in_specs=[SMEM] + [VMEM] * 8,
        out_specs=VMEM,
        compiler_params=PARAMS,
    )(offset, latent, lowered, mix_same, got_core, got_mix_same, got_mix_cross, got_full_same, got_full_cross)


def solution(mesh):
    return jax.shard_map(
        per_device,
        mesh=mesh,
        in_specs=(
            P(("pano", "rows"), "blk", None),
            P("pano"),
            P(("pano", "blk"), None),
            P(None, None, None, "rows"),
            P(None, None, None, "rows"),
            P(),
            P(),
            P(),
        ),
        out_specs=P(("pano", "rows"), "blk", None),
        check_vma=False,
    )
```

time: 54.8 us -> 42.8 us (0.78)
  the two profiles are of different devices: /device:TPU:2 before, /device:TPU:1 now
where the time goes in v1:
time: 42.8 us; the launch traced here: 42.5 us
  starting transfers between devices  17.2 us (40%)
  Pallas kernels  8.81 us (21%)
  waiting for transfers between devices  8.19 us (19%)
  local copies, waits for them, and re-layouts  4.25 us (10%)
  other arithmetic  3.18 us (7%)
  between operations  0.88 us (2%)
    ppermute x13, starting transfers between devices, moved(): return lax.ppermute(value, ('blk', 'rows'), pairs)  17.2 us
    ppermute x13, waiting for transfers between devices, moved(): return lax.ppermute(value, ('blk', 'rows'), pairs)  8.19 us
    pallas_call x1, Pallas kernels, per_device(): pl.pallas_call(functools.partial(first_kernel, size), out_shape=jax.Shape...  4.32 us
    unnamed x12, local copies, waits for them, and re-layouts  4.11 us
    pallas_call x1, Pallas kernels, per_device(): pl.pallas_call(second_kernel, out_shape=(piece,) * 4, in_specs=[SMEM] + [...  3.32 us
    select_n x1, other arithmetic, per_device(): mix = jnp.where((col >= anchor) ^ odd, lowered, beyond)  1.24 us
    pallas_call x1, Pallas kernels, per_device(): pl.pallas_call(last_kernel, out_shape=jax.ShapeDtypeStruct(latent.shape,...  1.17 us
    convert_element_type x1, other arithmetic, per_device(): lowered = latent.astype(BF16)  0.99 us
  transfers between devices with their start and end apart: 13, of which 6 were waited for; matrix products, arithmetic and copies ran while one was open for 5% of the time, Pallas kernels for 10%

profile of v1, /device:TPU:1, one launch (start us, length us, event | category | flops | bytes accessed | tf_op | source)
XLA Modules:
  0.0 42.5 jit_solution(11904485719544089116)
XLA Ops:
  0.0 1.0 %convert_element_type.9.lowered = bf16[4,32,640]{2,1,0:T(8,128)(2,1)S(1)} convert(f32[4,32,640]{2,1,0:T(8,128)} %latent.1) | non-fusion elementwise | flops 81920 | bytes 491520 | tf_op jit(solution)/shard_map/convert_element_type | solution.py:193
  1.0 4.2 %collective-permute-start = (bf16[4,32,640]{2,1,0:T(8,128)(2,1)S(1)}, bf16[4,32,640]{2,1,0:T(8,128)(2,1)S(1)}, u32[]{:S(2)}, u32[]{:S(2)}) collective-permute-start(bf16[4,32,640]{2,1,0:T(8,128)(2,1)S(1)} %convert_element_type.9.lowered), channel_id=1, source_target_pairs={{0,12},{1,13},{2,6},{3,7},{4,0},{5,1},{6,10},{7,11},{8,4},{9,5},{1... | collective-permute-start | bytes 491528 | tf_op jit(solution)/shard_map/ppermute | solution.py:26
  5.2 0.7 %convert_bitcast_fusion = f32[64]{0:T(128)S(1)} fusion(s32[1,64]{1,0:T(1,128)} %param.10), kind=kLoop, calls=%fused_computation.5 | loop fusion | flops 64 | bytes 512 | tf_op jit(solution)/shard_map/convert_element_type | solution.py:196
  5.8 0.2 collective-permute-start.6
  6.0 0.6 %collective-permute-start.5 = (f32[64]{0:T(128)S(1)}, f32[64]{0:T(128)S(1)}, u32[]{:S(2)}, u32[]{:S(2)}) collective-permute-start(f32[64]{0:T(128)S(1)} %convert_bitcast_fusion), channel_id=1, source_target_pairs={{0,0},{1,1},{2,6},{3,7},{4,4},{5,5},{6,10},{7,11},{8,8},{9,9},{10,... | collective-permute-start | bytes 776 | tf_op jit(solution)/shard_map/ppermute | solution.py:26
  6.7 4.1 %collective-permute-start.2 = (bf16[4,32,640]{2,1,0:T(8,128)(2,1)S(1)}, bf16[4,32,640]{2,1,0:T(8,128)(2,1)S(1)}, u32[]{:S(2)}, u32[]{:S(2)}) collective-permute-start(bf16[4,32,640]{2,1,0:T(8,128)(2,1)S(1)} %convert_element_type.9.lowered), channel_id=1, source_target_pairs={{0,2},{1,3},{2,0},{3,1},{4,6},{5,7},{6,4},{7,5},{8,10},{9,11},{10,... | collective-permute-start | bytes 491528 | tf_op jit(solution)/shard_map/ppermute | solution.py:26
  11.6 0.0 collective-permute-done
  11.6 1.2 %broadcast_select_fusion.mix = bf16[4,32,640]{2,1,0:T(8,128)(2,1)S(1)} fusion(bf16[4,32,640]{2,1,0:T(8,128)(2,1)S(1)} %collective-permute-done, pred[32]{0:T(512)(128)(4,1)S(1)} %compare_xor_fusion, f32[4,32,640]{2,1,0:T(8,128)} %latent.1), kind=kLoop, calls=%fused_computation | loop fusion | flops 163840 | bytes 655392 | tf_op jit(solution)/shard_map/jit(_where)/select_n | solution.py:208
  12.8 2.1 %collective-permute-start.1 = (bf16[4,32,640]{2,1,0:T(8,128)(2,1)S(1)}, bf16[4,32,640]{2,1,0:T(8,128)(2,1)S(1)}, u32[]{:S(2)}, u32[]{:S(2)}) collective-permute-start(bf16[4,32,640]{2,1,0:T(8,128)(2,1)S(1)} %broadcast_select_fusion.mix), channel_id=1, source_target_pairs={{0,1},{1,0},{2,3},{3,2},{4,5},{5,4},{6,7},{7,6},{8,9},{9,8},{10,11... | collective-permute-start | bytes 491528 | tf_op jit(solution)/shard_map/ppermute | solution.py:26
  15.0 0.0 collective-permute-done.2.full
  15.0 1.2 %collective-permute-start.3 = (bf16[4,32,640]{2,1,0:T(8,128)(2,1)S(1)}, bf16[4,32,640]{2,1,0:T(8,128)(2,1)S(1)}, u32[]{:S(2)}, u32[]{:S(2)}) collective-permute-start(bf16[4,32,640]{2,1,0:T(8,128)(2,1)S(1)} %collective-permute-done.2.full), channel_id=1, source_target_pairs={{0,1},{1,0},{2,3},{3,2},{4,5},{5,4},{6,7},{7,6},{8,9},{9,8},{10,11... | collective-permute-start | bytes 491528 | tf_op jit(solution)/shard_map/ppermute | solution.py:26
  16.2 0.1 slice.6
  16.2 0.9 %collective-permute-done.3.full_other = bf16[4,32,640]{2,1,0:T(8,128)(2,1)S(1)} collective-permute-done((bf16[4,32,640]{2,1,0:T(8,128)(2,1)S(1)}, bf16[4,32,640]{2,1,0:T(8,128)(2,1)S(1)}, u32[]{:S(2)}, u32[]{:S(2)}) %collective-permute-start.3) | collective-permute-done | bytes 163872 | tf_op jit(solution)/shard_map/ppermute | solution.py:26
  17.2 2.0 %copy-done.1 = bf16[3,3,640,320]{2,3,1,0:T(8,128)(2,1)S(1)} copy-done((bf16[3,3,640,320]{2,3,1,0:T(8,128)(2,1)S(1)}, bf16[3,3,640,320]{2,3,1,0:T(8,128)(2,1)}, u32[]{:S(2)}) %copy-start.1) | copy-done | bytes 3686424
  19.2 0.7 %copy-done.3 = f32[640]{0:T(1024)S(1)} copy-done((f32[640]{0:T(1024)S(1)}, f32[640]{0:T(1024)}, u32[]{:S(2)}) %copy-start.3) | copy-done | bytes 2584
  19.9 0.7 %copy-done.4 = f32[640]{0:T(1024)S(1)} copy-done((f32[640]{0:T(1024)S(1)}, f32[640]{0:T(1024)}, u32[]{:S(2)}) %copy-start.4) | copy-done | bytes 2584
  20.6 0.7 %copy-done.5 = f32[640]{0:T(1024)S(1)} copy-done((f32[640]{0:T(1024)S(1)}, f32[640]{0:T(1024)}, u32[]{:S(2)}) %copy-start.5) | copy-done | bytes 2584
  21.3 4.3 %shard_map.82.own = bf16[8,64,320]{2,1,0:T(8,128)(2,1)S(1)} custom-call(s32[1]{0:T(128)} %copy.9.anchor_ref, bf16[4,32,640]{2,1,0:T(8,128)(2,1)S(1)} %broadcast_select_fusion.mix, bf16[4,32,640]{2,1,0:T(8,128)(2,1)S(1)} %collective-permute-done.1.mix_other, bf16[4,32,640]{2,1,0:T(8,128)(2,1)S(1)} %collective-permute-done.2.full, ...), custom_call_target="tpu_custom_call" | custom-call | tf_op jit(solution)/shard_map/pallas_call | solution.py:216
  25.6 0.4 collective-permute-start.4
  26.0 0.1 add_divide_fusion
  26.1 0.2 select_reduce_fusion
  26.3 1.1 %collective-permute-done.4.other = bf16[8,64,320]{2,1,0:T(8,128)(2,1)S(1)} collective-permute-done((bf16[8,64,320]{2,1,0:T(8,128)(2,1)S(1)}, bf16[8,64,320]{2,1,0:T(8,128)(2,1)S(1)}, u32[]{:S(2)}, u32[]{:S(2)}) %collective-permute-start.4) | collective-permute-done | bytes 327712 | tf_op jit(solution)/shard_map/ppermute | solution.py:26
  27.4 0.1 broadcast_in_dim.21.share
  27.5 3.3 %shard_map.83 = (bf16[4,32,320]{2,1,0:T(8,128)(2,1)S(1)}, bf16[4,32,320]{2,1,0:T(8,128)(2,1)S(1)}, bf16[4,32,320]{2,1,0:T(8,128)(2,1)S(1)}, bf16[4,32,320]{2,1,0:T(8,128)(2,1)S(1)}) custom-call(s32[1]{0:T(128)} %copy.9.anchor_ref, bf16[8,64,320]{2,1,0:T(8,128)(2,1)S(1)} %shard_map.82.own, bf16[8,64,320]{2,1,0:T(8,128)(2,1)S(1)} %collective-permute-done.4.other, ...), custom_call_target="tpu_custom_call" | custom-call | tf_op jit(solution)/shard_map/pallas_call | solution.py:226
  30.8 1.8 %collective-permute-start.11 = (bf16[4,32,320]{2,1,0:T(8,128)(2,1)S(1)}, bf16[4,32,320]{2,1,0:T(8,128)(2,1)S(1)}, u32[]{:S(2)}, u32[]{:S(2)}) collective-permute-start(bf16[4,32,320]{2,1,0:T(8,128)(2,1)S(1)} %get-tuple-element.11), channel_id=1, source_target_pairs={{0,2},{1,3},{2,0},{3,1},{4,6},{5,7},{6,4},{7,5},{8,10},{9,11},{10,... | collective-permute-start | bytes 245768 | tf_op jit(solution)/shard_map/ppermute | solution.py:26
  32.6 0.3 collective-permute-start.12
  32.9 2.3 %collective-permute-start.10 = (bf16[4,32,320]{2,1,0:T(8,128)(2,1)S(1)}, bf16[4,32,320]{2,1,0:T(8,128)(2,1)S(1)}, u32[]{:S(2)}, u32[]{:S(2)}) collective-permute-start(bf16[4,32,320]{2,1,0:T(8,128)(2,1)S(1)} %get-tuple-element.10), channel_id=1, source_target_pairs={{0,5},{1,4},{2,15},{3,14},{4,9},{5,8},{6,3},{7,2},{8,13},{9,12},{1... | collective-permute-start | bytes 245768 | tf_op jit(solution)/shard_map/ppermute | solution.py:26
  35.2 0.2 collective-permute-done.11.full_same
  35.4 2.5 %collective-permute-done.12.full_cross = bf16[4,32,320]{2,1,0:T(8,128)(2,1)S(1)} collective-permute-done((bf16[4,32,320]{2,1,0:T(8,128)(2,1)S(1)}, bf16[4,32,320]{2,1,0:T(8,128)(2,1)S(1)}, u32[]{:S(2)}, u32[]{:S(2)}) %collective-permute-start.12) | collective-permute-done | bytes 81952 | tf_op jit(solution)/shard_map/ppermute | solution.py:26
  37.9 0.8 %collective-permute-done.9.mix_same = bf16[4,32,320]{2,1,0:T(8,128)(2,1)S(1)} collective-permute-done((bf16[4,32,320]{2,1,0:T(8,128)(2,1)S(1)}, bf16[4,32,320]{2,1,0:T(8,128)(2,1)S(1)}, u32[]{:S(2)}, u32[]{:S(2)}) %collective-permute-start.9) | collective-permute-done | bytes 81952 | tf_op jit(solution)/shard_map/ppermute | solution.py:26
  38.8 2.6 %collective-permute-done.10.mix_cross = bf16[4,32,320]{2,1,0:T(8,128)(2,1)S(1)} collective-permute-done((bf16[4,32,320]{2,1,0:T(8,128)(2,1)S(1)}, bf16[4,32,320]{2,1,0:T(8,128)(2,1)S(1)}, u32[]{:S(2)}, u32[]{:S(2)}) %collective-permute-start.10) | collective-permute-done | bytes 81952 | tf_op jit(solution)/shard_map/ppermute | solution.py:26
  41.4 1.2 %shard_map.84 = f32[4,32,640]{2,1,0:T(8,128)} custom-call(s32[1]{0:T(128)} %copy.9.anchor_ref, f32[4,32,640]{2,1,0:T(8,128)S(1)} %copy-done.2, bf16[4,32,640]{2,1,0:T(8,128)(2,1)S(1)} %convert_element_type.9.lowered, bf16[4,32,320]{2,1,0:T(8,128)(2,1)S(1)} %get-tuple-element.9.mix_own, bf16[4,32,320]{2,1,0:T(8,128)(2,1)S(1)} %collective-permute-done.8.mix_core, ...), custom_call_target="tpu_custom_call" | custom-call | tf_op jit(solution)/shard_map/pallas_call | solution.py:243
  (19 shorter events, 0.1 us)
Async XLA Ops:
  1.0 10.6 %collective-permute-start = (bf16[4,32,640]{2,1,0:T(8,128)(2,1)S(1)}, bf16[4,32,640]{2,1,0:T(8,128)(2,1)S(1)}, u32[]{:S(2)}, u32[]{:S(2)}) collective-permute-start(bf16[4,32,640]{2,1,0:T(8,128)(2,1)S(1)} %convert_element_type.9.lowered), channel_id=1, source_target_pairs={{0,12},{1,13},{2,6},{3,7},{4,0},{5,1},{6,10},{7,11},{8,4},{9,5},{1... | collective-permute-start | bytes 491528 | tf_op jit(solution)/shard_map/ppermute | solution.py:26
  5.8 20.2 %collective-permute-start.7 = (f32[64]{0:T(128)S(1)}, f32[64]{0:T(128)S(1)}, u32[]{:S(2)}, u32[]{:S(2)}) collective-permute-start(f32[64]{0:T(128)S(1)} %convert_bitcast_fusion), channel_id=1, source_target_pairs={{0,2},{1,3},{2,0},{3,1},{4,6},{5,7},{6,4},{7,5},{8,10},{9,11},{10,... | collective-permute-start | bytes 776 | tf_op jit(solution)/shard_map/ppermute | solution.py:26
  5.8 10.3 %collective-permute-start.6 = (f32[64]{0:T(128)S(1)}, f32[64]{0:T(128)S(1)}, u32[]{:S(2)}, u32[]{:S(2)}) collective-permute-start(f32[64]{0:T(128)S(1)} %convert_bitcast_fusion), channel_id=1, source_target_pairs={{0,6},{1,7},{2,4},{3,5},{4,10},{5,11},{6,8},{7,9},{8,14},{9,15},{1... | collective-permute-start | bytes 776 | tf_op jit(solution)/shard_map/ppermute | solution.py:26
  6.0 20.0 %collective-permute-start.5 = (f32[64]{0:T(128)S(1)}, f32[64]{0:T(128)S(1)}, u32[]{:S(2)}, u32[]{:S(2)}) collective-permute-start(f32[64]{0:T(128)S(1)} %convert_bitcast_fusion), channel_id=1, source_target_pairs={{0,0},{1,1},{2,6},{3,7},{4,4},{5,5},{6,10},{7,11},{8,8},{9,9},{10,... | collective-permute-start | bytes 776 | tf_op jit(solution)/shard_map/ppermute | solution.py:26
  6.7 8.3 %collective-permute-start.2 = (bf16[4,32,640]{2,1,0:T(8,128)(2,1)S(1)}, bf16[4,32,640]{2,1,0:T(8,128)(2,1)S(1)}, u32[]{:S(2)}, u32[]{:S(2)}) collective-permute-start(bf16[4,32,640]{2,1,0:T(8,128)(2,1)S(1)} %convert_element_type.9.lowered), channel_id=1, source_target_pairs={{0,2},{1,3},{2,0},{3,1},{4,6},{5,7},{6,4},{7,5},{8,10},{9,11},{10,... | collective-permute-start | bytes 491528 | tf_op jit(solution)/shard_map/ppermute | solution.py:26
  10.8 16.7 %copy-start = (bf16[3,3,640,320]{2,3,1,0:T(8,128)(2,1)S(1)}, bf16[3,3,640,320]{2,3,1,0:T(8,128)(2,1)}, u32[]{:S(2)}) copy-start(bf16[3,3,640,320]{2,3,1,0:T(8,128)(2,1)} %param.12) | copy-start | bytes 11059204
  12.8 4.3 %collective-permute-start.1 = (bf16[4,32,640]{2,1,0:T(8,128)(2,1)S(1)}, bf16[4,32,640]{2,1,0:T(8,128)(2,1)S(1)}, u32[]{:S(2)}, u32[]{:S(2)}) collective-permute-start(bf16[4,32,640]{2,1,0:T(8,128)(2,1)S(1)} %broadcast_select_fusion.mix), channel_id=1, source_target_pairs={{0,1},{1,0},{2,3},{3,2},{4,5},{5,4},{6,7},{7,6},{8,9},{9,8},{10,11... | collective-permute-start | bytes 491528 | tf_op jit(solution)/shard_map/ppermute | solution.py:26
  15.0 2.2 %collective-permute-start.3 = (bf16[4,32,640]{2,1,0:T(8,128)(2,1)S(1)}, bf16[4,32,640]{2,1,0:T(8,128)(2,1)S(1)}, u32[]{:S(2)}, u32[]{:S(2)}) collective-permute-start(bf16[4,32,640]{2,1,0:T(8,128)(2,1)S(1)} %collective-permute-done.2.full), channel_id=1, source_target_pairs={{0,1},{1,0},{2,3},{3,2},{4,5},{5,4},{6,7},{7,6},{8,9},{9,8},{10,11... | collective-permute-start | bytes 491528 | tf_op jit(solution)/shard_map/ppermute | solution.py:26
  17.2 2.0 %copy-start.1 = (bf16[3,3,640,320]{2,3,1,0:T(8,128)(2,1)S(1)}, bf16[3,3,640,320]{2,3,1,0:T(8,128)(2,1)}, u32[]{:S(2)}) copy-start(bf16[3,3,640,320]{2,3,1,0:T(8,128)(2,1)} %param.11) | copy-start | bytes 11059204
  19.2 0.7 %copy-start.3 = (f32[640]{0:T(1024)S(1)}, f32[640]{0:T(1024)}, u32[]{:S(2)}) copy-start(f32[640]{0:T(1024)} %gain_one.1) | copy-start | bytes 7684
  19.9 0.7 %copy-start.4 = (f32[640]{0:T(1024)S(1)}, f32[640]{0:T(1024)}, u32[]{:S(2)}) copy-start(f32[640]{0:T(1024)} %time_bias.1) | copy-start | bytes 7684
  20.6 0.7 %copy-start.5 = (f32[640]{0:T(1024)S(1)}, f32[640]{0:T(1024)}, u32[]{:S(2)}) copy-start(f32[640]{0:T(1024)} %gain_two.1) | copy-start | bytes 7684
  21.3 20.1 %copy-start.2 = (f32[4,32,640]{2,1,0:T(8,128)S(1)}, f32[4,32,640]{2,1,0:T(8,128)}, u32[]{:S(2)}) copy-start(f32[4,32,640]{2,1,0:T(8,128)} %latent.1) | copy-start | bytes 983044
  25.6 1.8 %collective-permute-start.4 = (bf16[8,64,320]{2,1,0:T(8,128)(2,1)S(1)}, bf16[8,64,320]{2,1,0:T(8,128)(2,1)S(1)}, u32[]{:S(2)}, u32[]{:S(2)}) collective-permute-start(bf16[8,64,320]{2,1,0:T(8,128)(2,1)S(1)} %shard_map.82.own), channel_id=1, source_target_pairs={{0,1},{1,0},{2,3},{3,2},{4,5},{5,4},{6,7},{7,6},{8,9},{9,8},{10,11... | collective-permute-start | bytes 983048 | tf_op jit(solution)/shard_map/ppermute | solution.py:26
  30.8 4.6 %collective-permute-start.11 = (bf16[4,32,320]{2,1,0:T(8,128)(2,1)S(1)}, bf16[4,32,320]{2,1,0:T(8,128)(2,1)S(1)}, u32[]{:S(2)}, u32[]{:S(2)}) collective-permute-start(bf16[4,32,320]{2,1,0:T(8,128)(2,1)S(1)} %get-tuple-element.11), channel_id=1, source_target_pairs={{0,2},{1,3},{2,0},{3,1},{4,6},{5,7},{6,4},{7,5},{8,10},{9,11},{10,... | collective-permute-start | bytes 245768 | tf_op jit(solution)/shard_map/ppermute | solution.py:26
  32.6 5.3 %collective-permute-start.12 = (bf16[4,32,320]{2,1,0:T(8,128)(2,1)S(1)}, bf16[4,32,320]{2,1,0:T(8,128)(2,1)S(1)}, u32[]{:S(2)}, u32[]{:S(2)}) collective-permute-start(bf16[4,32,320]{2,1,0:T(8,128)(2,1)S(1)} %get-tuple-element.12), channel_id=1, source_target_pairs={{0,3},{1,2},{2,1},{3,0},{4,7},{5,6},{6,5},{7,4},{8,11},{9,10},{10,... | collective-permute-start | bytes 245768 | tf_op jit(solution)/shard_map/ppermute | solution.py:26
  32.9 5.8 %collective-permute-start.9 = (bf16[4,32,320]{2,1,0:T(8,128)(2,1)S(1)}, bf16[4,32,320]{2,1,0:T(8,128)(2,1)S(1)}, u32[]{:S(2)}, u32[]{:S(2)}) collective-permute-start(bf16[4,32,320]{2,1,0:T(8,128)(2,1)S(1)} %get-tuple-element.9.mix_own), channel_id=1, source_target_pairs={{0,4},{1,5},{2,14},{3,15},{4,8},{5,9},{6,2},{7,3},{8,12},{9,13},{1... | collective-permute-start | bytes 245768 | tf_op jit(solution)/shard_map/ppermute | solution.py:26
  32.9 8.4 %collective-permute-start.10 = (bf16[4,32,320]{2,1,0:T(8,128)(2,1)S(1)}, bf16[4,32,320]{2,1,0:T(8,128)(2,1)S(1)}, u32[]{:S(2)}, u32[]{:S(2)}) collective-permute-start(bf16[4,32,320]{2,1,0:T(8,128)(2,1)S(1)} %get-tuple-element.10), channel_id=1, source_target_pairs={{0,5},{1,4},{2,15},{3,14},{4,9},{5,8},{6,3},{7,2},{8,13},{9,12},{1... | collective-permute-start | bytes 245768 | tf_op jit(solution)/shard_map/ppermute | solution.py:26
  35.2 6.2 %collective-permute-start.8 = (bf16[4,32,320]{2,1,0:T(8,128)(2,1)S(1)}, bf16[4,32,320]{2,1,0:T(8,128)(2,1)S(1)}, u32[]{:S(2)}, u32[]{:S(2)}) collective-permute-start(bf16[4,32,320]{2,1,0:T(8,128)(2,1)S(1)} %get-tuple-element.10), channel_id=1, source_target_pairs={{0,1},{1,0},{2,3},{3,2},{4,5},{5,4},{6,7},{7,6},{8,9},{9,8},{10,11... | collective-permute-start | bytes 245768 | tf_op jit(solution)/shard_map/ppermute | solution.py:26

commit v2 on v1

v2 whole, which is shorter than its diff:
```python
import functools
import math

import jax
import jax.numpy as jnp
from jax import lax
from jax.experimental import pallas as pl
from jax.experimental.pallas import tpu as pltpu
from jax.sharding import PartitionSpec as P

GROUPS = 32
PARAMS = pltpu.CompilerParams(vmem_limit_bytes=20 * 2**20)
VMEM = pl.BlockSpec(memory_space=pltpu.VMEM)
HBM = pl.BlockSpec(memory_space=pltpu.HBM)
SMEM = pl.BlockSpec(memory_space=pltpu.SMEM)
F32 = jnp.float32
BF16 = jnp.bfloat16


def moved(value, step, flip):
    blocks, cores = lax.axis_size("blk"), lax.axis_size("rows")
    pairs = [
        (b * cores + r, (step(b) % blocks) * cores + (r ^ flip))
        for b in range(blocks)
        for r in range(cores)
    ]
    return lax.ppermute(value, ("blk", "rows"), pairs)


def split3(x):
    high = x.astype(BF16)
    rest = x - high.astype(F32)
    mid = rest.astype(BF16)
    low = (rest - mid.astype(F32)).astype(BF16)
    return [high.astype(F32), mid.astype(F32), low.astype(F32)]


def regroup(first, second, table):
    rows = jnp.concatenate(split3(first) + split3(second) + [jnp.zeros_like(first)] * 2, axis=0)
    out = jnp.dot(rows.astype(BF16), table, preferred_element_type=F32)
    return out[0:1] + out[1:2] + out[2:3], out[3:4] + out[4:5] + out[5:6]


def group_scale(summed, squares, count, size):
    channels, lanes = summed.shape[1], 128
    ch = lax.broadcasted_iota(jnp.int32, (channels, lanes), 0)
    low = lax.broadcasted_iota(jnp.int32, (channels, lanes), 1) * size
    gather = jnp.where((ch >= low) & (ch < low + size), 1.0, 0.0).astype(BF16)
    ch = lax.broadcasted_iota(jnp.int32, (lanes, channels), 1)
    low = lax.broadcasted_iota(jnp.int32, (lanes, channels), 0) * size
    spread = jnp.where((ch >= low) & (ch < low + size), 1.0, 0.0).astype(BF16)
    total, total_sq = regroup(summed, squares, gather)
    mean = total / count
    scale = lax.rsqrt(total_sq / count - mean * mean + 1e-05)
    return regroup(mean, scale, spread)


def silu(u):
    half = 0.5 * u
    return half + half * jnp.tanh(half)


def nine_taps(frame, weight, acc, arriving=()):
    height, columns = frame.shape[0] - 2, frame.shape[1]
    for a in range(3):
        if arriving:
            arriving[a].wait()
        patch = frame[a : a + height].reshape(height * columns, frame.shape[2])
        taps = weight[a].reshape(-1, weight.shape[3])
        part = lax.dot_general(patch, taps, (((1,), (1,)), ((), ())), preferred_element_type=F32)
        if a == 0:
            acc[...] = part
        else:
            acc[...] += part


def joined_taps(acc, row, columns, outs, edges):
    block = acc[row * columns : (row + 1) * columns]
    left = pltpu.roll(block[:, :outs], 1, 0) * edges[0][:, :1]
    right = pltpu.roll(block[:, 2 * outs :], columns - 1, 0) * edges[1][:, :1]
    return block[:, outs : 2 * outs] + left + right


def half_of(row, outs, core):
    return jnp.where(core == 0, row[:, :outs], row[:, outs:])


def first_kernel(size, mix, mix_other, full, full_other, edges, w_one, w_two, gain_one, gain_two, time_bias, out, w_next, frame, acc, hidden, w, one_in, two_in, bias_in, sems):
    core = lax.axis_index("rows")
    small = [
        pltpu.make_async_copy(source, target, sems.at[4 + i])
        for i, (source, target) in enumerate(((gain_one, one_in), (gain_two, two_in), (time_bias, bias_in)))
    ]
    taps = [pltpu.make_async_copy(w_one.at[a], w.at[a], sems.at[a]) for a in range(3)]
    later = pltpu.make_async_copy(w_two, w_next, sems.at[3])
    for copy in small + taps + [later]:
        copy.start()
    rows, half_cols, channels = mix.shape
    columns, height, outs = 2 * half_cols, 2 * rows, out.shape[2]
    count = height * columns * size
    summed = jnp.zeros((1, channels), F32)
    squares = jnp.zeros((1, channels), F32)
    for ref in (mix, mix_other, full, full_other):
        v = ref[...].astype(F32).reshape(rows * half_cols, channels)
        summed += jnp.sum(v, axis=0, keepdims=True)
        squares += jnp.sum(v * v, axis=0, keepdims=True)
    mean, scale = group_scale(summed, squares, count, size)
    for copy in small:
        copy.wait()
    scale = scale * one_in[...].reshape(1, -1)
    frame[0] = jnp.zeros(frame.shape[1:], BF16)
    frame[height + 1] = jnp.zeros(frame.shape[1:], BF16)
    for ref, mine, col in ((mix, 0, 0), (full, 0, half_cols), (mix_other, 1, 0), (full_other, 1, half_cols)):
        start = 1 + rows * (core ^ mine)
        for row in range(rows):
            v = ref[row].astype(F32)
            frame[start + row, col : col + half_cols] = silu((v - mean) * scale).astype(BF16)
    nine_taps(frame, w, acc, taps)
    bias = half_of(bias_in[...].reshape(1, -1), outs, core)
    summed = jnp.zeros((1, outs), F32)
    squares = jnp.zeros((1, outs), F32)
    for row in range(height):
        v = joined_taps(acc, row, columns, outs, edges) + bias
        hidden[row] = v
        summed += jnp.sum(v, axis=0, keepdims=True)
        squares += jnp.sum(v * v, axis=0, keepdims=True)
    mean, scale = group_scale(summed, squares, count, size)
    scale = scale * half_of(two_in[...].reshape(1, -1), outs, core)
    for row in range(height):
        out[row] = silu((hidden[row] - mean) * scale).astype(BF16)
    later.wait()


def second_kernel(own, other, w, edges, share, mix_same, mix_cross, full_same, full_cross, frame, acc, result):
    core = lax.axis_index("rows")
    height, columns, outs = own.shape
    rows, half_cols = height // 2, columns // 2
    frame[0] = jnp.zeros(frame.shape[1:], BF16)
    frame[height + 1] = jnp.zeros(frame.shape[1:], BF16)

    @pl.when(core == 0)
    def _():
        for row in range(height):
            frame[1 + row] = jnp.concatenate([own[row], other[row]], axis=1)

    @pl.when(core == 1)
    def _():
        for row in range(height):
            frame[1 + row] = jnp.concatenate([other[row], own[row]], axis=1)

    nine_taps(frame, w, acc)
    part = jnp.broadcast_to(share[:, :1], (columns, outs))
    for row in range(height):
        result[row] = joined_taps(acc, row, columns, outs, edges) * part
    for out, flip, col in (
        (mix_same, 0, 0),
        (mix_cross, 1, 0),
        (full_same, 0, half_cols),
        (full_cross, 1, half_cols),
    ):
        start = rows * (core ^ flip)
        for row in range(rows):
            out[row] = result[start + row, col : col + half_cols].astype(BF16)


def last_kernel(latent, lowered, edges, inverse, mix_own, mix_core, mix_same, mix_cross, full_same, full_cross, out):
    core = lax.axis_index("rows")
    odd = lax.axis_index("blk") & 1
    rows, cols, outs = mix_own.shape
    late = jnp.broadcast_to(edges[2, :cols, :1], (cols, outs)) > 0.5
    keep = late ^ (odd == 1)
    own_scale = math.sqrt(0.7 / 0.5)
    join_scale = math.sqrt(0.3) - math.sqrt(0.7 / 0.5) * math.sqrt(0.5)
    part = join_scale * inverse[:, :1]
    for row in range(rows):
        same = jnp.where(keep, mix_own[row].astype(F32), mix_same[row].astype(F32)) + full_same[row].astype(F32)
        cross = jnp.where(keep, mix_core[row].astype(F32), mix_cross[row].astype(F32)) + full_cross[row].astype(F32)
        base = own_scale * latent[row] + join_scale * lowered[row].astype(F32)

        @pl.when(core == 0)
        def _():
            out[row] = base + part * jnp.concatenate([same, cross], axis=1)

        @pl.when(core == 1)
        def _():
            out[row] = base + part * jnp.concatenate([cross, same], axis=1)


def by_column(values, anchor):
    columns = values.shape[0]
    spot = lax.broadcasted_iota(jnp.int32, (columns, columns), 0) - anchor
    spot = jnp.where(spot < 0, spot + columns, spot)
    picked = spot == lax.broadcasted_iota(jnp.int32, (columns, columns), 1)
    placed = jnp.sum(jnp.where(picked, values[None, :], 0.0), axis=1)
    return jnp.broadcast_to(placed[:, None], (columns, 128))


def per_device(latent, offset, counts, conv_one, conv_two, gain_one, gain_two, time_bias):
    rows, stride, channels = latent.shape
    outs = conv_one.shape[3]
    size = channels // GROUPS
    height, columns = 2 * rows, 2 * stride
    odd = (lax.axis_index("blk") & 1) == 1
    anchor = offset[0]

    lowered = lax.optimization_barrier(latent.astype(BF16))
    full = moved(lowered, lambda b: b ^ 1, 0)
    beyond = moved(lowered, lambda b: b + 2 if b % 2 else b - 2, 0)
    row = counts[0].astype(F32)
    row_one = moved(row, lambda b: b + 1, 0)
    row_two = moved(row, lambda b: b + 2, 0)
    share = by_column(jnp.where(odd, row_two, row), anchor)
    now = by_column(row, anchor)[:stride]
    then = by_column(row_two, anchor)[:stride]
    always = by_column(row_one, anchor)[stride:]
    col = lax.broadcasted_iota(jnp.int32, (stride, 1), 0)
    inverse = 1.0 / (always + jnp.where(col >= anchor, now, then))

    spot = lax.broadcasted_iota(jnp.int32, (3, columns, 128), 1)
    kind = lax.broadcasted_iota(jnp.int32, (3, columns, 128), 0)
    cut = jnp.where(kind == 0, spot == anchor, spot == jnp.where(anchor == 0, columns, anchor) - 1)
    edges = jnp.where(jnp.where(kind == 2, spot < anchor, cut), 0.0, 1.0)

    full_other = moved(full, lambda b: b, 1)
    col = lax.broadcasted_iota(jnp.int32, lowered.shape, 1)
    mix = jnp.where((col >= anchor) ^ odd, lowered, beyond)
    mix_other = moved(mix, lambda b: b, 1)

    frame = pltpu.VMEM((height + 2, columns, channels), BF16)
    acc = pltpu.VMEM((height * columns, 3 * outs), F32)
    result = pltpu.VMEM((height, columns, outs), F32)
    weights = (3, 3, outs, channels)
    own, w_next = pl.pallas_call(
        functools.partial(first_kernel, size),
        out_shape=(
            jax.ShapeDtypeStruct((height, columns, outs), BF16),
            jax.ShapeDtypeStruct(weights, BF16),
        ),
        in_specs=[VMEM] * 5 + [HBM] * 5,
        out_specs=(VMEM, VMEM),
        scratch_shapes=[
            frame,
            acc,
            result,
            pltpu.VMEM(weights, BF16),
            pltpu.VMEM((channels,), F32),
            pltpu.VMEM((channels,), F32),
            pltpu.VMEM((channels,), F32),
            pltpu.SemaphoreType.DMA((7,)),
        ],
        compiler_params=PARAMS,
    )(mix, mix_other, full, full_other, edges, *[
        pltpu.with_memory_space_constraint(v, pltpu.HBM)
        for v in (jnp.swapaxes(conv_one, 2, 3), jnp.swapaxes(conv_two, 2, 3), gain_one, gain_two, time_bias)
    ])
    other = moved(own, lambda b: b, 1)
    piece = jax.ShapeDtypeStruct((rows, stride, outs), BF16)
    mix_same, mix_cross, full_same, full_cross = pl.pallas_call(
        second_kernel,
        out_shape=(piece,) * 4,
        in_specs=[VMEM] * 5,
        out_specs=(VMEM,) * 4,
        scratch_shapes=[frame, acc, result],
        compiler_params=PARAMS,
    )(own, other, w_next, edges, share)

    def aside(b):
        return b - 2 if b % 2 else b + 2

    got_mix_same = moved(mix_same, aside, 0)
    got_mix_cross = moved(mix_cross, aside, 1)
    got_full_same = moved(full_same, lambda b: b ^ 1, 0)
    got_full_cross = moved(full_cross, lambda b: b ^ 1, 1)
    got_core = moved(mix_cross, lambda b: b, 1)
    return pl.pallas_call(
        last_kernel,
        out_shape=jax.ShapeDtypeStruct(latent.shape, F32),
        in_specs=[VMEM] * 10,
        out_specs=VMEM,
        compiler_params=PARAMS,
    )(latent, lowered, edges, inverse, mix_same, got_core, got_mix_same, got_mix_cross, got_full_same, got_full_cross)


def solution(mesh):
    return jax.shard_map(
        per_device,
        mesh=mesh,
        in_specs=(
            P(("pano", "rows"), "blk", None),
            P("pano"),
            P(("pano", "blk"), None),
            P(None, None, None, "rows"),
            P(None, None, None, "rows"),
            P(),
            P(),
            P(),
        ),
        out_specs=P(("pano", "rows"), "blk", None),
        check_vma=False,
    )
```

time: 42.8 us -> 34.4 us (0.80)
  the two profiles are of different devices: /device:TPU:1 before, /device:TPU:0 now
where the time goes in v2:
time: 34.4 us; the launch traced here: 34.3 us
  waiting for transfers between devices  11.1 us (32%)
  starting transfers between devices  10.2 us (30%)
  Pallas kernels  9.84 us (29%)
  other arithmetic  2.19 us (6%)
  between operations  0.79 us (2%)
    ppermute x12, waiting for transfers between devices, moved(): return lax.ppermute(value, ('blk', 'rows'), pairs)  11.1 us
    ppermute x12, starting transfers between devices, moved(): return lax.ppermute(value, ('blk', 'rows'), pairs)  10.2 us
    pallas_call x1, Pallas kernels, per_device(): pl.pallas_call(functools.partial(first_kernel, size), out_shape=(jax.Shap...  5.29 us
    pallas_call x1, Pallas kernels, per_device(): pl.pallas_call(second_kernel, out_shape=(piece,) * 4, in_specs=[VMEM] * 5...  3.32 us
    pallas_call x1, Pallas kernels, per_device(): pl.pallas_call(last_kernel, out_shape=jax.ShapeDtypeStruct(latent.shape,...  1.22 us
    convert_element_type x1, other arithmetic, per_device(): lowered = lax.optimization_barrier(latent.astype(BF16))  0.99 us
  transfers between devices with their start and end apart: 12, of which 6 were waited for; matrix products, arithmetic and copies ran while one was open for 4% of the time, Pallas kernels for 15%

profile of v2, /device:TPU:0, one launch (start us, length us, event | category | flops | bytes accessed | tf_op | source)
XLA Modules:
  0.0 34.3 jit_solution(2692245102149278223)
XLA Ops:
  0.0 1.0 %convert_element_type.10.lowered = bf16[4,32,640]{2,1,0:T(8,128)(2,1)S(1)} convert(f32[4,32,640]{2,1,0:T(8,128)} %latent.1) | non-fusion elementwise | flops 81920 | bytes 491520 | tf_op jit(solution)/shard_map/convert_element_type | solution.py:206
  1.0 5.1 %collective-permute-start.2 = (bf16[4,32,640]{2,1,0:T(8,128)(2,1)S(1)}, bf16[4,32,640]{2,1,0:T(8,128)(2,1)S(1)}, u32[]{:S(2)}, u32[]{:S(2)}) collective-permute-start(bf16[4,32,640]{2,1,0:T(8,128)(2,1)S(1)} %convert_element_type.10.lowered), channel_id=1, source_target_pairs={{0,12},{1,13},{2,6},{3,7},{4,0},{5,1},{6,10},{7,11},{8,4},{9,5},{1... | collective-permute-start | bytes 491528 | tf_op jit(solution)/shard_map/ppermute | solution.py:27
  6.1 0.0 collective-permute-start.4
  6.1 0.7 %convert_bitcast_fusion = f32[64]{0:T(128)S(1)} fusion(s32[1,64]{1,0:T(1,128)} %param.10), kind=kLoop, calls=%fused_computation.11 | loop fusion | flops 64 | bytes 512 | tf_op jit(solution)/shard_map/convert_element_type | solution.py:209
  6.8 1.0 %collective-permute-start.1 = (f32[64]{0:T(128)S(1)}, f32[64]{0:T(128)S(1)}, u32[]{:S(2)}, u32[]{:S(2)}) collective-permute-start(f32[64]{0:T(128)S(1)} %convert_bitcast_fusion), channel_id=1, source_target_pairs={{0,4},{1,5},{2,6},{3,7},{4,8},{5,9},{6,10},{7,11},{8,12},{9,13},{1... | collective-permute-start | bytes 776 | tf_op jit(solution)/shard_map/ppermute | solution.py:27
  7.8 1.0 %collective-permute-start = (f32[64]{0:T(128)S(1)}, f32[64]{0:T(128)S(1)}, u32[]{:S(2)}, u32[]{:S(2)}) collective-permute-start(f32[64]{0:T(128)S(1)} %convert_bitcast_fusion), channel_id=1, source_target_pairs={{0,2},{1,3},{2,4},{3,5},{4,6},{5,7},{6,8},{7,9},{8,10},{9,11},{10,... | collective-permute-start | bytes 776 | tf_op jit(solution)/shard_map/ppermute | solution.py:27
  9.5 0.1 select_select_fusion.edges
  9.6 0.0 collective-permute-done.2
  9.7 0.1 broadcast_select_fusion.mix
  9.7 0.1 collective-permute-start.3
  9.8 2.0 %collective-permute-done.4.full = bf16[4,32,640]{2,1,0:T(8,128)(2,1)S(1)} collective-permute-done((bf16[4,32,640]{2,1,0:T(8,128)(2,1)S(1)}, bf16[4,32,640]{2,1,0:T(8,128)(2,1)S(1)}, u32[]{:S(2)}, u32[]{:S(2)}) %collective-permute-start.4) | collective-permute-done | bytes 163872 | tf_op jit(solution)/shard_map/ppermute | solution.py:27
  11.8 0.0 collective-permute-done.3.mix_other
  11.8 1.4 %collective-permute-done.5.full_other = bf16[4,32,640]{2,1,0:T(8,128)(2,1)S(1)} collective-permute-done((bf16[4,32,640]{2,1,0:T(8,128)(2,1)S(1)}, bf16[4,32,640]{2,1,0:T(8,128)(2,1)S(1)}, u32[]{:S(2)}, u32[]{:S(2)}) %collective-permute-start.5) | collective-permute-done | bytes 163872 | tf_op jit(solution)/shard_map/ppermute | solution.py:27
  13.2 5.3 %shard_map.82 = (bf16[8,64,320]{2,1,0:T(8,128)(2,1)S(1)}, bf16[3,3,320,640]{3,2,1,0:T(8,128)(2,1)S(1)}) custom-call(bf16[4,32,640]{2,1,0:T(8,128)(2,1)S(1)} %broadcast_select_fusion.mix, bf16[4,32,640]{2,1,0:T(8,128)(2,1)S(1)} %collective-permute-done.3.mix_other, bf16[4,32,640]{2,1,0:T(8,128)(2,1)S(1)} %collective-permute-done.4.full, ...), custom_call_target="tpu_custom_call" | custom-call | tf_op jit(solution)/shard_map/pallas_call | solution.py:233
  18.5 0.0 copy-start
  18.5 0.2 collective-permute-start.6
  18.7 0.0 collective-permute-done.1
  18.7 0.0 collective-permute-done
  18.7 0.2 select_reduce_fusion
  19.0 0.1 slice.15
  19.0 1.3 %collective-permute-done.6.other = bf16[8,64,320]{2,1,0:T(8,128)(2,1)S(1)} collective-permute-done((bf16[8,64,320]{2,1,0:T(8,128)(2,1)S(1)}, bf16[8,64,320]{2,1,0:T(8,128)(2,1)S(1)}, u32[]{:S(2)}, u32[]{:S(2)}) %collective-permute-start.6) | collective-permute-done | bytes 327712 | tf_op jit(solution)/shard_map/ppermute | solution.py:27
  20.3 0.1 broadcast_in_dim.85.share
  20.4 3.3 %shard_map.83 = (bf16[4,32,320]{2,1,0:T(8,128)(2,1)S(1)}, bf16[4,32,320]{2,1,0:T(8,128)(2,1)S(1)}, bf16[4,32,320]{2,1,0:T(8,128)(2,1)S(1)}, bf16[4,32,320]{2,1,0:T(8,128)(2,1)S(1)}) custom-call(bf16[8,64,320]{2,1,0:T(8,128)(2,1)S(1)} %get-tuple-element.11.own, bf16[8,64,320]{2,1,0:T(8,128)(2,1)S(1)} %collective-permute-done.6.other, ...), custom_call_target="tpu_custom_call" | custom-call | tf_op jit(solution)/shard_map/pallas_call | solution.py:258
  23.7 0.2 collective-permute-start.7
  23.9 2.5 %collective-permute-start.10 = (bf16[4,32,320]{2,1,0:T(8,128)(2,1)S(1)}, bf16[4,32,320]{2,1,0:T(8,128)(2,1)S(1)}, u32[]{:S(2)}, u32[]{:S(2)}) collective-permute-start(bf16[4,32,320]{2,1,0:T(8,128)(2,1)S(1)} %get-tuple-element.15), channel_id=1, source_target_pairs={{0,2},{1,3},{2,0},{3,1},{4,6},{5,7},{6,4},{7,5},{8,10},{9,11},{10,... | collective-permute-start | bytes 245768 | tf_op jit(solution)/shard_map/ppermute | solution.py:27
  26.4 0.1 add_divide_fusion.inverse
  26.5 3.4 %collective-permute-done.10.full_same = bf16[4,32,320]{2,1,0:T(8,128)(2,1)S(1)} collective-permute-done((bf16[4,32,320]{2,1,0:T(8,128)(2,1)S(1)}, bf16[4,32,320]{2,1,0:T(8,128)(2,1)S(1)}, u32[]{:S(2)}, u32[]{:S(2)}) %collective-permute-start.10) | collective-permute-done | bytes 81952 | tf_op jit(solution)/shard_map/ppermute | solution.py:27
  29.9 1.6 %collective-permute-done.11.full_cross = bf16[4,32,320]{2,1,0:T(8,128)(2,1)S(1)} collective-permute-done((bf16[4,32,320]{2,1,0:T(8,128)(2,1)S(1)}, bf16[4,32,320]{2,1,0:T(8,128)(2,1)S(1)}, u32[]{:S(2)}, u32[]{:S(2)}) %collective-permute-start.11) | collective-permute-done | bytes 81952 | tf_op jit(solution)/shard_map/ppermute | solution.py:27
  31.5 0.0 collective-permute-done.7.mix_core
  31.5 1.5 %collective-permute-done.8.mix_same = bf16[4,32,320]{2,1,0:T(8,128)(2,1)S(1)} collective-permute-done((bf16[4,32,320]{2,1,0:T(8,128)(2,1)S(1)}, bf16[4,32,320]{2,1,0:T(8,128)(2,1)S(1)}, u32[]{:S(2)}, u32[]{:S(2)}) %collective-permute-start.8) | collective-permute-done | bytes 81952 | tf_op jit(solution)/shard_map/ppermute | solution.py:27
  33.0 0.0 collective-permute-done.9.mix_cross
  33.1 1.2 %shard_map.84 = f32[4,32,640]{2,1,0:T(8,128)} custom-call(f32[4,32,640]{2,1,0:T(8,128)S(1)} %copy-done, bf16[4,32,640]{2,1,0:T(8,128)(2,1)S(1)} %convert_element_type.10.lowered, f32[3,64,128]{2,1,0:T(8,128)S(1)} %select_select_fusion.edges, f32[32,128]{1,0:T(8,128)S(1)} %add_divide_fusion.inverse, bf16[4,32,320]{2,1,0:T(8,128)(2,1)S(1)} %get-tuple-element.13.mix_own, ...), custom_call_target="tpu_custom_call" | custom-call | tf_op jit(solution)/shard_map/pallas_call | solution.py:275
  (15 shorter events, 0.1 us)
Async XLA Ops:
  1.0 8.6 %collective-permute-start.2 = (bf16[4,32,640]{2,1,0:T(8,128)(2,1)S(1)}, bf16[4,32,640]{2,1,0:T(8,128)(2,1)S(1)}, u32[]{:S(2)}, u32[]{:S(2)}) collective-permute-start(bf16[4,32,640]{2,1,0:T(8,128)(2,1)S(1)} %convert_element_type.10.lowered), channel_id=1, source_target_pairs={{0,12},{1,13},{2,6},{3,7},{4,0},{5,1},{6,10},{7,11},{8,4},{9,5},{1... | collective-permute-start | bytes 491528 | tf_op jit(solution)/shard_map/ppermute | solution.py:27
  6.1 5.7 %collective-permute-start.4 = (bf16[4,32,640]{2,1,0:T(8,128)(2,1)S(1)}, bf16[4,32,640]{2,1,0:T(8,128)(2,1)S(1)}, u32[]{:S(2)}, u32[]{:S(2)}) collective-permute-start(bf16[4,32,640]{2,1,0:T(8,128)(2,1)S(1)} %convert_element_type.10.lowered), channel_id=1, source_target_pairs={{0,2},{1,3},{2,0},{3,1},{4,6},{5,7},{6,4},{7,5},{8,10},{9,11},{10,... | collective-permute-start | bytes 491528 | tf_op jit(solution)/shard_map/ppermute | solution.py:27
  6.8 11.9 %collective-permute-start.1 = (f32[64]{0:T(128)S(1)}, f32[64]{0:T(128)S(1)}, u32[]{:S(2)}, u32[]{:S(2)}) collective-permute-start(f32[64]{0:T(128)S(1)} %convert_bitcast_fusion), channel_id=1, source_target_pairs={{0,4},{1,5},{2,6},{3,7},{4,8},{5,9},{6,10},{7,11},{8,12},{9,13},{1... | collective-permute-start | bytes 776 | tf_op jit(solution)/shard_map/ppermute | solution.py:27
  7.8 10.9 %collective-permute-start = (f32[64]{0:T(128)S(1)}, f32[64]{0:T(128)S(1)}, u32[]{:S(2)}, u32[]{:S(2)}) collective-permute-start(f32[64]{0:T(128)S(1)} %convert_bitcast_fusion), channel_id=1, source_target_pairs={{0,2},{1,3},{2,4},{3,5},{4,6},{5,7},{6,8},{7,9},{8,10},{9,11},{10,... | collective-permute-start | bytes 776 | tf_op jit(solution)/shard_map/ppermute | solution.py:27
  9.7 2.1 %collective-permute-start.3 = (bf16[4,32,640]{2,1,0:T(8,128)(2,1)S(1)}, bf16[4,32,640]{2,1,0:T(8,128)(2,1)S(1)}, u32[]{:S(2)}, u32[]{:S(2)}) collective-permute-start(bf16[4,32,640]{2,1,0:T(8,128)(2,1)S(1)} %broadcast_select_fusion.mix), channel_id=1, source_target_pairs={{0,1},{1,0},{2,3},{3,2},{4,5},{5,4},{6,7},{7,6},{8,9},{9,8},{10,11... | collective-permute-start | bytes 491528 | tf_op jit(solution)/shard_map/ppermute | solution.py:27
  11.8 1.4 %collective-permute-start.5 = (bf16[4,32,640]{2,1,0:T(8,128)(2,1)S(1)}, bf16[4,32,640]{2,1,0:T(8,128)(2,1)S(1)}, u32[]{:S(2)}, u32[]{:S(2)}) collective-permute-start(bf16[4,32,640]{2,1,0:T(8,128)(2,1)S(1)} %collective-permute-done.4.full), channel_id=1, source_target_pairs={{0,1},{1,0},{2,3},{3,2},{4,5},{5,4},{6,7},{7,6},{8,9},{9,8},{10,11... | collective-permute-start | bytes 491528 | tf_op jit(solution)/shard_map/ppermute | solution.py:27
  13.2 5.5 %copy-start.1 = (s32[1,64]{1,0:T(1,128)S(1)}, s32[1,64]{1,0:T(1,128)}, u32[]{:S(2)}) copy-start(s32[1,64]{1,0:T(1,128)} %param.10) | copy-start | bytes 772
  18.5 14.6 %copy-start = (f32[4,32,640]{2,1,0:T(8,128)S(1)}, f32[4,32,640]{2,1,0:T(8,128)}, u32[]{:S(2)}) copy-start(f32[4,32,640]{2,1,0:T(8,128)} %latent.1) | copy-start | bytes 983044
  18.5 1.8 %collective-permute-start.6 = (bf16[8,64,320]{2,1,0:T(8,128)(2,1)S(1)}, bf16[8,64,320]{2,1,0:T(8,128)(2,1)S(1)}, u32[]{:S(2)}, u32[]{:S(2)}) collective-permute-start(bf16[8,64,320]{2,1,0:T(8,128)(2,1)S(1)} %get-tuple-element.11.own), channel_id=1, source_target_pairs={{0,1},{1,0},{2,3},{3,2},{4,5},{5,4},{6,7},{7,6},{8,9},{9,8},{10,11... | collective-permute-start | bytes 983048 | tf_op jit(solution)/shard_map/ppermute | solution.py:27
  23.7 7.8 %collective-permute-start.7 = (bf16[4,32,320]{2,1,0:T(8,128)(2,1)S(1)}, bf16[4,32,320]{2,1,0:T(8,128)(2,1)S(1)}, u32[]{:S(2)}, u32[]{:S(2)}) collective-permute-start(bf16[4,32,320]{2,1,0:T(8,128)(2,1)S(1)} %get-tuple-element.14), channel_id=1, source_target_pairs={{0,1},{1,0},{2,3},{3,2},{4,5},{5,4},{6,7},{7,6},{8,9},{9,8},{10,11... | collective-permute-start | bytes 245768 | tf_op jit(solution)/shard_map/ppermute | solution.py:27
  23.9 9.1 %collective-permute-start.9 = (bf16[4,32,320]{2,1,0:T(8,128)(2,1)S(1)}, bf16[4,32,320]{2,1,0:T(8,128)(2,1)S(1)}, u32[]{:S(2)}, u32[]{:S(2)}) collective-permute-start(bf16[4,32,320]{2,1,0:T(8,128)(2,1)S(1)} %get-tuple-element.14), channel_id=1, source_target_pairs={{0,5},{1,4},{2,15},{3,14},{4,9},{5,8},{6,3},{7,2},{8,13},{9,12},{1... | collective-permute-start | bytes 245768 | tf_op jit(solution)/shard_map/ppermute | solution.py:27
  23.9 6.0 %collective-permute-start.10 = (bf16[4,32,320]{2,1,0:T(8,128)(2,1)S(1)}, bf16[4,32,320]{2,1,0:T(8,128)(2,1)S(1)}, u32[]{:S(2)}, u32[]{:S(2)}) collective-permute-start(bf16[4,32,320]{2,1,0:T(8,128)(2,1)S(1)} %get-tuple-element.15), channel_id=1, source_target_pairs={{0,2},{1,3},{2,0},{3,1},{4,6},{5,7},{6,4},{7,5},{8,10},{9,11},{10,... | collective-permute-start | bytes 245768 | tf_op jit(solution)/shard_map/ppermute | solution.py:27
  26.4 5.1 %collective-permute-start.11 = (bf16[4,32,320]{2,1,0:T(8,128)(2,1)S(1)}, bf16[4,32,320]{2,1,0:T(8,128)(2,1)S(1)}, u32[]{:S(2)}, u32[]{:S(2)}) collective-permute-start(bf16[4,32,320]{2,1,0:T(8,128)(2,1)S(1)} %get-tuple-element.16), channel_id=1, source_target_pairs={{0,3},{1,2},{2,1},{3,0},{4,7},{5,6},{6,5},{7,4},{8,11},{9,10},{10,... | collective-permute-start | bytes 245768 | tf_op jit(solution)/shard_map/ppermute | solution.py:27
  26.4 6.6 %collective-permute-start.8 = (bf16[4,32,320]{2,1,0:T(8,128)(2,1)S(1)}, bf16[4,32,320]{2,1,0:T(8,128)(2,1)S(1)}, u32[]{:S(2)}, u32[]{:S(2)}) collective-permute-start(bf16[4,32,320]{2,1,0:T(8,128)(2,1)S(1)} %get-tuple-element.13.mix_own), channel_id=1, source_target_pairs={{0,4},{1,5},{2,14},{3,15},{4,8},{5,9},{6,2},{7,3},{8,12},{9,13},{1... | collective-permute-start | bytes 245768 | tf_op jit(solution)/shard_map/ppermute | solution.py:27

commit v3 on v2

--- a/solution.py
+++ b/solution.py
@@ -60,11 +60,9 @@
     return half + half * jnp.tanh(half)
 
 
-def nine_taps(frame, weight, acc, arriving=()):
+def nine_taps(frame, weight, acc):
     height, columns = frame.shape[0] - 2, frame.shape[1]
     for a in range(3):
-        if arriving:
-            arriving[a].wait()
         patch = frame[a : a + height].reshape(height * columns, frame.shape[2])
         taps = weight[a].reshape(-1, weight.shape[3])
         part = lax.dot_general(patch, taps, (((1,), (1,)), ((), ())), preferred_element_type=F32)
@@ -81,22 +79,79 @@
     return block[:, outs : 2 * outs] + left + right
 
 
+TAIL = 8
+
+
+def packed(rows, columns, outs, tail=0):
+    return jax.ShapeDtypeStruct((rows * columns // 2 + tail, 2 * outs), BF16)
+
+
+def put(ref, row, rows, value):
+    half, outs, columns = rows // 2, ref.shape[1] // 2, value.shape[0]
+    spot = (row % half) * columns
+    ref[spot : spot + columns, (row // half) * outs : (row // half + 1) * outs] = value
+
+
+def get(ref, row, rows, columns):
+    half, outs = rows // 2, ref.shape[1] // 2
+    spot = (row % half) * columns
+    return ref[spot : spot + columns, (row // half) * outs : (row // half + 1) * outs]
+
+
 def half_of(row, outs, core):
     return jnp.where(core == 0, row[:, :outs], row[:, outs:])
 
 
-def first_kernel(size, mix, mix_other, full, full_other, edges, w_one, w_two, gain_one, gain_two, time_bias, out, w_next, frame, acc, hidden, w, one_in, two_in, bias_in, sems):
+def lower_kernel(latent, counts, lowered, load, held, counted, sems):
+    rows, cols, _ = latent.shape
+    copies = [pltpu.make_async_copy(latent.at[row], held.at[row], sems.at[row]) for row in range(rows)]
+    copies.append(pltpu.make_async_copy(counts, counted, sems.at[rows]))
+    for copy in copies:
+        copy.start()
+    for row in range(rows):
+        copies[row].wait()
+        value = held[row].astype(BF16)
+        lowered[row] = value
+        load[row * cols : (row + 1) * cols] = value
+    copies[rows].wait()
+    put_counts(load, rows * cols, counted[...].astype(F32))
+
+
+def ready_kernel(w_one, w, sem):
+    copy = pltpu.make_async_copy(w_one, w, sem)
+    copy.start()
+    copy.wait()
+
+
+def put_counts(ref, start, row):
+    tail = ref.shape[0] - start
+    room = ref.shape[1] - row.shape[1]
+    wide = jnp.concatenate([row, jnp.zeros((1, room), F32)], axis=1)
+    ref[start:] = jnp.broadcast_to(wide, (tail, ref.shape[1])).astype(BF16)
+
+
+def get_counts(ref, start, columns):
+    return ref[start : start + 8].astype(F32)[:1, :columns]
+
+
+def by_column(values, anchor, columns):
+    spot = lax.broadcasted_iota(jnp.int32, (columns, columns), 0) - anchor
+    spot = jnp.where(spot < 0, spot + columns, spot)
+    picked = spot == lax.broadcasted_iota(jnp.int32, (columns, columns), 1)
+    return jnp.sum(jnp.where(picked, values, 0.0), axis=1, keepdims=True)
+
+
+def first_kernel(size, mix, mix_other, full, full_other, edges, w, w_two, gain_one, gain_two, time_bias, out, w_next, frame, acc, hidden, one_in, two_in, bias_in, sems):
     core = lax.axis_index("rows")
     small = [
-        pltpu.make_async_copy(source, target, sems.at[4 + i])
+        pltpu.make_async_copy(source, target, sems.at[1 + i])
         for i, (source, target) in enumerate(((gain_one, one_in), (gain_two, two_in), (time_bias, bias_in)))
     ]
-    taps = [pltpu.make_async_copy(w_one.at[a], w.at[a], sems.at[a]) for a in range(3)]
-    later = pltpu.make_async_copy(w_two, w_next, sems.at[3])
-    for copy in small + taps + [later]:
+    later = pltpu.make_async_copy(w_two, w_next, sems.at[0])
+    for copy in small + [later]:
         copy.start()
     rows, half_cols, channels = mix.shape
-    columns, height, outs = 2 * half_cols, 2 * rows, out.shape[2]
+    columns, height, outs = 2 * half_cols, 2 * rows, out.shape[1] // 2
     count = height * columns * size
     summed = jnp.zeros((1, channels), F32)
     squares = jnp.zeros((1, channels), F32)
@@ -115,7 +170,7 @@
         for row in range(rows):
             v = ref[row].astype(F32)
             frame[start + row, col : col + half_cols] = silu((v - mean) * scale).astype(BF16)
-    nine_taps(frame, w, acc, taps)
+    nine_taps(frame, w, acc)
     bias = half_of(bias_in[...].reshape(1, -1), outs, core)
     summed = jnp.zeros((1, outs), F32)
     squares = jnp.zeros((1, outs), F32)
@@ -127,13 +182,15 @@
     mean, scale = group_scale(summed, squares, count, size)
     scale = scale * half_of(two_in[...].reshape(1, -1), outs, core)
     for row in range(height):
-        out[row] = silu((hidden[row] - mean) * scale).astype(BF16)
+        put(out, row, height, silu((hidden[row] - mean) * scale).astype(BF16))
     later.wait()
 
 
-def second_kernel(own, other, w, edges, share, mix_same, mix_cross, full_same, full_cross, frame, acc, result):
+def second_kernel(anchor_ref, own, other, w, edges, counts, load, mix_same, mix_cross, full_same, full_cross, frame, acc, result):
     core = lax.axis_index("rows")
-    height, columns, outs = own.shape
+    odd = (lax.axis_index("blk") & 1) == 1
+    height, columns = frame.shape[0] - 2, frame.shape[1]
+    outs = own.shape[1] // 2
     rows, half_cols = height // 2, columns // 2
     frame[0] = jnp.zeros(frame.shape[1:], BF16)
     frame[height + 1] = jnp.zeros(frame.shape[1:], BF16)
@@ -141,15 +198,16 @@
     @pl.when(core == 0)
     def _():
         for row in range(height):
-            frame[1 + row] = jnp.concatenate([own[row], other[row]], axis=1)
+            frame[1 + row] = jnp.concatenate([get(ref, row, height, columns) for ref in (own, other)], axis=1)
 
     @pl.when(core == 1)
     def _():
         for row in range(height):
-            frame[1 + row] = jnp.concatenate([other[row], own[row]], axis=1)
+            frame[1 + row] = jnp.concatenate([get(ref, row, height, columns) for ref in (other, own)], axis=1)
 
     nine_taps(frame, w, acc)
-    part = jnp.broadcast_to(share[:, :1], (columns, outs))
+    own_row = jnp.where(odd, get_counts(load, rows * half_cols, columns), counts[...].astype(F32))
+    part = jnp.broadcast_to(by_column(own_row, anchor_ref[0], columns), (columns, outs))
     for row in range(height):
         result[row] = joined_taps(acc, row, columns, outs, edges) * part
     for out, flip, col in (
@@ -160,39 +218,54 @@
     ):
         start = rows * (core ^ flip)
         for row in range(rows):
-            out[row] = result[start + row, col : col + half_cols].astype(BF16)
-
-
-def last_kernel(latent, lowered, edges, inverse, mix_own, mix_core, mix_same, mix_cross, full_same, full_cross, out):
+            put(out, row, rows, result[start + row, col : col + half_cols].astype(BF16))
+    for out in (mix_same, full_same):
+        put_counts(out, rows * half_cols // 2, own_row)
+
+
+def last_kernel(anchor_ref, latent, lowered, counts, load, mix_own, mix_core, mix_same, mix_cross, full_same, full_cross, out, done, sems):
     core = lax.axis_index("rows")
-    odd = lax.axis_index("blk") & 1
-    rows, cols, outs = mix_own.shape
-    late = jnp.broadcast_to(edges[2, :cols, :1], (cols, outs)) > 0.5
-    keep = late ^ (odd == 1)
+    odd = (lax.axis_index("blk") & 1) == 1
+    anchor = anchor_ref[0]
+    rows, cols, outs = latent.shape[0], latent.shape[1], latent.shape[2] // 2
+    late = lax.broadcasted_iota(jnp.int32, (cols, outs), 0) >= anchor
+    keep = late ^ odd
+    tail = rows * cols // 2
+    own_row = jnp.where(odd, get_counts(load, rows * cols, 2 * cols), counts[...].astype(F32))
+    always = by_column(get_counts(full_same, tail, 2 * cols), anchor, 2 * cols)[cols:]
+    ours = by_column(own_row, anchor, 2 * cols)[:cols]
+    theirs = by_column(get_counts(mix_same, tail, 2 * cols), anchor, 2 * cols)[:cols]
+    weight = always + jnp.where(keep[:, :1], ours, theirs)
     own_scale = math.sqrt(0.7 / 0.5)
     join_scale = math.sqrt(0.3) - math.sqrt(0.7 / 0.5) * math.sqrt(0.5)
-    part = join_scale * inverse[:, :1]
+    part = join_scale / weight
+
+    copies = [pltpu.make_async_copy(done.at[row], out.at[row], sems.at[row]) for row in range(rows)]
+
+    def summed(row, own, far, full):
+        own, far, full = (get(ref, row, rows, cols).astype(F32) for ref in (own, far, full))
+        return jnp.where(keep, own, far) + full
+
     for row in range(rows):
-        same = jnp.where(keep, mix_own[row].astype(F32), mix_same[row].astype(F32)) + full_same[row].astype(F32)
-        cross = jnp.where(keep, mix_core[row].astype(F32), mix_cross[row].astype(F32)) + full_cross[row].astype(F32)
+        same = summed(row, mix_own, mix_same, full_same)
+        cross = summed(row, mix_core, mix_cross, full_cross)
         base = own_scale * latent[row] + join_scale * lowered[row].astype(F32)
 
         @pl.when(core == 0)
         def _():
-            out[row] = base + part * jnp.concatenate([same, cross], axis=1)
+            done[row] = base + part * jnp.concatenate([same, cross], axis=1)
 
         @pl.when(core == 1)
         def _():
-            out[row] = base + part * jnp.concatenate([cross, same], axis=1)
-
-
-def by_column(values, anchor):
-    columns = values.shape[0]
-    spot = lax.broadcasted_iota(jnp.int32, (columns, columns), 0) - anchor
-    spot = jnp.where(spot < 0, spot + columns, spot)
-    picked = spot == lax.broadcasted_iota(jnp.int32, (columns, columns), 1)
-    placed = jnp.sum(jnp.where(picked, values[None, :], 0.0), axis=1)
-    return jnp.broadcast_to(placed[:, None], (columns, 128))
+            done[row] = base + part * jnp.concatenate([cross, same], axis=1)
+
+        copies[row].start()
+    for copy in copies:
+        copy.wait()
+
+
+def in_hbm(value):
+    return pltpu.with_memory_space_constraint(value, pltpu.HBM)
 
 
 def per_device(latent, offset, counts, conv_one, conv_two, gain_one, gain_two, time_bias):
@@ -203,19 +276,31 @@
     odd = (lax.axis_index("blk") & 1) == 1
     anchor = offset[0]
 
-    lowered = lax.optimization_barrier(latent.astype(BF16))
+    conv_one, conv_two = (jnp.swapaxes(v, 2, 3) for v in (conv_one, conv_two))
+    lowered, load, held, counted = pl.pallas_call(
+        lower_kernel,
+        out_shape=(
+            jax.ShapeDtypeStruct(latent.shape, BF16),
+            jax.ShapeDtypeStruct((rows * stride + TAIL, channels), BF16),
+            jax.ShapeDtypeStruct(latent.shape, F32),
+            jax.ShapeDtypeStruct(counts.shape, counts.dtype),
+        ),
+        in_specs=[HBM] * 2,
+        out_specs=(VMEM,) * 4,
+        scratch_shapes=[pltpu.SemaphoreType.DMA((rows + 1,))],
+        compiler_params=PARAMS,
+    )(in_hbm(latent), in_hbm(counts))
+    w_first = pl.pallas_call(
+        ready_kernel,
+        out_shape=jax.ShapeDtypeStruct(conv_one.shape, BF16),
+        in_specs=[HBM],
+        out_specs=VMEM,
+        scratch_shapes=[pltpu.SemaphoreType.DMA],
+        compiler_params=PARAMS,
+    )(in_hbm(conv_one))
     full = moved(lowered, lambda b: b ^ 1, 0)
-    beyond = moved(lowered, lambda b: b + 2 if b % 2 else b - 2, 0)
-    row = counts[0].astype(F32)
-    row_one = moved(row, lambda b: b + 1, 0)
-    row_two = moved(row, lambda b: b + 2, 0)
-    share = by_column(jnp.where(odd, row_two, row), anchor)
-    now = by_column(row, anchor)[:stride]
-    then = by_column(row_two, anchor)[:stride]
-    always = by_column(row_one, anchor)[stride:]
-    col = lax.broadcasted_iota(jnp.int32, (stride, 1), 0)
-    inverse = 1.0 / (always + jnp.where(col >= anchor, now, then))
-
+    load = moved(load, lambda b: b + 2 if b % 2 else b - 2, 0)
+    beyond = load[: rows * stride].reshape(latent.shape)
     spot = lax.broadcasted_iota(jnp.int32, (3, columns, 128), 1)
     kind = lax.broadcasted_iota(jnp.int32, (3, columns, 128), 0)
     cut = jnp.where(kind == 0, spot == anchor, spot == jnp.where(anchor == 0, columns, anchor) - 1)
@@ -233,36 +318,32 @@
     own, w_next = pl.pallas_call(
         functools.partial(first_kernel, size),
         out_shape=(
-            jax.ShapeDtypeStruct((height, columns, outs), BF16),
+            packed(height, columns, outs),
             jax.ShapeDtypeStruct(weights, BF16),
         ),
-        in_specs=[VMEM] * 5 + [HBM] * 5,
+        in_specs=[VMEM] * 6 + [HBM] * 4,
         out_specs=(VMEM, VMEM),
         scratch_shapes=[
             frame,
             acc,
             result,
-            pltpu.VMEM(weights, BF16),
             pltpu.VMEM((channels,), F32),
             pltpu.VMEM((channels,), F32),
             pltpu.VMEM((channels,), F32),
-            pltpu.SemaphoreType.DMA((7,)),
+            pltpu.SemaphoreType.DMA((4,)),
         ],
         compiler_params=PARAMS,
-    )(mix, mix_other, full, full_other, edges, *[
-        pltpu.with_memory_space_constraint(v, pltpu.HBM)
-        for v in (jnp.swapaxes(conv_one, 2, 3), jnp.swapaxes(conv_two, 2, 3), gain_one, gain_two, time_bias)
-    ])
+    )(mix, mix_other, full, full_other, edges, w_first, *[in_hbm(v) for v in (conv_two, gain_one, gain_two, time_bias)])
     other = moved(own, lambda b: b, 1)
-    piece = jax.ShapeDtypeStruct((rows, stride, outs), BF16)
+    marked, plain = packed(rows, stride, outs, TAIL), packed(rows, stride, outs)
     mix_same, mix_cross, full_same, full_cross = pl.pallas_call(
         second_kernel,
-        out_shape=(piece,) * 4,
-        in_specs=[VMEM] * 5,
+        out_shape=(marked, plain, marked, plain),
+        in_specs=[SMEM] + [VMEM] * 6,
         out_specs=(VMEM,) * 4,
         scratch_shapes=[frame, acc, result],
         compiler_params=PARAMS,
-    )(own, other, w_next, edges, share)
+    )(offset, own, other, w_next, edges, counted, load)
 
     def aside(b):
         return b - 2 if b % 2 else b + 2
@@ -275,10 +356,11 @@
     return pl.pallas_call(
         last_kernel,
         out_shape=jax.ShapeDtypeStruct(latent.shape, F32),
-        in_specs=[VMEM] * 10,
-        out_specs=VMEM,
-        compiler_params=PARAMS,
-    )(latent, lowered, edges, inverse, mix_same, got_core, got_mix_same, got_mix_cross, got_full_same, got_full_cross)
+        in_specs=[SMEM] + [VMEM] * 10,
+        out_specs=HBM,
+        scratch_shapes=[pltpu.VMEM(latent.shape, F32), pltpu.SemaphoreType.DMA((rows,))],
+        compiler_params=PARAMS,
+    )(offset, held, lowered, counted, load, mix_same, got_core, got_mix_same, got_mix_cross, got_full_same, got_full_cross)
 
 
 def solution(mesh):

time: 34.4 us -> 35.5 us (1.032)
  the two profiles are of different devices: /device:TPU:0 before, /device:TPU:1 now
where the time goes in v3:
time: 35.5 us; the launch traced here: 35.3 us
  starting transfers between devices  14.1 us (40%)
  Pallas kernels  12.4 us (35%)
  waiting for transfers between devices  7.86 us (22%)
  between operations  0.75 us (2%)
    ppermute x10, starting transfers between devices, moved(): return lax.ppermute(value, ('blk', 'rows'), pairs)  14.1 us
    ppermute x10, waiting for transfers between devices, moved(): return lax.ppermute(value, ('blk', 'rows'), pairs)  7.86 us
    pallas_call x1, Pallas kernels, per_device(): pl.pallas_call(functools.partial(first_kernel, size), out_shape=(packed(h...  4.63 us
    pallas_call x1, Pallas kernels, per_device(): pl.pallas_call(second_kernel, out_shape=(marked, plain, marked, plain), i...  3.41 us
    pallas_call x1, Pallas kernels, per_device(): pl.pallas_call(ready_kernel, out_shape=jax.ShapeDtypeStruct(conv_one.shap...  2.05 us
    pallas_call x1, Pallas kernels, per_device(): pl.pallas_call(last_kernel, out_shape=jax.ShapeDtypeStruct(latent.shape,...  1.2 us
    pallas_call x1, Pallas kernels, per_device(): pl.pallas_call(lower_kernel, out_shape=(jax.ShapeDtypeStruct(latent.shape...  1.06 us
  transfers between devices with their start and end apart: 10, of which 5 were waited for; matrix products, arithmetic and copies ran while one was open for 1% of the time, Pallas kernels for 6%

profile of v3, /device:TPU:1, one launch (start us, length us, event | category | flops | bytes accessed | tf_op | source)
XLA Modules:
  0.0 35.3 jit_solution(7523093260419595621)
XLA Ops:
  0.0 1.1 %shard_map.82 = (bf16[4,32,640]{2,1,0:T(8,128)(2,1)S(1)}, bf16[136,640]{1,0:T(8,128)(2,1)S(1)}, f32[4,32,640]{2,1,0:T(8,128)S(1)}, s32[1,64]{1,0:T(1,128)S(1)}) custom-call(f32[4,32,640]{2,1,0:T(8,128)} %latent.1, s32[1,64]{1,0:T(1,128)} %counts.1), custom_call_target="tpu_custom_call" | custom-call | tf_op jit(solution)/shard_map/pallas_call | solution.py:280
  1.1 2.1 %collective-permute-start.2 = (bf16[4,32,640]{2,1,0:T(8,128)(2,1)S(1)}, bf16[4,32,640]{2,1,0:T(8,128)(2,1)S(1)}, u32[]{:S(2)}, u32[]{:S(2)}) collective-permute-start(bf16[4,32,640]{2,1,0:T(8,128)(2,1)S(1)} %get-tuple-element.16.lowered), channel_id=1, source_target_pairs={{0,2},{1,3},{2,0},{3,1},{4,6},{5,7},{6,4},{7,5},{8,10},{9,11},{10,... | collective-permute-start | bytes 491528 | tf_op jit(solution)/shard_map/ppermute | solution.py:27
  3.2 3.3 %collective-permute-start = (bf16[136,640]{1,0:T(8,128)(2,1)S(1)}, bf16[136,640]{1,0:T(8,128)(2,1)S(1)}, u32[]{:S(2)}, u32[]{:S(2)}) collective-permute-start(bf16[136,640]{1,0:T(8,128)(2,1)S(1)} %get-tuple-element.18), channel_id=1, source_target_pairs={{0,12},{1,13},{2,6},{3,7},{4,0},{5,1},{6,10},{7,11},{8,4},{9,5},{1... | collective-permute-start | bytes 522248 | tf_op jit(solution)/shard_map/ppermute | solution.py:27
  7.2 2.1 %shard_map.83.w = bf16[3,3,320,640]{3,2,1,0:T(8,128)(2,1)S(1)} custom-call(bf16[3,3,320,640]{3,2,1,0:T(8,128)(2,1)} %bitcast.8), custom_call_target="tpu_custom_call" | custom-call | tf_op jit(solution)/shard_map/pallas_call | solution.py:293
  9.3 0.0 collective-permute-done.2.full
  9.3 1.3 %collective-permute-start.3 = (bf16[4,32,640]{2,1,0:T(8,128)(2,1)S(1)}, bf16[4,32,640]{2,1,0:T(8,128)(2,1)S(1)}, u32[]{:S(2)}, u32[]{:S(2)}) collective-permute-start(bf16[4,32,640]{2,1,0:T(8,128)(2,1)S(1)} %collective-permute-done.2.full), channel_id=1, source_target_pairs={{0,1},{1,0},{2,3},{3,2},{4,5},{5,4},{6,7},{7,6},{8,9},{9,8},{10,11... | collective-permute-start | bytes 491528 | tf_op jit(solution)/shard_map/ppermute | solution.py:27
  10.6 0.0 collective-permute-done.load
  10.6 0.1 broadcast_select_fusion.mix
  10.7 0.6 %collective-permute-start.1 = (bf16[4,32,640]{2,1,0:T(8,128)(2,1)S(1)}, bf16[4,32,640]{2,1,0:T(8,128)(2,1)S(1)}, u32[]{:S(2)}, u32[]{:S(2)}) collective-permute-start(bf16[4,32,640]{2,1,0:T(8,128)(2,1)S(1)} %broadcast_select_fusion.mix), channel_id=1, source_target_pairs={{0,1},{1,0},{2,3},{3,2},{4,5},{5,4},{6,7},{7,6},{8,9},{9,8},{10,11... | collective-permute-start | bytes 491528 | tf_op jit(solution)/shard_map/ppermute | solution.py:27
  11.3 0.1 select_select_fusion.edges
  11.4 0.2 collective-permute-done.3.full_other
  11.6 0.7 %collective-permute-done.1.mix_other = bf16[4,32,640]{2,1,0:T(8,128)(2,1)S(1)} collective-permute-done((bf16[4,32,640]{2,1,0:T(8,128)(2,1)S(1)}, bf16[4,32,640]{2,1,0:T(8,128)(2,1)S(1)}, u32[]{:S(2)}, u32[]{:S(2)}) %collective-permute-start.1) | collective-permute-done | bytes 163872 | tf_op jit(solution)/shard_map/ppermute | solution.py:27
  12.3 4.6 %shard_map.84 = (bf16[256,640]{1,0:T(8,128)(2,1)S(1)}, bf16[3,3,320,640]{3,2,1,0:T(8,128)(2,1)S(1)}) custom-call(bf16[4,32,640]{2,1,0:T(8,128)(2,1)S(1)} %broadcast_select_fusion.mix, bf16[4,32,640]{2,1,0:T(8,128)(2,1)S(1)} %collective-permute-done.1.mix_other, bf16[4,32,640]{2,1,0:T(8,128)(2,1)S(1)} %collective-permute-done.2.full, ...), custom_call_target="tpu_custom_call" | custom-call | tf_op jit(solution)/shard_map/pallas_call | solution.py:318
  17.0 0.4 %collective-permute-start.4 = (bf16[256,640]{1,0:T(8,128)(2,1)S(1)}, bf16[256,640]{1,0:T(8,128)(2,1)S(1)}, u32[]{:S(2)}, u32[]{:S(2)}) collective-permute-start(bf16[256,640]{1,0:T(8,128)(2,1)S(1)} %get-tuple-element.19.own), channel_id=1, source_target_pairs={{0,1},{1,0},{2,3},{3,2},{4,5},{5,4},{6,7},{7,6},{8,9},{9,8},{10,11... | collective-permute-start | bytes 983048 | tf_op jit(solution)/shard_map/ppermute | solution.py:27
  17.4 1.3 %collective-permute-done.4.other = bf16[256,640]{1,0:T(8,128)(2,1)S(1)} collective-permute-done((bf16[256,640]{1,0:T(8,128)(2,1)S(1)}, bf16[256,640]{1,0:T(8,128)(2,1)S(1)}, u32[]{:S(2)}, u32[]{:S(2)}) %collective-permute-start.4) | collective-permute-done | bytes 327712 | tf_op jit(solution)/shard_map/ppermute | solution.py:27
  18.7 3.4 %shard_map.85 = (bf16[72,640]{1,0:T(8,128)(2,1)S(1)}, bf16[64,640]{1,0:T(8,128)(2,1)S(1)}, bf16[72,640]{1,0:T(8,128)(2,1)S(1)}, bf16[64,640]{1,0:T(8,128)(2,1)S(1)}) custom-call(s32[1]{0:T(128)} %copy.9.anchor_ref, bf16[256,640]{1,0:T(8,128)(2,1)S(1)} %get-tuple-element.19.own, bf16[256,640]{1,0:T(8,128)(2,1)S(1)} %collective-permute-done.4.other, ...), custom_call_target="tpu_custom_call" | custom-call | tf_op jit(solution)/shard_map/pallas_call | solution.py:339
  22.1 1.1 %collective-permute-start.8 = (bf16[72,640]{1,0:T(8,128)(2,1)S(1)}, bf16[72,640]{1,0:T(8,128)(2,1)S(1)}, u32[]{:S(2)}, u32[]{:S(2)}) collective-permute-start(bf16[72,640]{1,0:T(8,128)(2,1)S(1)} %get-tuple-element.23), channel_id=1, source_target_pairs={{0,2},{1,3},{2,0},{3,1},{4,6},{5,7},{6,4},{7,5},{8,10},{9,11},{10,... | collective-permute-start | bytes 276488 | tf_op jit(solution)/shard_map/ppermute | solution.py:27
  23.2 0.0 collective-permute-start.6
  23.2 5.3 %collective-permute-start.9 = (bf16[64,640]{1,0:T(8,128)(2,1)S(1)}, bf16[64,640]{1,0:T(8,128)(2,1)S(1)}, u32[]{:S(2)}, u32[]{:S(2)}) collective-permute-start(bf16[64,640]{1,0:T(8,128)(2,1)S(1)} %get-tuple-element.24), channel_id=1, source_target_pairs={{0,3},{1,2},{2,1},{3,0},{4,7},{5,6},{6,5},{7,4},{8,11},{9,10},{10,... | collective-permute-start | bytes 245768 | tf_op jit(solution)/shard_map/ppermute | solution.py:27
  28.4 0.0 collective-permute-start.7
  28.4 0.0 collective-permute-start.5
  28.4 2.1 %collective-permute-done.9.full_cross = bf16[64,640]{1,0:T(8,128)(2,1)S(1)} collective-permute-done((bf16[64,640]{1,0:T(8,128)(2,1)S(1)}, bf16[64,640]{1,0:T(8,128)(2,1)S(1)}, u32[]{:S(2)}, u32[]{:S(2)}) %collective-permute-start.9) | collective-permute-done | bytes 81952 | tf_op jit(solution)/shard_map/ppermute | solution.py:27
  30.5 3.5 %collective-permute-done.7.mix_cross = bf16[64,640]{1,0:T(8,128)(2,1)S(1)} collective-permute-done((bf16[64,640]{1,0:T(8,128)(2,1)S(1)}, bf16[64,640]{1,0:T(8,128)(2,1)S(1)}, u32[]{:S(2)}, u32[]{:S(2)}) %collective-permute-start.7) | collective-permute-done | bytes 81952 | tf_op jit(solution)/shard_map/ppermute | solution.py:27
  34.1 0.0 collective-permute-done.5.mix_core
  34.1 0.0 collective-permute-done.8.full_same
  34.1 0.0 collective-permute-done.6.mix_same
  34.1 1.2 %shard_map.86 = f32[4,32,640]{2,1,0:T(8,128)} custom-call(s32[1]{0:T(128)} %copy.9.anchor_ref, f32[4,32,640]{2,1,0:T(8,128)S(1)} %get-tuple-element.15.latent, bf16[4,32,640]{2,1,0:T(8,128)(2,1)S(1)} %get-tuple-element.16.lowered, s32[1,64]{1,0:T(1,128)S(1)} %get-tuple-element.17.counts, bf16[136,640]{1,0:T(8,128)(2,1)S(1)} %collective-permute-done.load, ...), custom_call_target="tpu_custom_call" | custom-call | tf_op jit(solution)/shard_map/pallas_call | solution.py:356
  (5 shorter events, 0.0 us)
Async XLA Ops:
  1.1 8.2 %collective-permute-start.2 = (bf16[4,32,640]{2,1,0:T(8,128)(2,1)S(1)}, bf16[4,32,640]{2,1,0:T(8,128)(2,1)S(1)}, u32[]{:S(2)}, u32[]{:S(2)}) collective-permute-start(bf16[4,32,640]{2,1,0:T(8,128)(2,1)S(1)} %get-tuple-element.16.lowered), channel_id=1, source_target_pairs={{0,2},{1,3},{2,0},{3,1},{4,6},{5,7},{6,4},{7,5},{8,10},{9,11},{10,... | collective-permute-start | bytes 491528 | tf_op jit(solution)/shard_map/ppermute | solution.py:27
  3.2 7.4 %collective-permute-start = (bf16[136,640]{1,0:T(8,128)(2,1)S(1)}, bf16[136,640]{1,0:T(8,128)(2,1)S(1)}, u32[]{:S(2)}, u32[]{:S(2)}) collective-permute-start(bf16[136,640]{1,0:T(8,128)(2,1)S(1)} %get-tuple-element.18), channel_id=1, source_target_pairs={{0,12},{1,13},{2,6},{3,7},{4,0},{5,1},{6,10},{7,11},{8,4},{9,5},{1... | collective-permute-start | bytes 522248 | tf_op jit(solution)/shard_map/ppermute | solution.py:27
  9.3 2.3 %collective-permute-start.3 = (bf16[4,32,640]{2,1,0:T(8,128)(2,1)S(1)}, bf16[4,32,640]{2,1,0:T(8,128)(2,1)S(1)}, u32[]{:S(2)}, u32[]{:S(2)}) collective-permute-start(bf16[4,32,640]{2,1,0:T(8,128)(2,1)S(1)} %collective-permute-done.2.full), channel_id=1, source_target_pairs={{0,1},{1,0},{2,3},{3,2},{4,5},{5,4},{6,7},{7,6},{8,9},{9,8},{10,11... | collective-permute-start | bytes 491528 | tf_op jit(solution)/shard_map/ppermute | solution.py:27
  10.7 1.6 %collective-permute-start.1 = (bf16[4,32,640]{2,1,0:T(8,128)(2,1)S(1)}, bf16[4,32,640]{2,1,0:T(8,128)(2,1)S(1)}, u32[]{:S(2)}, u32[]{:S(2)}) collective-permute-start(bf16[4,32,640]{2,1,0:T(8,128)(2,1)S(1)} %broadcast_select_fusion.mix), channel_id=1, source_target_pairs={{0,1},{1,0},{2,3},{3,2},{4,5},{5,4},{6,7},{7,6},{8,9},{9,8},{10,11... | collective-permute-start | bytes 491528 | tf_op jit(solution)/shard_map/ppermute | solution.py:27
  17.0 1.7 %collective-permute-start.4 = (bf16[256,640]{1,0:T(8,128)(2,1)S(1)}, bf16[256,640]{1,0:T(8,128)(2,1)S(1)}, u32[]{:S(2)}, u32[]{:S(2)}) collective-permute-start(bf16[256,640]{1,0:T(8,128)(2,1)S(1)} %get-tuple-element.19.own), channel_id=1, source_target_pairs={{0,1},{1,0},{2,3},{3,2},{4,5},{5,4},{6,7},{7,6},{8,9},{9,8},{10,11... | collective-permute-start | bytes 983048 | tf_op jit(solution)/shard_map/ppermute | solution.py:27
  22.1 12.0 %collective-permute-start.8 = (bf16[72,640]{1,0:T(8,128)(2,1)S(1)}, bf16[72,640]{1,0:T(8,128)(2,1)S(1)}, u32[]{:S(2)}, u32[]{:S(2)}) collective-permute-start(bf16[72,640]{1,0:T(8,128)(2,1)S(1)} %get-tuple-element.23), channel_id=1, source_target_pairs={{0,2},{1,3},{2,0},{3,1},{4,6},{5,7},{6,4},{7,5},{8,10},{9,11},{10,... | collective-permute-start | bytes 276488 | tf_op jit(solution)/shard_map/ppermute | solution.py:27
  23.2 10.9 %collective-permute-start.6 = (bf16[72,640]{1,0:T(8,128)(2,1)S(1)}, bf16[72,640]{1,0:T(8,128)(2,1)S(1)}, u32[]{:S(2)}, u32[]{:S(2)}) collective-permute-start(bf16[72,640]{1,0:T(8,128)(2,1)S(1)} %get-tuple-element.21.mix_own), channel_id=1, source_target_pairs={{0,4},{1,5},{2,14},{3,15},{4,8},{5,9},{6,2},{7,3},{8,12},{9,13},{1... | collective-permute-start | bytes 276488 | tf_op jit(solution)/shard_map/ppermute | solution.py:27
  23.2 7.4 %collective-permute-start.9 = (bf16[64,640]{1,0:T(8,128)(2,1)S(1)}, bf16[64,640]{1,0:T(8,128)(2,1)S(1)}, u32[]{:S(2)}, u32[]{:S(2)}) collective-permute-start(bf16[64,640]{1,0:T(8,128)(2,1)S(1)} %get-tuple-element.24), channel_id=1, source_target_pairs={{0,3},{1,2},{2,1},{3,0},{4,7},{5,6},{6,5},{7,4},{8,11},{9,10},{10,... | collective-permute-start | bytes 245768 | tf_op jit(solution)/shard_map/ppermute | solution.py:27
  28.4 5.7 %collective-permute-start.7 = (bf16[64,640]{1,0:T(8,128)(2,1)S(1)}, bf16[64,640]{1,0:T(8,128)(2,1)S(1)}, u32[]{:S(2)}, u32[]{:S(2)}) collective-permute-start(bf16[64,640]{1,0:T(8,128)(2,1)S(1)} %get-tuple-element.22), channel_id=1, source_target_pairs={{0,5},{1,4},{2,15},{3,14},{4,9},{5,8},{6,3},{7,2},{8,13},{9,12},{1... | collective-permute-start | bytes 245768 | tf_op jit(solution)/shard_map/ppermute | solution.py:27
  28.4 5.7 %collective-permute-start.5 = (bf16[64,640]{1,0:T(8,128)(2,1)S(1)}, bf16[64,640]{1,0:T(8,128)(2,1)S(1)}, u32[]{:S(2)}, u32[]{:S(2)}) collective-permute-start(bf16[64,640]{1,0:T(8,128)(2,1)S(1)} %get-tuple-element.22), channel_id=1, source_target_pairs={{0,1},{1,0},{2,3},{3,2},{4,5},{5,4},{6,7},{7,6},{8,9},{9,8},{10,11... | collective-permute-start | bytes 245768 | tf_op jit(solution)/shard_map/ppermute | solution.py:27

commit v4 on v3

--- a/solution.py
+++ b/solution.py
@@ -60,23 +60,40 @@
     return half + half * jnp.tanh(half)
 
 
-def nine_taps(frame, weight, acc):
-    height, columns = frame.shape[0] - 2, frame.shape[1]
-    for a in range(3):
-        patch = frame[a : a + height].reshape(height * columns, frame.shape[2])
-        taps = weight[a].reshape(-1, weight.shape[3])
-        part = lax.dot_general(patch, taps, (((1,), (1,)), ((), ())), preferred_element_type=F32)
-        if a == 0:
-            acc[...] = part
-        else:
-            acc[...] += part
+def arranged(weight, target, sem):
+    outs = weight.shape[2]
+    whole = outs // 128 * 128
+    copies, start = [], 0
+    for part in (slice(0, whole), slice(whole, outs)):
+        for b in range(3):
+            size = part.stop - part.start
+            for a in range(3):
+                spot = target.at[a, start : start + size]
+                copies.append(pltpu.make_async_copy(weight.at[a, b, part], spot, sem.at[len(copies)]))
+            start += size
+    return copies
+
+
+def nine_taps(frame, weight, acc, first=None):
+    height, columns, channels = frame.shape[0] - 2, frame.shape[1], frame.shape[2]
+    patch = jnp.concatenate(
+        [frame[a : a + height].reshape(height * columns, channels) for a in range(3)], axis=1
+    )
+    some = slice(None) if first is None else pl.ds(pl.multiple_of(first, 128), channels)
+    taps = jnp.concatenate([weight[a, :, some] for a in range(3)], axis=1)
+    acc[...] = lax.dot_general(patch, taps, (((1,), (1,)), ((), ())), preferred_element_type=F32)
 
 
 def joined_taps(acc, row, columns, outs, edges):
     block = acc[row * columns : (row + 1) * columns]
-    left = pltpu.roll(block[:, :outs], 1, 0) * edges[0][:, :1]
-    right = pltpu.roll(block[:, 2 * outs :], columns - 1, 0) * edges[1][:, :1]
-    return block[:, outs : 2 * outs] + left + right
+    whole = outs // 128 * 128
+
+    def joined(start, width):
+        first, second, third = (block[:, start + b * width : start + (b + 1) * width] for b in range(3))
+        cuts = [jnp.concatenate([edges[b]] * pl.cdiv(width, 128), axis=1)[:, :width] for b in range(2)]
+        return second + pltpu.roll(first, 1, 0) * cuts[0] + pltpu.roll(third, columns - 1, 0) * cuts[1]
+
+    return jnp.concatenate([joined(0, whole), joined(3 * whole, outs - whole)], axis=1)
 
 
 TAIL = 8
@@ -117,10 +134,20 @@
     put_counts(load, rows * cols, counted[...].astype(F32))
 
 
-def ready_kernel(w_one, w, sem):
-    copy = pltpu.make_async_copy(w_one, w, sem)
-    copy.start()
-    copy.wait()
+def ready_kernel(w_one, w_two, gain_one, gain_two, time_bias, w, w_next, table, one_in, two_in, bias_in, small_sems, sems):
+    small = [
+        pltpu.make_async_copy(source, target, small_sems.at[i])
+        for i, (source, target) in enumerate(((gain_one, one_in), (gain_two, two_in), (time_bias, bias_in)))
+    ]
+    copies = arranged(w_one, w, sems.at[0]) + arranged(w_two, w_next, sems.at[1])
+    for copy in small + copies:
+        copy.start()
+    table[...] = jnp.zeros_like(table)
+    for i, ref in enumerate((one_in, two_in, bias_in)):
+        small[i].wait()
+        table[i : i + 1] = ref[...].reshape(1, -1)
+    for copy in copies:
+        copy.wait()
 
 
 def put_counts(ref, start, row):
@@ -141,15 +168,8 @@
     return jnp.sum(jnp.where(picked, values, 0.0), axis=1, keepdims=True)
 
 
-def first_kernel(size, mix, mix_other, full, full_other, edges, w, w_two, gain_one, gain_two, time_bias, out, w_next, frame, acc, hidden, one_in, two_in, bias_in, sems):
+def first_kernel(size, mix, mix_other, full, full_other, edges, w, table, out, frame, acc, hidden):
     core = lax.axis_index("rows")
-    small = [
-        pltpu.make_async_copy(source, target, sems.at[1 + i])
-        for i, (source, target) in enumerate(((gain_one, one_in), (gain_two, two_in), (time_bias, bias_in)))
-    ]
-    later = pltpu.make_async_copy(w_two, w_next, sems.at[0])
-    for copy in small + [later]:
-        copy.start()
     rows, half_cols, channels = mix.shape
     columns, height, outs = 2 * half_cols, 2 * rows, out.shape[1] // 2
     count = height * columns * size
@@ -160,9 +180,7 @@
         summed += jnp.sum(v, axis=0, keepdims=True)
         squares += jnp.sum(v * v, axis=0, keepdims=True)
     mean, scale = group_scale(summed, squares, count, size)
-    for copy in small:
-        copy.wait()
-    scale = scale * one_in[...].reshape(1, -1)
+    scale = scale * table[0:1]
     frame[0] = jnp.zeros(frame.shape[1:], BF16)
     frame[height + 1] = jnp.zeros(frame.shape[1:], BF16)
     for ref, mine, col in ((mix, 0, 0), (full, 0, half_cols), (mix_other, 1, 0), (full_other, 1, half_cols)):
@@ -171,7 +189,7 @@
             v = ref[row].astype(F32)
             frame[start + row, col : col + half_cols] = silu((v - mean) * scale).astype(BF16)
     nine_taps(frame, w, acc)
-    bias = half_of(bias_in[...].reshape(1, -1), outs, core)
+    bias = half_of(table[2:3], outs, core)
     summed = jnp.zeros((1, outs), F32)
     squares = jnp.zeros((1, outs), F32)
     for row in range(height):
@@ -180,36 +198,64 @@
         summed += jnp.sum(v, axis=0, keepdims=True)
         squares += jnp.sum(v * v, axis=0, keepdims=True)
     mean, scale = group_scale(summed, squares, count, size)
-    scale = scale * half_of(two_in[...].reshape(1, -1), outs, core)
+    scale = scale * half_of(table[1:2], outs, core)
     for row in range(height):
         put(out, row, height, silu((hidden[row] - mean) * scale).astype(BF16))
-    later.wait()
-
-
-def second_kernel(anchor_ref, own, other, w, edges, counts, load, mix_same, mix_cross, full_same, full_cross, frame, acc, result):
+
+
+def near_channels(outs):
+    return outs // 128 * 128
+
+
+def near_kernel(own, w, edges, part, frame, acc):
+    core = lax.axis_index("rows")
+    height, columns, near = frame.shape[0] - 2, frame.shape[1], frame.shape[2]
+    outs = own.shape[1] // 2
+    for edge in (0, height + 1):
+        frame[edge] = jnp.zeros(frame.shape[1:], BF16)
+
+    @pl.when(core == 0)
+    def _():
+        for row in range(height):
+            frame[1 + row] = get(own, row, height, columns)[:, :near]
+
+    @pl.when(core == 1)
+    def _():
+        for row in range(height):
+            frame[1 + row] = get(own, row, height, columns)[:, outs - near :]
+
+    nine_taps(frame, w, acc, core * (2 * outs - near))
+    for row in range(height):
+        part[row] = joined_taps(acc, row, columns, outs, edges)
+
+
+def second_kernel(anchor_ref, own, other, w, edges, near_part, counts, load, mix_same, mix_cross, full_same, full_cross, frame, acc, result):
     core = lax.axis_index("rows")
     odd = (lax.axis_index("blk") & 1) == 1
     height, columns = frame.shape[0] - 2, frame.shape[1]
     outs = own.shape[1] // 2
+    near = near_channels(outs)
     rows, half_cols = height // 2, columns // 2
-    frame[0] = jnp.zeros(frame.shape[1:], BF16)
-    frame[height + 1] = jnp.zeros(frame.shape[1:], BF16)
+    for edge in (0, height + 1):
+        frame[edge] = jnp.zeros(frame.shape[1:], BF16)
 
     @pl.when(core == 0)
     def _():
         for row in range(height):
-            frame[1 + row] = jnp.concatenate([get(ref, row, height, columns) for ref in (own, other)], axis=1)
+            mine, theirs = (get(ref, row, height, columns) for ref in (own, other))
+            frame[1 + row] = jnp.concatenate([mine[:, near:], theirs], axis=1)
 
     @pl.when(core == 1)
     def _():
         for row in range(height):
-            frame[1 + row] = jnp.concatenate([get(ref, row, height, columns) for ref in (other, own)], axis=1)
-
-    nine_taps(frame, w, acc)
+            mine, theirs = (get(ref, row, height, columns) for ref in (own, other))
+            frame[1 + row] = jnp.concatenate([theirs, mine[:, : outs - near]], axis=1)
+
+    nine_taps(frame, w, acc, (1 - core) * near)
     own_row = jnp.where(odd, get_counts(load, rows * half_cols, columns), counts[...].astype(F32))
     part = jnp.broadcast_to(by_column(own_row, anchor_ref[0], columns), (columns, outs))
     for row in range(height):
-        result[row] = joined_taps(acc, row, columns, outs, edges) * part
+        result[row] = (joined_taps(acc, row, columns, outs, edges) + near_part[row]) * part
     for out, flip, col in (
         (mix_same, 0, 0),
         (mix_cross, 1, 0),
@@ -290,14 +336,16 @@
         scratch_shapes=[pltpu.SemaphoreType.DMA((rows + 1,))],
         compiler_params=PARAMS,
     )(in_hbm(latent), in_hbm(counts))
-    w_first = pl.pallas_call(
+    weights = jax.ShapeDtypeStruct((3, 3 * outs, channels), BF16)
+    vector = pltpu.VMEM((channels,), F32)
+    w_first, w_next, table = pl.pallas_call(
         ready_kernel,
-        out_shape=jax.ShapeDtypeStruct(conv_one.shape, BF16),
-        in_specs=[HBM],
-        out_specs=VMEM,
-        scratch_shapes=[pltpu.SemaphoreType.DMA],
-        compiler_params=PARAMS,
-    )(in_hbm(conv_one))
+        out_shape=(weights, weights, jax.ShapeDtypeStruct((8, channels), F32)),
+        in_specs=[HBM] * 5,
+        out_specs=(VMEM,) * 3,
+        scratch_shapes=[vector] * 3 + [pltpu.SemaphoreType.DMA((3,)), pltpu.SemaphoreType.DMA((2, 18))],
+        compiler_params=PARAMS,
+    )(*[in_hbm(v) for v in (conv_one, conv_two, gain_one, gain_two, time_bias)])
     full = moved(lowered, lambda b: b ^ 1, 0)
     load = moved(load, lambda b: b + 2 if b % 2 else b - 2, 0)
     beyond = load[: rows * stride].reshape(latent.shape)
@@ -314,36 +362,33 @@
     frame = pltpu.VMEM((height + 2, columns, channels), BF16)
     acc = pltpu.VMEM((height * columns, 3 * outs), F32)
     result = pltpu.VMEM((height, columns, outs), F32)
-    weights = (3, 3, outs, channels)
-    own, w_next = pl.pallas_call(
+    own = pl.pallas_call(
         functools.partial(first_kernel, size),
-        out_shape=(
-            packed(height, columns, outs),
-            jax.ShapeDtypeStruct(weights, BF16),
-        ),
-        in_specs=[VMEM] * 6 + [HBM] * 4,
-        out_specs=(VMEM, VMEM),
-        scratch_shapes=[
-            frame,
-            acc,
-            result,
-            pltpu.VMEM((channels,), F32),
-            pltpu.VMEM((channels,), F32),
-            pltpu.VMEM((channels,), F32),
-            pltpu.SemaphoreType.DMA((4,)),
-        ],
-        compiler_params=PARAMS,
-    )(mix, mix_other, full, full_other, edges, w_first, *[in_hbm(v) for v in (conv_two, gain_one, gain_two, time_bias)])
+        out_shape=packed(height, columns, outs),
+        in_specs=[VMEM] * 7,
+        out_specs=VMEM,
+        scratch_shapes=[frame, acc, result],
+        compiler_params=PARAMS,
+    )(mix, mix_other, full, full_other, edges, w_first, table)
     other = moved(own, lambda b: b, 1)
+    near = near_channels(outs)
+    near_part = pl.pallas_call(
+        near_kernel,
+        out_shape=jax.ShapeDtypeStruct((height, columns, outs), F32),
+        in_specs=[VMEM] * 3,
+        out_specs=VMEM,
+        scratch_shapes=[pltpu.VMEM((height + 2, columns, near), BF16), acc],
+        compiler_params=PARAMS,
+    )(own, w_next, edges)
     marked, plain = packed(rows, stride, outs, TAIL), packed(rows, stride, outs)
     mix_same, mix_cross, full_same, full_cross = pl.pallas_call(
         second_kernel,
         out_shape=(marked, plain, marked, plain),
-        in_specs=[SMEM] + [VMEM] * 6,
+        in_specs=[SMEM] + [VMEM] * 7,
         out_specs=(VMEM,) * 4,
-        scratch_shapes=[frame, acc, result],
-        compiler_params=PARAMS,
-    )(offset, own, other, w_next, edges, counted, load)
+        scratch_shapes=[pltpu.VMEM((height + 2, columns, channels - near), BF16), acc, result],
+        compiler_params=PARAMS,
+    )(offset, own, other, w_next, edges, near_part, counted, load)
 
     def aside(b):
         return b - 2 if b % 2 else b + 2

time: 35.5 us -> 33.5 us (0.944)
  starting transfers between devices: 14.1 us -> 12.2 us
  waiting for transfers between devices: 7.86 us -> 7.05 us
  Pallas kernels: 12.4 us -> 13.1 us
    pallas_call x2 -> x3, Pallas kernels: 6.69 us -> 8.74 us  [the longest x1 3.95 us: per_device(): pl.pallas_call(functools.partial(first_kernel, size), out_shape=packed(he...]
    ppermute x10, starting transfers between devices: 14.1 us -> 12.2 us  [moved(): return lax.ppermute(value, ('blk', 'rows'), pairs)]
    pallas_call x1, Pallas kernels: 3.41 us -> 2.12 us  [per_device(): pl.pallas_call(second_kernel, out_shape=(marked, plain, marked, plain), i...]
    ppermute x10, waiting for transfers between devices: 7.86 us -> 7.05 us  [moved(): return lax.ppermute(value, ('blk', 'rows'), pairs)]
  transfers between devices with their start and end apart: 10 -> 10, of which waited for: 5 -> 5; matrix products, arithmetic and copies ran while one was open for 1% -> 1% of each run, Pallas kernels for 6% -> 14%
where the time goes in v4:
time: 33.5 us; the launch traced here: 33.3 us
  Pallas kernels  13.1 us (39%)
  starting transfers between devices  12.2 us (36%)
  waiting for transfers between devices  7.05 us (21%)
  between operations  0.75 us (2%)
    ppermute x10, starting transfers between devices, moved(): return lax.ppermute(value, ('blk', 'rows'), pairs)  12.2 us
    ppermute x10, waiting for transfers between devices, moved(): return lax.ppermute(value, ('blk', 'rows'), pairs)  7.05 us
    pallas_call x1, Pallas kernels, per_device(): pl.pallas_call(functools.partial(first_kernel, size), out_shape=packed(he...  3.95 us
    pallas_call x1, Pallas kernels, per_device(): pl.pallas_call(ready_kernel, out_shape=(weights, weights, jax.ShapeDtypeS...  3.42 us
    pallas_call x1, Pallas kernels, per_device(): pl.pallas_call(second_kernel, out_shape=(marked, plain, marked, plain), i...  2.12 us
    pallas_call x1, Pallas kernels, per_device(): pl.pallas_call(near_kernel, out_shape=jax.ShapeDtypeStruct((height, colum...  1.37 us
    pallas_call x1, Pallas kernels, per_device(): pl.pallas_call(last_kernel, out_shape=jax.ShapeDtypeStruct(latent.shape,...  1.2 us
    pallas_call x1, Pallas kernels, per_device(): pl.pallas_call(lower_kernel, out_shape=(jax.ShapeDtypeStruct(latent.shape...  1.06 us
  transfers between devices with their start and end apart: 10, of which 5 were waited for; matrix products, arithmetic and copies ran while one was open for 1% of the time, Pallas kernels for 14%

profile of v4, /device:TPU:1, one launch (start us, length us, event | category | flops | bytes accessed | tf_op | source)
XLA Modules:
  0.0 33.3 jit_solution(9327351414807361953)
XLA Ops:
  0.0 1.1 %shard_map.82 = (bf16[4,32,640]{2,1,0:T(8,128)(2,1)S(1)}, bf16[136,640]{1,0:T(8,128)(2,1)S(1)}, f32[4,32,640]{2,1,0:T(8,128)S(1)}, s32[1,64]{1,0:T(1,128)S(1)}) custom-call(f32[4,32,640]{2,1,0:T(8,128)} %latent.1, s32[1,64]{1,0:T(1,128)} %counts.1), custom_call_target="tpu_custom_call" | custom-call | tf_op jit(solution)/shard_map/pallas_call | solution.py:326
  1.1 2.1 %collective-permute-start.2 = (bf16[4,32,640]{2,1,0:T(8,128)(2,1)S(1)}, bf16[4,32,640]{2,1,0:T(8,128)(2,1)S(1)}, u32[]{:S(2)}, u32[]{:S(2)}) collective-permute-start(bf16[4,32,640]{2,1,0:T(8,128)(2,1)S(1)} %get-tuple-element.17.lowered), channel_id=1, source_target_pairs={{0,2},{1,3},{2,0},{3,1},{4,6},{5,7},{6,4},{7,5},{8,10},{9,11},{10,... | collective-permute-start | bytes 491528 | tf_op jit(solution)/shard_map/ppermute | solution.py:27
  3.2 3.3 %collective-permute-start = (bf16[136,640]{1,0:T(8,128)(2,1)S(1)}, bf16[136,640]{1,0:T(8,128)(2,1)S(1)}, u32[]{:S(2)}, u32[]{:S(2)}) collective-permute-start(bf16[136,640]{1,0:T(8,128)(2,1)S(1)} %get-tuple-element.19), channel_id=1, source_target_pairs={{0,12},{1,13},{2,6},{3,7},{4,0},{5,1},{6,10},{7,11},{8,4},{9,5},{1... | collective-permute-start | bytes 522248 | tf_op jit(solution)/shard_map/ppermute | solution.py:27
  7.2 3.4 %shard_map.83 = (bf16[3,960,640]{2,1,0:T(8,128)(2,1)S(1)}, bf16[3,960,640]{2,1,0:T(8,128)(2,1)S(1)}, f32[8,640]{1,0:T(8,128)S(1)}) custom-call(bf16[3,3,320,640]{3,2,1,0:T(8,128)(2,1)} %bitcast.8, bf16[3,3,320,640]{3,2,1,0:T(8,128)(2,1)} %bitcast.9, f32[640]{0:T(1024)} %gain_one.1, f32[640]{0:T(1024)} %gain_two.1, f32[640]{0:T(1024)} %time_bias.1), custom_call_target="tpu_custom_call" | custom-call | tf_op jit(solution)/shard_map/pallas_call | solution.py:341
  10.6 0.0 collective-permute-done.2.full
  10.6 1.3 %collective-permute-start.3 = (bf16[4,32,640]{2,1,0:T(8,128)(2,1)S(1)}, bf16[4,32,640]{2,1,0:T(8,128)(2,1)S(1)}, u32[]{:S(2)}, u32[]{:S(2)}) collective-permute-start(bf16[4,32,640]{2,1,0:T(8,128)(2,1)S(1)} %collective-permute-done.2.full), channel_id=1, source_target_pairs={{0,1},{1,0},{2,3},{3,2},{4,5},{5,4},{6,7},{7,6},{8,9},{9,8},{10,11... | collective-permute-start | bytes 491528 | tf_op jit(solution)/shard_map/ppermute | solution.py:27
  11.9 0.0 collective-permute-done.load
  12.0 0.1 broadcast_select_fusion.mix
  12.0 0.1 collective-permute-start.1
  12.1 0.1 select_select_fusion.edges
  12.2 0.7 %collective-permute-done.3.full_other = bf16[4,32,640]{2,1,0:T(8,128)(2,1)S(1)} collective-permute-done((bf16[4,32,640]{2,1,0:T(8,128)(2,1)S(1)}, bf16[4,32,640]{2,1,0:T(8,128)(2,1)S(1)}, u32[]{:S(2)}, u32[]{:S(2)}) %collective-permute-start.3) | collective-permute-done | bytes 163872 | tf_op jit(solution)/shard_map/ppermute | solution.py:27
  13.0 0.6 %collective-permute-done.1.mix_other = bf16[4,32,640]{2,1,0:T(8,128)(2,1)S(1)} collective-permute-done((bf16[4,32,640]{2,1,0:T(8,128)(2,1)S(1)}, bf16[4,32,640]{2,1,0:T(8,128)(2,1)S(1)}, u32[]{:S(2)}, u32[]{:S(2)}) %collective-permute-start.1) | collective-permute-done | bytes 163872 | tf_op jit(solution)/shard_map/ppermute | solution.py:27
  13.5 4.0 %shard_map.84.own = bf16[256,640]{1,0:T(8,128)(2,1)S(1)} custom-call(bf16[4,32,640]{2,1,0:T(8,128)(2,1)S(1)} %broadcast_select_fusion.mix, bf16[4,32,640]{2,1,0:T(8,128)(2,1)S(1)} %collective-permute-done.1.mix_other, bf16[4,32,640]{2,1,0:T(8,128)(2,1)S(1)} %collective-permute-done.2.full, bf16[4,32,640]{2,1,0:T(8,128)(2,1)S(1)} %collective-permute-done.3.full_other, ...), custom_call_target="tpu_custom_call" | custom-call | tf_op jit(solution)/shard_map/pallas_call | solution.py:365
  17.5 0.2 collective-permute-start.4
  17.7 1.4 %shard_map.85.near_part = f32[8,64,320]{2,1,0:T(8,128)S(1)} custom-call(bf16[256,640]{1,0:T(8,128)(2,1)S(1)} %shard_map.84.own, bf16[3,960,640]{2,1,0:T(8,128)(2,1)S(1)} %get-tuple-element.22.w, f32[3,64,128]{2,1,0:T(8,128)S(1)} %select_select_fusion.edges), custom_call_target="tpu_custom_call" | custom-call | tf_op jit(solution)/shard_map/pallas_call | solution.py:375
  19.0 0.1 collective-permute-done.4.other
  19.2 2.1 %shard_map.86 = (bf16[72,640]{1,0:T(8,128)(2,1)S(1)}, bf16[64,640]{1,0:T(8,128)(2,1)S(1)}, bf16[72,640]{1,0:T(8,128)(2,1)S(1)}, bf16[64,640]{1,0:T(8,128)(2,1)S(1)}) custom-call(s32[1]{0:T(128)} %copy.9.anchor_ref, bf16[256,640]{1,0:T(8,128)(2,1)S(1)} %shard_map.84.own, bf16[256,640]{1,0:T(8,128)(2,1)S(1)} %collective-permute-done.4.other, ...), custom_call_target="tpu_custom_call" | custom-call | tf_op jit(solution)/shard_map/pallas_call | solution.py:384
  21.3 0.1 collective-permute-start.8
  21.4 0.1 collective-permute-start.6
  21.4 5.0 %collective-permute-start.9 = (bf16[64,640]{1,0:T(8,128)(2,1)S(1)}, bf16[64,640]{1,0:T(8,128)(2,1)S(1)}, u32[]{:S(2)}, u32[]{:S(2)}) collective-permute-start(bf16[64,640]{1,0:T(8,128)(2,1)S(1)} %get-tuple-element.26), channel_id=1, source_target_pairs={{0,3},{1,2},{2,1},{3,0},{4,7},{5,6},{6,5},{7,4},{8,11},{9,10},{10,... | collective-permute-start | bytes 245768 | tf_op jit(solution)/shard_map/ppermute | solution.py:27
  26.5 0.0 collective-permute-start.7
  26.5 0.0 collective-permute-start.5
  26.5 2.2 %collective-permute-done.9.full_cross = bf16[64,640]{1,0:T(8,128)(2,1)S(1)} collective-permute-done((bf16[64,640]{1,0:T(8,128)(2,1)S(1)}, bf16[64,640]{1,0:T(8,128)(2,1)S(1)}, u32[]{:S(2)}, u32[]{:S(2)}) %collective-permute-start.9) | collective-permute-done | bytes 81952 | tf_op jit(solution)/shard_map/ppermute | solution.py:27
  28.7 3.4 %collective-permute-done.7.mix_cross = bf16[64,640]{1,0:T(8,128)(2,1)S(1)} collective-permute-done((bf16[64,640]{1,0:T(8,128)(2,1)S(1)}, bf16[64,640]{1,0:T(8,128)(2,1)S(1)}, u32[]{:S(2)}, u32[]{:S(2)}) %collective-permute-start.7) | collective-permute-done | bytes 81952 | tf_op jit(solution)/shard_map/ppermute | solution.py:27
  32.1 0.0 collective-permute-done.5.mix_core
  32.1 0.0 collective-permute-done.8.full_same
  32.1 0.0 collective-permute-done.6.mix_same
  32.1 1.2 %shard_map.87 = f32[4,32,640]{2,1,0:T(8,128)} custom-call(s32[1]{0:T(128)} %copy.9.anchor_ref, f32[4,32,640]{2,1,0:T(8,128)S(1)} %get-tuple-element.16.latent, bf16[4,32,640]{2,1,0:T(8,128)(2,1)S(1)} %get-tuple-element.17.lowered, s32[1,64]{1,0:T(1,128)S(1)} %get-tuple-element.18.counts, bf16[136,640]{1,0:T(8,128)(2,1)S(1)} %collective-permute-done.load, ...), custom_call_target="tpu_custom_call" | custom-call | tf_op jit(solution)/shard_map/pallas_call | solution.py:401
  (5 shorter events, 0.0 us)
Async XLA Ops:
  1.1 9.6 %collective-permute-start.2 = (bf16[4,32,640]{2,1,0:T(8,128)(2,1)S(1)}, bf16[4,32,640]{2,1,0:T(8,128)(2,1)S(1)}, u32[]{:S(2)}, u32[]{:S(2)}) collective-permute-start(bf16[4,32,640]{2,1,0:T(8,128)(2,1)S(1)} %get-tuple-element.17.lowered), channel_id=1, source_target_pairs={{0,2},{1,3},{2,0},{3,1},{4,6},{5,7},{6,4},{7,5},{8,10},{9,11},{10,... | collective-permute-start | bytes 491528 | tf_op jit(solution)/shard_map/ppermute | solution.py:27
  3.2 8.8 %collective-permute-start = (bf16[136,640]{1,0:T(8,128)(2,1)S(1)}, bf16[136,640]{1,0:T(8,128)(2,1)S(1)}, u32[]{:S(2)}, u32[]{:S(2)}) collective-permute-start(bf16[136,640]{1,0:T(8,128)(2,1)S(1)} %get-tuple-element.19), channel_id=1, source_target_pairs={{0,12},{1,13},{2,6},{3,7},{4,0},{5,1},{6,10},{7,11},{8,4},{9,5},{1... | collective-permute-start | bytes 522248 | tf_op jit(solution)/shard_map/ppermute | solution.py:27
  10.6 2.3 %collective-permute-start.3 = (bf16[4,32,640]{2,1,0:T(8,128)(2,1)S(1)}, bf16[4,32,640]{2,1,0:T(8,128)(2,1)S(1)}, u32[]{:S(2)}, u32[]{:S(2)}) collective-permute-start(bf16[4,32,640]{2,1,0:T(8,128)(2,1)S(1)} %collective-permute-done.2.full), channel_id=1, source_target_pairs={{0,1},{1,0},{2,3},{3,2},{4,5},{5,4},{6,7},{7,6},{8,9},{9,8},{10,11... | collective-permute-start | bytes 491528 | tf_op jit(solution)/shard_map/ppermute | solution.py:27
  12.0 1.5 %collective-permute-start.1 = (bf16[4,32,640]{2,1,0:T(8,128)(2,1)S(1)}, bf16[4,32,640]{2,1,0:T(8,128)(2,1)S(1)}, u32[]{:S(2)}, u32[]{:S(2)}) collective-permute-start(bf16[4,32,640]{2,1,0:T(8,128)(2,1)S(1)} %broadcast_select_fusion.mix), channel_id=1, source_target_pairs={{0,1},{1,0},{2,3},{3,2},{4,5},{5,4},{6,7},{7,6},{8,9},{9,8},{10,11... | collective-permute-start | bytes 491528 | tf_op jit(solution)/shard_map/ppermute | solution.py:27
  17.5 1.7 %collective-permute-start.4 = (bf16[256,640]{1,0:T(8,128)(2,1)S(1)}, bf16[256,640]{1,0:T(8,128)(2,1)S(1)}, u32[]{:S(2)}, u32[]{:S(2)}) collective-permute-start(bf16[256,640]{1,0:T(8,128)(2,1)S(1)} %shard_map.84.own), channel_id=1, source_target_pairs={{0,1},{1,0},{2,3},{3,2},{4,5},{5,4},{6,7},{7,6},{8,9},{9,8},{10,11... | collective-permute-start | bytes 983048 | tf_op jit(solution)/shard_map/ppermute | solution.py:27
  21.3 10.8 %collective-permute-start.8 = (bf16[72,640]{1,0:T(8,128)(2,1)S(1)}, bf16[72,640]{1,0:T(8,128)(2,1)S(1)}, u32[]{:S(2)}, u32[]{:S(2)}) collective-permute-start(bf16[72,640]{1,0:T(8,128)(2,1)S(1)} %get-tuple-element.25), channel_id=1, source_target_pairs={{0,2},{1,3},{2,0},{3,1},{4,6},{5,7},{6,4},{7,5},{8,10},{9,11},{10,... | collective-permute-start | bytes 276488 | tf_op jit(solution)/shard_map/ppermute | solution.py:27
  21.4 10.8 %collective-permute-start.6 = (bf16[72,640]{1,0:T(8,128)(2,1)S(1)}, bf16[72,640]{1,0:T(8,128)(2,1)S(1)}, u32[]{:S(2)}, u32[]{:S(2)}) collective-permute-start(bf16[72,640]{1,0:T(8,128)(2,1)S(1)} %get-tuple-element.23.mix_own), channel_id=1, source_target_pairs={{0,4},{1,5},{2,14},{3,15},{4,8},{5,9},{6,2},{7,3},{8,12},{9,13},{1... | collective-permute-start | bytes 276488 | tf_op jit(solution)/shard_map/ppermute | solution.py:27
  21.4 7.3 %collective-permute-start.9 = (bf16[64,640]{1,0:T(8,128)(2,1)S(1)}, bf16[64,640]{1,0:T(8,128)(2,1)S(1)}, u32[]{:S(2)}, u32[]{:S(2)}) collective-permute-start(bf16[64,640]{1,0:T(8,128)(2,1)S(1)} %get-tuple-element.26), channel_id=1, source_target_pairs={{0,3},{1,2},{2,1},{3,0},{4,7},{5,6},{6,5},{7,4},{8,11},{9,10},{10,... | collective-permute-start | bytes 245768 | tf_op jit(solution)/shard_map/ppermute | solution.py:27
  26.5 5.7 %collective-permute-start.7 = (bf16[64,640]{1,0:T(8,128)(2,1)S(1)}, bf16[64,640]{1,0:T(8,128)(2,1)S(1)}, u32[]{:S(2)}, u32[]{:S(2)}) collective-permute-start(bf16[64,640]{1,0:T(8,128)(2,1)S(1)} %get-tuple-element.24), channel_id=1, source_target_pairs={{0,5},{1,4},{2,15},{3,14},{4,9},{5,8},{6,3},{7,2},{8,13},{9,12},{1... | collective-permute-start | bytes 245768 | tf_op jit(solution)/shard_map/ppermute | solution.py:27
  26.5 5.7 %collective-permute-start.5 = (bf16[64,640]{1,0:T(8,128)(2,1)S(1)}, bf16[64,640]{1,0:T(8,128)(2,1)S(1)}, u32[]{:S(2)}, u32[]{:S(2)}) collective-permute-start(bf16[64,640]{1,0:T(8,128)(2,1)S(1)} %get-tuple-element.24), channel_id=1, source_target_pairs={{0,1},{1,0},{2,3},{3,2},{4,5},{5,4},{6,7},{7,6},{8,9},{9,8},{10,11... | collective-permute-start | bytes 245768 | tf_op jit(solution)/shard_map/ppermute | solution.py:27

commit v5 on v4

--- a/solution.py
+++ b/solution.py
@@ -41,26 +41,26 @@
     return out[0:1] + out[1:2] + out[2:3], out[3:4] + out[4:5] + out[5:6]
 
 
-def group_scale(summed, squares, count, size):
-    channels, lanes = summed.shape[1], 128
-    ch = lax.broadcasted_iota(jnp.int32, (channels, lanes), 0)
-    low = lax.broadcasted_iota(jnp.int32, (channels, lanes), 1) * size
-    gather = jnp.where((ch >= low) & (ch < low + size), 1.0, 0.0).astype(BF16)
-    ch = lax.broadcasted_iota(jnp.int32, (lanes, channels), 1)
-    low = lax.broadcasted_iota(jnp.int32, (lanes, channels), 0) * size
-    spread = jnp.where((ch >= low) & (ch < low + size), 1.0, 0.0).astype(BF16)
-    total, total_sq = regroup(summed, squares, gather)
+def group_tables(size, gather, spread):
+    for ref, (ch_axis, group_axis) in ((gather, (0, 1)), (spread, (1, 0))):
+        ch = lax.broadcasted_iota(jnp.int32, ref.shape, ch_axis)
+        low = lax.broadcasted_iota(jnp.int32, ref.shape, group_axis) * size
+        ref[...] = jnp.where((ch >= low) & (ch < low + size), 1.0, 0.0).astype(BF16)
+
+
+def group_scale(summed, squares, count, gather, spread):
+    channels = summed.shape[1]
+    total, total_sq = regroup(summed, squares, gather[:channels])
     mean = total / count
     scale = lax.rsqrt(total_sq / count - mean * mean + 1e-05)
-    return regroup(mean, scale, spread)
-
-
-def silu(u):
-    half = 0.5 * u
+    return regroup(mean, scale, spread[:, :channels])
+
+
+def silu_of_twice(half):
     return half + half * jnp.tanh(half)
 
 
-def arranged(weight, target, sem):
+def arranged(core, weight, target, sem):
     outs = weight.shape[2]
     whole = outs // 128 * 128
     copies, start = [], 0
@@ -69,19 +69,29 @@
             size = part.stop - part.start
             for a in range(3):
                 spot = target.at[a, start : start + size]
-                copies.append(pltpu.make_async_copy(weight.at[a, b, part], spot, sem.at[len(copies)]))
+                tap = a + core * (2 - 2 * a)
+                copies.append(pltpu.make_async_copy(weight.at[tap, b, part], spot, sem.at[len(copies)]))
             start += size
     return copies
 
 
-def nine_taps(frame, weight, acc, first=None):
+def nine_taps(frame, weight, acc, channel=None):
     height, columns, channels = frame.shape[0] - 2, frame.shape[1], frame.shape[2]
     patch = jnp.concatenate(
         [frame[a : a + height].reshape(height * columns, channels) for a in range(3)], axis=1
     )
-    some = slice(None) if first is None else pl.ds(pl.multiple_of(first, 128), channels)
+    some = slice(None) if channel is None else pl.ds(pl.multiple_of(channel, 128), channels)
     taps = jnp.concatenate([weight[a, :, some] for a in range(3)], axis=1)
     acc[...] = lax.dot_general(patch, taps, (((1,), (1,)), ((), ())), preferred_element_type=F32)
+
+
+def clear_edges(frame):
+    for edge in (0, frame.shape[0] - 1):
+        frame[edge] = jnp.zeros(frame.shape[1:], BF16)
+
+
+def local_row(core, i, rows):
+    return i + core * (rows - 1 - 2 * i)
 
 
 def joined_taps(acc, row, columns, outs, edges):
@@ -134,14 +144,16 @@
     put_counts(load, rows * cols, counted[...].astype(F32))
 
 
-def ready_kernel(w_one, w_two, gain_one, gain_two, time_bias, w, w_next, table, one_in, two_in, bias_in, small_sems, sems):
+def ready_kernel(size, w_one, w_two, gain_one, gain_two, time_bias, w, w_next, table, gather, spread, one_in, two_in, bias_in, small_sems, sems):
     small = [
         pltpu.make_async_copy(source, target, small_sems.at[i])
         for i, (source, target) in enumerate(((gain_one, one_in), (gain_two, two_in), (time_bias, bias_in)))
     ]
-    copies = arranged(w_one, w, sems.at[0]) + arranged(w_two, w_next, sems.at[1])
+    core = lax.axis_index("rows")
+    copies = arranged(core, w_one, w, sems.at[0]) + arranged(core, w_two, w_next, sems.at[1])
     for copy in small + copies:
         copy.start()
+    group_tables(size, gather, spread)
     table[...] = jnp.zeros_like(table)
     for i, ref in enumerate((one_in, two_in, bias_in)):
         small[i].wait()
@@ -168,26 +180,29 @@
     return jnp.sum(jnp.where(picked, values, 0.0), axis=1, keepdims=True)
 
 
-def first_kernel(size, mix, mix_other, full, full_other, edges, w, table, out, frame, acc, hidden):
+def first_kernel(size, mix, mix_other, full, full_other, edges, w, table, gather, spread, out, frame, acc, hidden):
     core = lax.axis_index("rows")
     rows, half_cols, channels = mix.shape
     columns, height, outs = 2 * half_cols, 2 * rows, out.shape[1] // 2
     count = height * columns * size
+    clear_edges(frame)
     summed = jnp.zeros((1, channels), F32)
     squares = jnp.zeros((1, channels), F32)
     for ref in (mix, mix_other, full, full_other):
         v = ref[...].astype(F32).reshape(rows * half_cols, channels)
         summed += jnp.sum(v, axis=0, keepdims=True)
         squares += jnp.sum(v * v, axis=0, keepdims=True)
-    mean, scale = group_scale(summed, squares, count, size)
-    scale = scale * table[0:1]
-    frame[0] = jnp.zeros(frame.shape[1:], BF16)
-    frame[height + 1] = jnp.zeros(frame.shape[1:], BF16)
-    for ref, mine, col in ((mix, 0, 0), (full, 0, half_cols), (mix_other, 1, 0), (full_other, 1, half_cols)):
-        start = 1 + rows * (core ^ mine)
-        for row in range(rows):
-            v = ref[row].astype(F32)
-            frame[start + row, col : col + half_cols] = silu((v - mean) * scale).astype(BF16)
+    mean, scale = group_scale(summed, squares, count, gather, spread)
+    scale = scale * (0.5 * table[0:1])
+
+    def normed(row):
+        local = local_row(core, row % rows, rows)
+        for ref, col in ((mix, 0), (full, half_cols)) if row < rows else ((mix_other, 0), (full_other, half_cols)):
+            v = ref[local].astype(F32)
+            frame[1 + row, col : col + half_cols] = silu_of_twice((v - mean) * scale).astype(BF16)
+
+    for row in range(height):
+        normed(row)
     nine_taps(frame, w, acc)
     bias = half_of(table[2:3], outs, core)
     summed = jnp.zeros((1, outs), F32)
@@ -197,10 +212,10 @@
         hidden[row] = v
         summed += jnp.sum(v, axis=0, keepdims=True)
         squares += jnp.sum(v * v, axis=0, keepdims=True)
-    mean, scale = group_scale(summed, squares, count, size)
-    scale = scale * half_of(table[1:2], outs, core)
-    for row in range(height):
-        put(out, row, height, silu((hidden[row] - mean) * scale).astype(BF16))
+    mean, scale = group_scale(summed, squares, count, gather, spread)
+    scale = scale * (0.5 * half_of(table[1:2], outs, core))
+    for row in range(height):
+        put(out, row, height, silu_of_twice((hidden[row] - mean) * scale).astype(BF16))
 
 
 def near_channels(outs):
@@ -211,60 +226,40 @@
     core = lax.axis_index("rows")
     height, columns, near = frame.shape[0] - 2, frame.shape[1], frame.shape[2]
     outs = own.shape[1] // 2
-    for edge in (0, height + 1):
-        frame[edge] = jnp.zeros(frame.shape[1:], BF16)
-
-    @pl.when(core == 0)
-    def _():
-        for row in range(height):
-            frame[1 + row] = get(own, row, height, columns)[:, :near]
-
-    @pl.when(core == 1)
-    def _():
-        for row in range(height):
-            frame[1 + row] = get(own, row, height, columns)[:, outs - near :]
-
+    clear_edges(frame)
+    for row in range(height):
+        mine = get(own, row, height, columns)
+        frame[1 + row] = jnp.where(core == 0, mine[:, :near], mine[:, outs - near :])
     nine_taps(frame, w, acc, core * (2 * outs - near))
     for row in range(height):
         part[row] = joined_taps(acc, row, columns, outs, edges)
 
 
-def second_kernel(anchor_ref, own, other, w, edges, near_part, counts, load, mix_same, mix_cross, full_same, full_cross, frame, acc, result):
+def second_kernel(anchor_ref, own, other, w, edges, near_part, counts, load, mix_same, mix_cross, full_same, full_cross, frame, acc):
     core = lax.axis_index("rows")
     odd = (lax.axis_index("blk") & 1) == 1
     height, columns = frame.shape[0] - 2, frame.shape[1]
     outs = own.shape[1] // 2
     near = near_channels(outs)
     rows, half_cols = height // 2, columns // 2
-    for edge in (0, height + 1):
-        frame[edge] = jnp.zeros(frame.shape[1:], BF16)
-
-    @pl.when(core == 0)
-    def _():
-        for row in range(height):
-            mine, theirs = (get(ref, row, height, columns) for ref in (own, other))
-            frame[1 + row] = jnp.concatenate([mine[:, near:], theirs], axis=1)
-
-    @pl.when(core == 1)
-    def _():
-        for row in range(height):
-            mine, theirs = (get(ref, row, height, columns) for ref in (own, other))
-            frame[1 + row] = jnp.concatenate([theirs, mine[:, : outs - near]], axis=1)
-
+    clear_edges(frame)
+    for row in range(height):
+        mine = get(own, row, height, columns)
+        theirs = get(other, height - 1 - row, height, columns)
+        frame[1 + row] = jnp.where(
+            core == 0,
+            jnp.concatenate([mine[:, near:], theirs], axis=1),
+            jnp.concatenate([theirs, mine[:, : outs - near]], axis=1),
+        )
     nine_taps(frame, w, acc, (1 - core) * near)
     own_row = jnp.where(odd, get_counts(load, rows * half_cols, columns), counts[...].astype(F32))
     part = jnp.broadcast_to(by_column(own_row, anchor_ref[0], columns), (columns, outs))
     for row in range(height):
-        result[row] = (joined_taps(acc, row, columns, outs, edges) + near_part[row]) * part
-    for out, flip, col in (
-        (mix_same, 0, 0),
-        (mix_cross, 1, 0),
-        (full_same, 0, half_cols),
-        (full_cross, 1, half_cols),
-    ):
-        start = rows * (core ^ flip)
-        for row in range(rows):
-            put(out, row, rows, result[start + row, col : col + half_cols].astype(BF16))
+        value = ((joined_taps(acc, row, columns, outs, edges) + near_part[row]) * part).astype(BF16)
+        mix, full = (mix_same, full_same) if row < rows else (mix_cross, full_cross)
+        spot = row if row < rows else height - 1 - row
+        put(mix, spot, rows, value[:half_cols])
+        put(full, spot, rows, value[half_cols:])
     for out in (mix_same, full_same):
         put_counts(out, rows * half_cols // 2, own_row)
 
@@ -286,25 +281,21 @@
     join_scale = math.sqrt(0.3) - math.sqrt(0.7 / 0.5) * math.sqrt(0.5)
     part = join_scale / weight
 
-    copies = [pltpu.make_async_copy(done.at[row], out.at[row], sems.at[row]) for row in range(rows)]
-
     def summed(row, own, far, full):
         own, far, full = (get(ref, row, rows, cols).astype(F32) for ref in (own, far, full))
         return jnp.where(keep, own, far) + full
 
+    copies = []
     for row in range(rows):
+        local = local_row(core, row, rows)
         same = summed(row, mix_own, mix_same, full_same)
         cross = summed(row, mix_core, mix_cross, full_cross)
-        base = own_scale * latent[row] + join_scale * lowered[row].astype(F32)
-
-        @pl.when(core == 0)
-        def _():
-            done[row] = base + part * jnp.concatenate([same, cross], axis=1)
-
-        @pl.when(core == 1)
-        def _():
-            done[row] = base + part * jnp.concatenate([cross, same], axis=1)
-
+        base = own_scale * latent[local] + join_scale * lowered[local].astype(F32)
+        both = jnp.where(
+            core == 0, jnp.concatenate([same, cross], axis=1), jnp.concatenate([cross, same], axis=1)
+        )
+        done[row] = base + part * both
+        copies.append(pltpu.make_async_copy(done.at[row], out.at[local], sems.at[row]))
         copies[row].start()
     for copy in copies:
         copy.wait()
@@ -338,11 +329,17 @@
     )(in_hbm(latent), in_hbm(counts))
     weights = jax.ShapeDtypeStruct((3, 3 * outs, channels), BF16)
     vector = pltpu.VMEM((channels,), F32)
-    w_first, w_next, table = pl.pallas_call(
-        ready_kernel,
-        out_shape=(weights, weights, jax.ShapeDtypeStruct((8, channels), F32)),
+    w_first, w_next, table, gather, spread = pl.pallas_call(
+        functools.partial(ready_kernel, size),
+        out_shape=(
+            weights,
+            weights,
+            jax.ShapeDtypeStruct((8, channels), F32),
+            jax.ShapeDtypeStruct((channels, 128), BF16),
+            jax.ShapeDtypeStruct((128, channels), BF16),
+        ),
         in_specs=[HBM] * 5,
-        out_specs=(VMEM,) * 3,
+        out_specs=(VMEM,) * 5,
         scratch_shapes=[vector] * 3 + [pltpu.SemaphoreType.DMA((3,)), pltpu.SemaphoreType.DMA((2, 18))],
         compiler_params=PARAMS,
     )(*[in_hbm(v) for v in (conv_one, conv_two, gain_one, gain_two, time_bias)])
@@ -365,11 +362,11 @@
     own = pl.pallas_call(
         functools.partial(first_kernel, size),
         out_shape=packed(height, columns, outs),
-        in_specs=[VMEM] * 7,
+        in_specs=[VMEM] * 9,
         out_specs=VMEM,
         scratch_shapes=[frame, acc, result],
         compiler_params=PARAMS,
-    )(mix, mix_other, full, full_other, edges, w_first, table)
+    )(mix, mix_other, full, full_other, edges, w_first, table, gather, spread)
     other = moved(own, lambda b: b, 1)
     near = near_channels(outs)
     near_part = pl.pallas_call(
@@ -386,7 +383,7 @@
         out_shape=(marked, plain, marked, plain),
         in_specs=[SMEM] + [VMEM] * 7,
         out_specs=(VMEM,) * 4,
-        scratch_shapes=[pltpu.VMEM((height + 2, columns, channels - near), BF16), acc, result],
+        scratch_shapes=[pltpu.VMEM((height + 2, columns, channels - near), BF16), acc],
         compiler_params=PARAMS,
     )(offset, own, other, w_next, edges, near_part, counted, load)
 

time: 33.5 us -> 32.6 us (0.973)
  Pallas kernels: 13.1 us -> 12.2 us
    pallas_call x1, Pallas kernels: 3.95 us -> 3.5 us  [per_device(): pl.pallas_call(functools.partial(first_kernel, size), out_shape=packed(he...]
  transfers between devices with their start and end apart: 10 -> 10, of which waited for: 5 -> 5; matrix products, arithmetic and copies ran while one was open for 1% -> 1% of each run, Pallas kernels for 14% -> 15%
where the time goes in v5:
time: 32.6 us; the launch traced here: 32.4 us
  Pallas kernels  12.2 us (37%)
  starting transfers between devices  12.1 us (37%)
  waiting for transfers between devices  7.09 us (22%)
  between operations  0.76 us (2%)
    ppermute x10, starting transfers between devices, moved(): return lax.ppermute(value, ('blk', 'rows'), pairs)  12.1 us
    ppermute x10, waiting for transfers between devices, moved(): return lax.ppermute(value, ('blk', 'rows'), pairs)  7.09 us
    pallas_call x1, Pallas kernels, per_device(): pl.pallas_call(functools.partial(first_kernel, size), out_shape=packed(he...  3.5 us
    pallas_call x1, Pallas kernels, per_device(): pl.pallas_call(functools.partial(ready_kernel, size), out_shape=(weights,...  3.43 us
    pallas_call x1, Pallas kernels, per_device(): pl.pallas_call(second_kernel, out_shape=(marked, plain, marked, plain), i...  1.94 us
    pallas_call x1, Pallas kernels, per_device(): pl.pallas_call(near_kernel, out_shape=jax.ShapeDtypeStruct((height, colum...  1.33 us
    pallas_call x1, Pallas kernels, per_device(): pl.pallas_call(lower_kernel, out_shape=(jax.ShapeDtypeStruct(latent.shape...  1.06 us
    pallas_call x1, Pallas kernels, per_device(): pl.pallas_call(last_kernel, out_shape=jax.ShapeDtypeStruct(latent.shape,...  0.91 us
  transfers between devices with their start and end apart: 10, of which 5 were waited for; matrix products, arithmetic and copies ran while one was open for 1% of the time, Pallas kernels for 15%

profile of v5, /device:TPU:1, one launch (start us, length us, event | category | flops | bytes accessed | tf_op | source)
XLA Modules:
  0.0 32.4 jit_solution(16231277495016020599)
XLA Ops:
  0.0 1.1 %shard_map.82 = (bf16[4,32,640]{2,1,0:T(8,128)(2,1)S(1)}, bf16[136,640]{1,0:T(8,128)(2,1)S(1)}, f32[4,32,640]{2,1,0:T(8,128)S(1)}, s32[1,64]{1,0:T(1,128)S(1)}) custom-call(f32[4,32,640]{2,1,0:T(8,128)} %latent.1, s32[1,64]{1,0:T(1,128)} %counts.1), custom_call_target="tpu_custom_call" | custom-call | tf_op jit(solution)/shard_map/pallas_call | solution.py:317
  1.1 2.1 %collective-permute-start.2 = (bf16[4,32,640]{2,1,0:T(8,128)(2,1)S(1)}, bf16[4,32,640]{2,1,0:T(8,128)(2,1)S(1)}, u32[]{:S(2)}, u32[]{:S(2)}) collective-permute-start(bf16[4,32,640]{2,1,0:T(8,128)(2,1)S(1)} %get-tuple-element.19.lowered), channel_id=1, source_target_pairs={{0,2},{1,3},{2,0},{3,1},{4,6},{5,7},{6,4},{7,5},{8,10},{9,11},{10,... | collective-permute-start | bytes 491528 | tf_op jit(solution)/shard_map/ppermute | solution.py:27
  3.2 3.3 %collective-permute-start = (bf16[136,640]{1,0:T(8,128)(2,1)S(1)}, bf16[136,640]{1,0:T(8,128)(2,1)S(1)}, u32[]{:S(2)}, u32[]{:S(2)}) collective-permute-start(bf16[136,640]{1,0:T(8,128)(2,1)S(1)} %get-tuple-element.21), channel_id=1, source_target_pairs={{0,12},{1,13},{2,6},{3,7},{4,0},{5,1},{6,10},{7,11},{8,4},{9,5},{1... | collective-permute-start | bytes 522248 | tf_op jit(solution)/shard_map/ppermute | solution.py:27
  7.2 3.4 %shard_map.83 = (bf16[3,960,640]{2,1,0:T(8,128)(2,1)S(1)}, bf16[3,960,640]{2,1,0:T(8,128)(2,1)S(1)}, f32[8,640]{1,0:T(8,128)S(1)}, bf16[640,128]{1,0:T(8,128)(2,1)S(1)}, bf16[128,640]{1,0:T(8,128)(2,1)S(1)}) custom-call(bf16[3,3,320,640]{3,2,1,0:T(8,128)(2,1)} %bitcast.8, bf16[3,3,320,640]{3,2,1,0:T(8,128)(2,1)} %bitcast.9, f32[640]{0:T(1024)} %gain_one.1, ...), custom_call_target="tpu_custom_call" | custom-call | tf_op jit(solution)/shard_map/pallas_call | solution.py:332
  10.6 0.0 collective-permute-done.2.full
  10.6 1.3 %collective-permute-start.3 = (bf16[4,32,640]{2,1,0:T(8,128)(2,1)S(1)}, bf16[4,32,640]{2,1,0:T(8,128)(2,1)S(1)}, u32[]{:S(2)}, u32[]{:S(2)}) collective-permute-start(bf16[4,32,640]{2,1,0:T(8,128)(2,1)S(1)} %collective-permute-done.2.full), channel_id=1, source_target_pairs={{0,1},{1,0},{2,3},{3,2},{4,5},{5,4},{6,7},{7,6},{8,9},{9,8},{10,11... | collective-permute-start | bytes 491528 | tf_op jit(solution)/shard_map/ppermute | solution.py:27
  11.9 0.0 collective-permute-done.load
  12.0 0.1 broadcast_select_fusion.mix
  12.1 0.1 collective-permute-start.1
  12.1 0.1 select_select_fusion.edges
  12.3 0.7 %collective-permute-done.3.full_other = bf16[4,32,640]{2,1,0:T(8,128)(2,1)S(1)} collective-permute-done((bf16[4,32,640]{2,1,0:T(8,128)(2,1)S(1)}, bf16[4,32,640]{2,1,0:T(8,128)(2,1)S(1)}, u32[]{:S(2)}, u32[]{:S(2)}) %collective-permute-start.3) | collective-permute-done | bytes 163872 | tf_op jit(solution)/shard_map/ppermute | solution.py:27
  13.0 0.6 %collective-permute-done.1.mix_other = bf16[4,32,640]{2,1,0:T(8,128)(2,1)S(1)} collective-permute-done((bf16[4,32,640]{2,1,0:T(8,128)(2,1)S(1)}, bf16[4,32,640]{2,1,0:T(8,128)(2,1)S(1)}, u32[]{:S(2)}, u32[]{:S(2)}) %collective-permute-start.1) | collective-permute-done | bytes 163872 | tf_op jit(solution)/shard_map/ppermute | solution.py:27
  13.5 3.5 %shard_map.84.own = bf16[256,640]{1,0:T(8,128)(2,1)S(1)} custom-call(bf16[4,32,640]{2,1,0:T(8,128)(2,1)S(1)} %broadcast_select_fusion.mix, bf16[4,32,640]{2,1,0:T(8,128)(2,1)S(1)} %collective-permute-done.1.mix_other, bf16[4,32,640]{2,1,0:T(8,128)(2,1)S(1)} %collective-permute-done.2.full, bf16[4,32,640]{2,1,0:T(8,128)(2,1)S(1)} %collective-permute-done.3.full_other, ...), custom_call_target="tpu_custom_call" | custom-call | tf_op jit(solution)/shard_map/pallas_call | solution.py:362
  17.0 0.2 collective-permute-start.4
  17.2 1.3 %shard_map.85.near_part = f32[8,64,320]{2,1,0:T(8,128)S(1)} custom-call(bf16[256,640]{1,0:T(8,128)(2,1)S(1)} %shard_map.84.own, bf16[3,960,640]{2,1,0:T(8,128)(2,1)S(1)} %get-tuple-element.26.w, f32[3,64,128]{2,1,0:T(8,128)S(1)} %select_select_fusion.edges), custom_call_target="tpu_custom_call" | custom-call | tf_op jit(solution)/shard_map/pallas_call | solution.py:372
  18.6 0.2 collective-permute-done.4.other
  18.7 1.9 %shard_map.86 = (bf16[72,640]{1,0:T(8,128)(2,1)S(1)}, bf16[64,640]{1,0:T(8,128)(2,1)S(1)}, bf16[72,640]{1,0:T(8,128)(2,1)S(1)}, bf16[64,640]{1,0:T(8,128)(2,1)S(1)}) custom-call(s32[1]{0:T(128)} %copy.9.anchor_ref, bf16[256,640]{1,0:T(8,128)(2,1)S(1)} %shard_map.84.own, bf16[256,640]{1,0:T(8,128)(2,1)S(1)} %collective-permute-done.4.other, ...), custom_call_target="tpu_custom_call" | custom-call | tf_op jit(solution)/shard_map/pallas_call | solution.py:381
  20.7 0.1 collective-permute-start.8
  20.8 0.1 collective-permute-start.6
  20.8 5.0 %collective-permute-start.9 = (bf16[64,640]{1,0:T(8,128)(2,1)S(1)}, bf16[64,640]{1,0:T(8,128)(2,1)S(1)}, u32[]{:S(2)}, u32[]{:S(2)}) collective-permute-start(bf16[64,640]{1,0:T(8,128)(2,1)S(1)} %get-tuple-element.30), channel_id=1, source_target_pairs={{0,3},{1,2},{2,1},{3,0},{4,7},{5,6},{6,5},{7,4},{8,11},{9,10},{10,... | collective-permute-start | bytes 245768 | tf_op jit(solution)/shard_map/ppermute | solution.py:27
  25.8 0.0 collective-permute-start.7
  25.8 0.0 collective-permute-start.5
  25.8 2.2 %collective-permute-done.9.full_cross = bf16[64,640]{1,0:T(8,128)(2,1)S(1)} collective-permute-done((bf16[64,640]{1,0:T(8,128)(2,1)S(1)}, bf16[64,640]{1,0:T(8,128)(2,1)S(1)}, u32[]{:S(2)}, u32[]{:S(2)}) %collective-permute-start.9) | collective-permute-done | bytes 81952 | tf_op jit(solution)/shard_map/ppermute | solution.py:27
  28.0 3.5 %collective-permute-done.7.mix_cross = bf16[64,640]{1,0:T(8,128)(2,1)S(1)} collective-permute-done((bf16[64,640]{1,0:T(8,128)(2,1)S(1)}, bf16[64,640]{1,0:T(8,128)(2,1)S(1)}, u32[]{:S(2)}, u32[]{:S(2)}) %collective-permute-start.7) | collective-permute-done | bytes 81952 | tf_op jit(solution)/shard_map/ppermute | solution.py:27
  31.5 0.0 collective-permute-done.5.mix_core
  31.5 0.0 collective-permute-done.8.full_same
  31.5 0.0 collective-permute-done.6.mix_same
  31.5 0.9 %shard_map.87 = f32[4,32,640]{2,1,0:T(8,128)} custom-call(s32[1]{0:T(128)} %copy.9.anchor_ref, f32[4,32,640]{2,1,0:T(8,128)S(1)} %get-tuple-element.18.latent, bf16[4,32,640]{2,1,0:T(8,128)(2,1)S(1)} %get-tuple-element.19.lowered, s32[1,64]{1,0:T(1,128)S(1)} %get-tuple-element.20.counts, bf16[136,640]{1,0:T(8,128)(2,1)S(1)} %collective-permute-done.load, ...), custom_call_target="tpu_custom_call" | custom-call | tf_op jit(solution)/shard_map/pallas_call | solution.py:398
  (5 shorter events, 0.0 us)
Async XLA Ops:
  1.1 9.6 %collective-permute-start.2 = (bf16[4,32,640]{2,1,0:T(8,128)(2,1)S(1)}, bf16[4,32,640]{2,1,0:T(8,128)(2,1)S(1)}, u32[]{:S(2)}, u32[]{:S(2)}) collective-permute-start(bf16[4,32,640]{2,1,0:T(8,128)(2,1)S(1)} %get-tuple-element.19.lowered), channel_id=1, source_target_pairs={{0,2},{1,3},{2,0},{3,1},{4,6},{5,7},{6,4},{7,5},{8,10},{9,11},{10,... | collective-permute-start | bytes 491528 | tf_op jit(solution)/shard_map/ppermute | solution.py:27
  3.2 8.8 %collective-permute-start = (bf16[136,640]{1,0:T(8,128)(2,1)S(1)}, bf16[136,640]{1,0:T(8,128)(2,1)S(1)}, u32[]{:S(2)}, u32[]{:S(2)}) collective-permute-start(bf16[136,640]{1,0:T(8,128)(2,1)S(1)} %get-tuple-element.21), channel_id=1, source_target_pairs={{0,12},{1,13},{2,6},{3,7},{4,0},{5,1},{6,10},{7,11},{8,4},{9,5},{1... | collective-permute-start | bytes 522248 | tf_op jit(solution)/shard_map/ppermute | solution.py:27
  10.6 2.3 %collective-permute-start.3 = (bf16[4,32,640]{2,1,0:T(8,128)(2,1)S(1)}, bf16[4,32,640]{2,1,0:T(8,128)(2,1)S(1)}, u32[]{:S(2)}, u32[]{:S(2)}) collective-permute-start(bf16[4,32,640]{2,1,0:T(8,128)(2,1)S(1)} %collective-permute-done.2.full), channel_id=1, source_target_pairs={{0,1},{1,0},{2,3},{3,2},{4,5},{5,4},{6,7},{7,6},{8,9},{9,8},{10,11... | collective-permute-start | bytes 491528 | tf_op jit(solution)/shard_map/ppermute | solution.py:27
  12.1 1.5 %collective-permute-start.1 = (bf16[4,32,640]{2,1,0:T(8,128)(2,1)S(1)}, bf16[4,32,640]{2,1,0:T(8,128)(2,1)S(1)}, u32[]{:S(2)}, u32[]{:S(2)}) collective-permute-start(bf16[4,32,640]{2,1,0:T(8,128)(2,1)S(1)} %broadcast_select_fusion.mix), channel_id=1, source_target_pairs={{0,1},{1,0},{2,3},{3,2},{4,5},{5,4},{6,7},{7,6},{8,9},{9,8},{10,11... | collective-permute-start | bytes 491528 | tf_op jit(solution)/shard_map/ppermute | solution.py:27
  17.0 1.7 %collective-permute-start.4 = (bf16[256,640]{1,0:T(8,128)(2,1)S(1)}, bf16[256,640]{1,0:T(8,128)(2,1)S(1)}, u32[]{:S(2)}, u32[]{:S(2)}) collective-permute-start(bf16[256,640]{1,0:T(8,128)(2,1)S(1)} %shard_map.84.own), channel_id=1, source_target_pairs={{0,1},{1,0},{2,3},{3,2},{4,5},{5,4},{6,7},{7,6},{8,9},{9,8},{10,11... | collective-permute-start | bytes 983048 | tf_op jit(solution)/shard_map/ppermute | solution.py:27
  20.7 10.8 %collective-permute-start.8 = (bf16[72,640]{1,0:T(8,128)(2,1)S(1)}, bf16[72,640]{1,0:T(8,128)(2,1)S(1)}, u32[]{:S(2)}, u32[]{:S(2)}) collective-permute-start(bf16[72,640]{1,0:T(8,128)(2,1)S(1)} %get-tuple-element.29), channel_id=1, source_target_pairs={{0,2},{1,3},{2,0},{3,1},{4,6},{5,7},{6,4},{7,5},{8,10},{9,11},{10,... | collective-permute-start | bytes 276488 | tf_op jit(solution)/shard_map/ppermute | solution.py:27
  20.8 10.7 %collective-permute-start.6 = (bf16[72,640]{1,0:T(8,128)(2,1)S(1)}, bf16[72,640]{1,0:T(8,128)(2,1)S(1)}, u32[]{:S(2)}, u32[]{:S(2)}) collective-permute-start(bf16[72,640]{1,0:T(8,128)(2,1)S(1)} %get-tuple-element.27.mix_own), channel_id=1, source_target_pairs={{0,4},{1,5},{2,14},{3,15},{4,8},{5,9},{6,2},{7,3},{8,12},{9,13},{1... | collective-permute-start | bytes 276488 | tf_op jit(solution)/shard_map/ppermute | solution.py:27
  20.8 7.2 %collective-permute-start.9 = (bf16[64,640]{1,0:T(8,128)(2,1)S(1)}, bf16[64,640]{1,0:T(8,128)(2,1)S(1)}, u32[]{:S(2)}, u32[]{:S(2)}) collective-permute-start(bf16[64,640]{1,0:T(8,128)(2,1)S(1)} %get-tuple-element.30), channel_id=1, source_target_pairs={{0,3},{1,2},{2,1},{3,0},{4,7},{5,6},{6,5},{7,4},{8,11},{9,10},{10,... | collective-permute-start | bytes 245768 | tf_op jit(solution)/shard_map/ppermute | solution.py:27
  25.8 5.7 %collective-permute-start.7 = (bf16[64,640]{1,0:T(8,128)(2,1)S(1)}, bf16[64,640]{1,0:T(8,128)(2,1)S(1)}, u32[]{:S(2)}, u32[]{:S(2)}) collective-permute-start(bf16[64,640]{1,0:T(8,128)(2,1)S(1)} %get-tuple-element.28), channel_id=1, source_target_pairs={{0,5},{1,4},{2,15},{3,14},{4,9},{5,8},{6,3},{7,2},{8,13},{9,12},{1... | collective-permute-start | bytes 245768 | tf_op jit(solution)/shard_map/ppermute | solution.py:27
  25.8 5.7 %collective-permute-start.5 = (bf16[64,640]{1,0:T(8,128)(2,1)S(1)}, bf16[64,640]{1,0:T(8,128)(2,1)S(1)}, u32[]{:S(2)}, u32[]{:S(2)}) collective-permute-start(bf16[64,640]{1,0:T(8,128)(2,1)S(1)} %get-tuple-element.28), channel_id=1, source_target_pairs={{0,1},{1,0},{2,3},{3,2},{4,5},{5,4},{6,7},{7,6},{8,9},{9,8},{10,11... | collective-permute-start | bytes 245768 | tf_op jit(solution)/shard_map/ppermute | solution.py:27

commit v6 on v5

--- a/solution.py
+++ b/solution.py
@@ -15,6 +15,8 @@
 SMEM = pl.BlockSpec(memory_space=pltpu.SMEM)
 F32 = jnp.float32
 BF16 = jnp.bfloat16
+OWN_SCALE = math.sqrt(0.7 / 0.5)
+JOIN_SCALE = math.sqrt(0.3) - math.sqrt(0.7 / 0.5) * math.sqrt(0.5)
 
 
 def moved(value, step, flip):
@@ -109,20 +111,50 @@
 TAIL = 8
 
 
+LANES = 128
+
+
+def stacked(pixels, channels, tail=0):
+    return jax.ShapeDtypeStruct((pixels * channels // LANES + tail, LANES), BF16)
+
+
 def packed(rows, columns, outs, tail=0):
-    return jax.ShapeDtypeStruct((rows * columns // 2 + tail, 2 * outs), BF16)
+    return stacked(rows * columns // 2, 2 * outs, tail)
+
+
+def spans(row, rows, columns, outs):
+    half, whole = rows // 2, outs // LANES
+    second, rest = row // half, outs % LANES
+    tiles = [(second * (whole + 1) + t, 0, t * LANES, LANES) for t in range(whole)]
+    tiles.append((whole, second * rest, whole * LANES, rest))
+    start = (row % half) * columns
+    return [
+        (
+            slice(tile * half * columns + start, tile * half * columns + start + columns),
+            slice(lane, lane + size),
+            slice(channel, channel + size),
+        )
+        for tile, lane, channel, size in tiles
+    ]
 
 
 def put(ref, row, rows, value):
-    half, outs, columns = rows // 2, ref.shape[1] // 2, value.shape[0]
-    spot = (row % half) * columns
-    ref[spot : spot + columns, (row // half) * outs : (row // half + 1) * outs] = value
-
-
-def get(ref, row, rows, columns):
-    half, outs = rows // 2, ref.shape[1] // 2
-    spot = (row % half) * columns
-    return ref[spot : spot + columns, (row // half) * outs : (row // half + 1) * outs]
+    for place, lanes, part in spans(row, rows, *value.shape):
+        ref[place, lanes] = value[:, part]
+
+
+def get(ref, row, rows, columns, outs):
+    return jnp.concatenate([ref[place, lanes] for place, lanes, _ in spans(row, rows, columns, outs)], axis=1)
+
+
+def row_of(ref, row, rows, columns, channels):
+    return jnp.concatenate(
+        [
+            ref[pl.ds(pl.multiple_of(t * rows * columns + row * columns, columns), columns)]
+            for t in range(channels // LANES)
+        ],
+        axis=1,
+    )
 
 
 def half_of(row, outs, core):
@@ -130,7 +162,7 @@
 
 
 def lower_kernel(latent, counts, lowered, load, held, counted, sems):
-    rows, cols, _ = latent.shape
+    rows, cols, channels = latent.shape
     copies = [pltpu.make_async_copy(latent.at[row], held.at[row], sems.at[row]) for row in range(rows)]
     copies.append(pltpu.make_async_copy(counts, counted, sems.at[rows]))
     for copy in copies:
@@ -138,13 +170,15 @@
     for row in range(rows):
         copies[row].wait()
         value = held[row].astype(BF16)
-        lowered[row] = value
-        load[row * cols : (row + 1) * cols] = value
+        for t in range(channels // LANES):
+            start = t * rows * cols + row * cols
+            for ref in (lowered, load):
+                ref[start : start + cols] = value[:, t * LANES : (t + 1) * LANES]
     copies[rows].wait()
-    put_counts(load, rows * cols, counted[...].astype(F32))
-
-
-def ready_kernel(size, w_one, w_two, gain_one, gain_two, time_bias, w, w_next, table, gather, spread, one_in, two_in, bias_in, small_sems, sems):
+    put_counts(load, counted[...].astype(F32))
+
+
+def ready_kernel(size, held, w_one, w_two, gain_one, gain_two, time_bias, w, w_next, table, gather, spread, base, one_in, two_in, bias_in, small_sems, sems):
     small = [
         pltpu.make_async_copy(source, target, small_sems.at[i])
         for i, (source, target) in enumerate(((gain_one, one_in), (gain_two, two_in), (time_bias, bias_in)))
@@ -154,6 +188,9 @@
     for copy in small + copies:
         copy.start()
     group_tables(size, gather, spread)
+    for row in range(held.shape[0]):
+        value = held[local_row(core, row, held.shape[0])]
+        base[row] = OWN_SCALE * value + JOIN_SCALE * value.astype(BF16).astype(F32)
     table[...] = jnp.zeros_like(table)
     for i, ref in enumerate((one_in, two_in, bias_in)):
         small[i].wait()
@@ -162,15 +199,13 @@
         copy.wait()
 
 
-def put_counts(ref, start, row):
-    tail = ref.shape[0] - start
-    room = ref.shape[1] - row.shape[1]
-    wide = jnp.concatenate([row, jnp.zeros((1, room), F32)], axis=1)
-    ref[start:] = jnp.broadcast_to(wide, (tail, ref.shape[1])).astype(BF16)
-
-
-def get_counts(ref, start, columns):
-    return ref[start : start + 8].astype(F32)[:1, :columns]
+def put_counts(ref, row):
+    wide = jnp.concatenate([row, jnp.zeros((1, LANES - row.shape[1]), F32)], axis=1)
+    ref[ref.shape[0] - TAIL :] = jnp.broadcast_to(wide, (TAIL, LANES)).astype(BF16)
+
+
+def get_counts(ref, columns):
+    return ref[ref.shape[0] - TAIL :].astype(F32)[:1, :columns]
 
 
 def by_column(values, anchor, columns):
@@ -180,16 +215,16 @@
     return jnp.sum(jnp.where(picked, values, 0.0), axis=1, keepdims=True)
 
 
-def first_kernel(size, mix, mix_other, full, full_other, edges, w, table, gather, spread, out, frame, acc, hidden):
+def first_kernel(size, rows, mix, mix_other, full, full_other, edges, w, table, gather, spread, out, frame, acc, hidden):
     core = lax.axis_index("rows")
-    rows, half_cols, channels = mix.shape
-    columns, height, outs = 2 * half_cols, 2 * rows, out.shape[1] // 2
+    height, columns, outs = hidden.shape
+    half_cols, channels = columns // 2, frame.shape[2]
     count = height * columns * size
     clear_edges(frame)
     summed = jnp.zeros((1, channels), F32)
     squares = jnp.zeros((1, channels), F32)
     for ref in (mix, mix_other, full, full_other):
-        v = ref[...].astype(F32).reshape(rows * half_cols, channels)
+        v = row_of(ref, 0, 1, rows * half_cols, channels).astype(F32)
         summed += jnp.sum(v, axis=0, keepdims=True)
         squares += jnp.sum(v * v, axis=0, keepdims=True)
     mean, scale = group_scale(summed, squares, count, gather, spread)
@@ -198,7 +233,7 @@
     def normed(row):
         local = local_row(core, row % rows, rows)
         for ref, col in ((mix, 0), (full, half_cols)) if row < rows else ((mix_other, 0), (full_other, half_cols)):
-            v = ref[local].astype(F32)
+            v = row_of(ref, local, rows, half_cols, channels).astype(F32)
             frame[1 + row, col : col + half_cols] = silu_of_twice((v - mean) * scale).astype(BF16)
 
     for row in range(height):
@@ -225,10 +260,10 @@
 def near_kernel(own, w, edges, part, frame, acc):
     core = lax.axis_index("rows")
     height, columns, near = frame.shape[0] - 2, frame.shape[1], frame.shape[2]
-    outs = own.shape[1] // 2
+    outs = part.shape[2]
     clear_edges(frame)
     for row in range(height):
-        mine = get(own, row, height, columns)
+        mine = get(own, row, height, columns, outs)
         frame[1 + row] = jnp.where(core == 0, mine[:, :near], mine[:, outs - near :])
     nine_taps(frame, w, acc, core * (2 * outs - near))
     for row in range(height):
@@ -239,20 +274,20 @@
     core = lax.axis_index("rows")
     odd = (lax.axis_index("blk") & 1) == 1
     height, columns = frame.shape[0] - 2, frame.shape[1]
-    outs = own.shape[1] // 2
+    outs = near_part.shape[2]
     near = near_channels(outs)
     rows, half_cols = height // 2, columns // 2
     clear_edges(frame)
     for row in range(height):
-        mine = get(own, row, height, columns)
-        theirs = get(other, height - 1 - row, height, columns)
+        mine = get(own, row, height, columns, outs)
+        theirs = get(other, height - 1 - row, height, columns, outs)
         frame[1 + row] = jnp.where(
             core == 0,
             jnp.concatenate([mine[:, near:], theirs], axis=1),
             jnp.concatenate([theirs, mine[:, : outs - near]], axis=1),
         )
     nine_taps(frame, w, acc, (1 - core) * near)
-    own_row = jnp.where(odd, get_counts(load, rows * half_cols, columns), counts[...].astype(F32))
+    own_row = jnp.where(odd, get_counts(load, columns), counts[...].astype(F32))
     part = jnp.broadcast_to(by_column(own_row, anchor_ref[0], columns), (columns, outs))
     for row in range(height):
         value = ((joined_taps(acc, row, columns, outs, edges) + near_part[row]) * part).astype(BF16)
@@ -261,28 +296,25 @@
         put(mix, spot, rows, value[:half_cols])
         put(full, spot, rows, value[half_cols:])
     for out in (mix_same, full_same):
-        put_counts(out, rows * half_cols // 2, own_row)
-
-
-def last_kernel(anchor_ref, latent, lowered, counts, load, mix_own, mix_core, mix_same, mix_cross, full_same, full_cross, out, done, sems):
+        put_counts(out, own_row)
+
+
+def last_kernel(anchor_ref, base, counts, load, mix_own, mix_core, mix_same, mix_cross, full_same, full_cross, out, done, sems):
     core = lax.axis_index("rows")
     odd = (lax.axis_index("blk") & 1) == 1
     anchor = anchor_ref[0]
-    rows, cols, outs = latent.shape[0], latent.shape[1], latent.shape[2] // 2
+    rows, cols, outs = base.shape[0], base.shape[1], base.shape[2] // 2
     late = lax.broadcasted_iota(jnp.int32, (cols, outs), 0) >= anchor
     keep = late ^ odd
-    tail = rows * cols // 2
-    own_row = jnp.where(odd, get_counts(load, rows * cols, 2 * cols), counts[...].astype(F32))
-    always = by_column(get_counts(full_same, tail, 2 * cols), anchor, 2 * cols)[cols:]
+    own_row = jnp.where(odd, get_counts(load, 2 * cols), counts[...].astype(F32))
+    always = by_column(get_counts(full_same, 2 * cols), anchor, 2 * cols)[cols:]
     ours = by_column(own_row, anchor, 2 * cols)[:cols]
-    theirs = by_column(get_counts(mix_same, tail, 2 * cols), anchor, 2 * cols)[:cols]
+    theirs = by_column(get_counts(mix_same, 2 * cols), anchor, 2 * cols)[:cols]
     weight = always + jnp.where(keep[:, :1], ours, theirs)
-    own_scale = math.sqrt(0.7 / 0.5)
-    join_scale = math.sqrt(0.3) - math.sqrt(0.7 / 0.5) * math.sqrt(0.5)
-    part = join_scale / weight
+    part = JOIN_SCALE / weight
 
     def summed(row, own, far, full):
-        own, far, full = (get(ref, row, rows, cols).astype(F32) for ref in (own, far, full))
+        own, far, full = (get(ref, row, rows, cols, outs).astype(F32) for ref in (own, far, full))
         return jnp.where(keep, own, far) + full
 
     copies = []
@@ -290,11 +322,10 @@
         local = local_row(core, row, rows)
         same = summed(row, mix_own, mix_same, full_same)
         cross = summed(row, mix_core, mix_cross, full_cross)
-        base = own_scale * latent[local] + join_scale * lowered[local].astype(F32)
         both = jnp.where(
             core == 0, jnp.concatenate([same, cross], axis=1), jnp.concatenate([cross, same], axis=1)
         )
-        done[row] = base + part * both
+        done[row] = base[row] + part * both
         copies.append(pltpu.make_async_copy(done.at[row], out.at[local], sems.at[row]))
         copies[row].start()
     for copy in copies:
@@ -317,8 +348,8 @@
     lowered, load, held, counted = pl.pallas_call(
         lower_kernel,
         out_shape=(
-            jax.ShapeDtypeStruct(latent.shape, BF16),
-            jax.ShapeDtypeStruct((rows * stride + TAIL, channels), BF16),
+            stacked(rows * stride, channels),
+            stacked(rows * stride, channels, TAIL),
             jax.ShapeDtypeStruct(latent.shape, F32),
             jax.ShapeDtypeStruct(counts.shape, counts.dtype),
         ),
@@ -329,7 +360,7 @@
     )(in_hbm(latent), in_hbm(counts))
     weights = jax.ShapeDtypeStruct((3, 3 * outs, channels), BF16)
     vector = pltpu.VMEM((channels,), F32)
-    w_first, w_next, table, gather, spread = pl.pallas_call(
+    w_first, w_next, table, gather, spread, base = pl.pallas_call(
         functools.partial(ready_kernel, size),
         out_shape=(
             weights,
@@ -337,30 +368,33 @@
             jax.ShapeDtypeStruct((8, channels), F32),
             jax.ShapeDtypeStruct((channels, 128), BF16),
             jax.ShapeDtypeStruct((128, channels), BF16),
+            jax.ShapeDtypeStruct(latent.shape, F32),
         ),
-        in_specs=[HBM] * 5,
-        out_specs=(VMEM,) * 5,
+        in_specs=[VMEM] + [HBM] * 5,
+        out_specs=(VMEM,) * 6,
         scratch_shapes=[vector] * 3 + [pltpu.SemaphoreType.DMA((3,)), pltpu.SemaphoreType.DMA((2, 18))],
         compiler_params=PARAMS,
-    )(*[in_hbm(v) for v in (conv_one, conv_two, gain_one, gain_two, time_bias)])
+    )(held, *[in_hbm(v) for v in (conv_one, conv_two, gain_one, gain_two, time_bias)])
     full = moved(lowered, lambda b: b ^ 1, 0)
     load = moved(load, lambda b: b + 2 if b % 2 else b - 2, 0)
-    beyond = load[: rows * stride].reshape(latent.shape)
+    beyond = load[: lowered.shape[0]]
+    blocks = (-1, stride, LANES)
     spot = lax.broadcasted_iota(jnp.int32, (3, columns, 128), 1)
     kind = lax.broadcasted_iota(jnp.int32, (3, columns, 128), 0)
     cut = jnp.where(kind == 0, spot == anchor, spot == jnp.where(anchor == 0, columns, anchor) - 1)
     edges = jnp.where(jnp.where(kind == 2, spot < anchor, cut), 0.0, 1.0)
 
     full_other = moved(full, lambda b: b, 1)
-    col = lax.broadcasted_iota(jnp.int32, lowered.shape, 1)
-    mix = jnp.where((col >= anchor) ^ odd, lowered, beyond)
+    lowered_blocks, beyond = lowered.reshape(blocks), beyond.reshape(blocks)
+    col = lax.broadcasted_iota(jnp.int32, beyond.shape, 1)
+    mix = jnp.where((col >= anchor) ^ odd, lowered_blocks, beyond).reshape(lowered.shape)
     mix_other = moved(mix, lambda b: b, 1)
 
     frame = pltpu.VMEM((height + 2, columns, channels), BF16)
     acc = pltpu.VMEM((height * columns, 3 * outs), F32)
     result = pltpu.VMEM((height, columns, outs), F32)
     own = pl.pallas_call(
-        functools.partial(first_kernel, size),
+        functools.partial(first_kernel, size, rows),
         out_shape=packed(height, columns, outs),
         in_specs=[VMEM] * 9,
         out_specs=VMEM,
@@ -398,11 +432,11 @@
     return pl.pallas_call(
         last_kernel,
         out_shape=jax.ShapeDtypeStruct(latent.shape, F32),
-        in_specs=[SMEM] + [VMEM] * 10,
+        in_specs=[SMEM] + [VMEM] * 9,
         out_specs=HBM,
         scratch_shapes=[pltpu.VMEM(latent.shape, F32), pltpu.SemaphoreType.DMA((rows,))],
         compiler_params=PARAMS,
-    )(offset, held, lowered, counted, load, mix_same, got_core, got_mix_same, got_mix_cross, got_full_same, got_full_cross)
+    )(offset, base, counted, load, mix_same, got_core, got_mix_same, got_mix_cross, got_full_same, got_full_cross)
 
 
 def solution(mesh):

time: 32.6 us -> 32.4 us (level)
  no operation moved by 1% of the time
where the time goes in v6:
time: 32.4 us; the launch traced here: 32.3 us
  Pallas kernels  12.1 us (37%)
  starting transfers between devices  11.9 us (37%)
  waiting for transfers between devices  7.12 us (22%)
  between operations  0.76 us (2%)
    ppermute x10, starting transfers between devices, moved(): return lax.ppermute(value, ('blk', 'rows'), pairs)  11.9 us
    ppermute x10, waiting for transfers between devices, moved(): return lax.ppermute(value, ('blk', 'rows'), pairs)  7.12 us
    pallas_call x1, Pallas kernels, per_device(): pl.pallas_call(functools.partial(first_kernel, size, rows), out_shape=pac...  3.53 us
    pallas_call x1, Pallas kernels, per_device(): pl.pallas_call(functools.partial(ready_kernel, size), out_shape=(weights,...  3.42 us
    pallas_call x1, Pallas kernels, per_device(): pl.pallas_call(second_kernel, out_shape=(marked, plain, marked, plain), i...  1.86 us
    pallas_call x1, Pallas kernels, per_device(): pl.pallas_call(near_kernel, out_shape=jax.ShapeDtypeStruct((height, colum...  1.3 us
    pallas_call x1, Pallas kernels, per_device(): pl.pallas_call(lower_kernel, out_shape=(stacked(rows * stride, channels),...  1.06 us
    pallas_call x1, Pallas kernels, per_device(): pl.pallas_call(last_kernel, out_shape=jax.ShapeDtypeStruct(latent.shape,...  0.95 us
  transfers between devices with their start and end apart: 10, of which 5 were waited for; matrix products, arithmetic and copies ran while one was open for 1% of the time, Pallas kernels for 15%

profile of v6, /device:TPU:1, one launch (start us, length us, event | category | flops | bytes accessed | tf_op | source)
XLA Modules:
  0.0 32.3 jit_solution(17359216913688284649)
XLA Ops:
  0.0 1.1 %shard_map.82 = (bf16[640,128]{1,0:T(8,128)(2,1)S(1)}, bf16[648,128]{1,0:T(8,128)(2,1)S(1)}, f32[4,32,640]{2,1,0:T(8,128)S(1)}, s32[1,64]{1,0:T(1,128)S(1)}) custom-call(f32[4,32,640]{2,1,0:T(8,128)} %latent.1, s32[1,64]{1,0:T(1,128)} %counts.1), custom_call_target="tpu_custom_call" | custom-call | tf_op jit(solution)/shard_map/pallas_call | solution.py:348
  1.1 2.1 %collective-permute-start.2 = (bf16[640,128]{1,0:T(8,128)(2,1)S(1)}, bf16[640,128]{1,0:T(8,128)(2,1)S(1)}, u32[]{:S(2)}, u32[]{:S(2)}) collective-permute-start(bf16[640,128]{1,0:T(8,128)(2,1)S(1)} %get-tuple-element.23), channel_id=1, source_target_pairs={{0,2},{1,3},{2,0},{3,1},{4,6},{5,7},{6,4},{7,5},{8,10},{9,11},{10,... | collective-permute-start | bytes 491528 | tf_op jit(solution)/shard_map/ppermute | solution.py:29
  3.2 3.3 %collective-permute-start = (bf16[648,128]{1,0:T(8,128)(2,1)S(1)}, bf16[648,128]{1,0:T(8,128)(2,1)S(1)}, u32[]{:S(2)}, u32[]{:S(2)}) collective-permute-start(bf16[648,128]{1,0:T(8,128)(2,1)S(1)} %get-tuple-element.22), channel_id=1, source_target_pairs={{0,12},{1,13},{2,6},{3,7},{4,0},{5,1},{6,10},{7,11},{8,4},{9,5},{1... | collective-permute-start | bytes 497672 | tf_op jit(solution)/shard_map/ppermute | solution.py:29
  7.2 0.1 xor.14
  7.3 3.4 %shard_map.83 = (bf16[3,960,640]{2,1,0:T(8,128)(2,1)S(1)}, bf16[3,960,640]{2,1,0:T(8,128)(2,1)S(1)}, f32[8,640]{1,0:T(8,128)S(1)}, bf16[640,128]{1,0:T(8,128)(2,...) custom-call(f32[4,32,640]{2,1,0:T(8,128)S(1)} %get-tuple-element.19.held, ...), custom_call_target="tpu_custom_call" | custom-call | tf_op jit(solution)/shard_map/pallas_call | solution.py:363
  10.7 0.0 collective-permute-done.2.full
  10.7 1.3 %collective-permute-start.3 = (bf16[640,128]{1,0:T(8,128)(2,1)S(1)}, bf16[640,128]{1,0:T(8,128)(2,1)S(1)}, u32[]{:S(2)}, u32[]{:S(2)}) collective-permute-start(bf16[640,128]{1,0:T(8,128)(2,1)S(1)} %collective-permute-done.2.full), channel_id=1, source_target_pairs={{0,1},{1,0},{2,3},{3,2},{4,5},{5,4},{6,7},{7,6},{8,9},{9,8},{10,11... | collective-permute-start | bytes 491528 | tf_op jit(solution)/shard_map/ppermute | solution.py:29
  12.0 0.0 collective-permute-done.load
  12.0 0.2 slice_select_fusion.mix
  12.2 0.1 collective-permute-start.1
  12.3 0.1 select_select_fusion.edges
  12.4 0.7 %collective-permute-done.3.full_other = bf16[640,128]{1,0:T(8,128)(2,1)S(1)} collective-permute-done((bf16[640,128]{1,0:T(8,128)(2,1)S(1)}, bf16[640,128]{1,0:T(8,128)(2,1)S(1)}, u32[]{:S(2)}, u32[]{:S(2)}) %collective-permute-start.3) | collective-permute-done | bytes 163872 | tf_op jit(solution)/shard_map/ppermute | solution.py:29
  13.1 0.6 %collective-permute-done.1.mix_other = bf16[640,128]{1,0:T(8,128)(2,1)S(1)} collective-permute-done((bf16[640,128]{1,0:T(8,128)(2,1)S(1)}, bf16[640,128]{1,0:T(8,128)(2,1)S(1)}, u32[]{:S(2)}, u32[]{:S(2)}) %collective-permute-start.1) | collective-permute-done | bytes 163872 | tf_op jit(solution)/shard_map/ppermute | solution.py:29
  13.7 3.5 %shard_map.84.own = bf16[1280,128]{1,0:T(8,128)(2,1)S(1)} custom-call(bf16[640,128]{1,0:T(8,128)(2,1)S(1)} %slice_select_fusion.mix, bf16[640,128]{1,0:T(8,128)(2,1)S(1)} %collective-permute-done.1.mix_other, bf16[640,128]{1,0:T(8,128)(2,1)S(1)} %collective-permute-done.2.full, bf16[640,128]{1,0:T(8,128)(2,1)S(1)} %collective-permute-done.3.full_other, ...), custom_call_target="tpu_custom_call" | custom-call | tf_op jit(solution)/shard_map/pallas_call | solution.py:396
  17.2 0.2 collective-permute-start.4
  17.4 1.3 %shard_map.85.near_part = f32[8,64,320]{2,1,0:T(8,128)S(1)} custom-call(bf16[1280,128]{1,0:T(8,128)(2,1)S(1)} %shard_map.84.own, bf16[3,960,640]{2,1,0:T(8,128)(2,1)S(1)} %get-tuple-element.28.w, f32[3,64,128]{2,1,0:T(8,128)S(1)} %select_select_fusion.edges), custom_call_target="tpu_custom_call" | custom-call | tf_op jit(solution)/shard_map/pallas_call | solution.py:406
  18.7 0.2 collective-permute-done.4.other
  18.9 1.9 %shard_map.86 = (bf16[328,128]{1,0:T(8,128)(2,1)S(1)}, bf16[320,128]{1,0:T(8,128)(2,1)S(1)}, bf16[328,128]{1,0:T(8,128)(2,1)S(1)}, bf16[320,128]{1,0:T(8,128)(2,1)S(1)}) custom-call(s32[1]{0:T(128)} %copy.9.anchor_ref, bf16[1280,128]{1,0:T(8,128)(2,1)S(1)} %shard_map.84.own, bf16[1280,128]{1,0:T(8,128)(2,1)S(1)} %collective-permute-done.4.other, ...), custom_call_target="tpu_custom_call" | custom-call | tf_op jit(solution)/shard_map/pallas_call | solution.py:415
  20.8 0.1 collective-permute-start.8
  20.8 0.1 collective-permute-start.6
  20.9 4.7 %collective-permute-start.9 = (bf16[320,128]{1,0:T(8,128)(2,1)S(1)}, bf16[320,128]{1,0:T(8,128)(2,1)S(1)}, u32[]{:S(2)}, u32[]{:S(2)}) collective-permute-start(bf16[320,128]{1,0:T(8,128)(2,1)S(1)} %get-tuple-element.32), channel_id=1, source_target_pairs={{0,3},{1,2},{2,1},{3,0},{4,7},{5,6},{6,5},{7,4},{8,11},{9,10},{10,... | collective-permute-start | bytes 245768 | tf_op jit(solution)/shard_map/ppermute | solution.py:29
  25.6 0.0 collective-permute-start.7
  25.6 0.0 collective-permute-start.5
  25.6 2.1 %collective-permute-done.9.full_cross = bf16[320,128]{1,0:T(8,128)(2,1)S(1)} collective-permute-done((bf16[320,128]{1,0:T(8,128)(2,1)S(1)}, bf16[320,128]{1,0:T(8,128)(2,1)S(1)}, u32[]{:S(2)}, u32[]{:S(2)}) %collective-permute-start.9) | collective-permute-done | bytes 81952 | tf_op jit(solution)/shard_map/ppermute | solution.py:29
  27.7 3.5 %collective-permute-done.7.mix_cross = bf16[320,128]{1,0:T(8,128)(2,1)S(1)} collective-permute-done((bf16[320,128]{1,0:T(8,128)(2,1)S(1)}, bf16[320,128]{1,0:T(8,128)(2,1)S(1)}, u32[]{:S(2)}, u32[]{:S(2)}) %collective-permute-start.7) | collective-permute-done | bytes 81952 | tf_op jit(solution)/shard_map/ppermute | solution.py:29
  31.3 0.0 collective-permute-done.5.mix_core
  31.3 0.0 collective-permute-done.8.full_same
  31.3 0.0 collective-permute-done.6.mix_same
  31.3 1.0 %shard_map.87 = f32[4,32,640]{2,1,0:T(8,128)} custom-call(s32[1]{0:T(128)} %copy.9.anchor_ref, f32[4,32,640]{2,1,0:T(8,128)S(1)} %get-tuple-element.20.base, s32[1,64]{1,0:T(1,128)S(1)} %get-tuple-element.21.counts, bf16[648,128]{1,0:T(8,128)(2,1)S(1)} %collective-permute-done.load, bf16[328,128]{1,0:T(8,128)(2,1)S(1)} %get-tuple-element.29.mix_own, ...), custom_call_target="tpu_custom_call" | custom-call | tf_op jit(solution)/shard_map/pallas_call | solution.py:432
  (5 shorter events, 0.0 us)
Async XLA Ops:
  1.1 9.7 %collective-permute-start.2 = (bf16[640,128]{1,0:T(8,128)(2,1)S(1)}, bf16[640,128]{1,0:T(8,128)(2,1)S(1)}, u32[]{:S(2)}, u32[]{:S(2)}) collective-permute-start(bf16[640,128]{1,0:T(8,128)(2,1)S(1)} %get-tuple-element.23), channel_id=1, source_target_pairs={{0,2},{1,3},{2,0},{3,1},{4,6},{5,7},{6,4},{7,5},{8,10},{9,11},{10,... | collective-permute-start | bytes 491528 | tf_op jit(solution)/shard_map/ppermute | solution.py:29
  3.2 8.9 %collective-permute-start = (bf16[648,128]{1,0:T(8,128)(2,1)S(1)}, bf16[648,128]{1,0:T(8,128)(2,1)S(1)}, u32[]{:S(2)}, u32[]{:S(2)}) collective-permute-start(bf16[648,128]{1,0:T(8,128)(2,1)S(1)} %get-tuple-element.22), channel_id=1, source_target_pairs={{0,12},{1,13},{2,6},{3,7},{4,0},{5,1},{6,10},{7,11},{8,4},{9,5},{1... | collective-permute-start | bytes 497672 | tf_op jit(solution)/shard_map/ppermute | solution.py:29
  10.7 2.3 %collective-permute-start.3 = (bf16[640,128]{1,0:T(8,128)(2,1)S(1)}, bf16[640,128]{1,0:T(8,128)(2,1)S(1)}, u32[]{:S(2)}, u32[]{:S(2)}) collective-permute-start(bf16[640,128]{1,0:T(8,128)(2,1)S(1)} %collective-permute-done.2.full), channel_id=1, source_target_pairs={{0,1},{1,0},{2,3},{3,2},{4,5},{5,4},{6,7},{7,6},{8,9},{9,8},{10,11... | collective-permute-start | bytes 491528 | tf_op jit(solution)/shard_map/ppermute | solution.py:29
  12.2 1.5 %collective-permute-start.1 = (bf16[640,128]{1,0:T(8,128)(2,1)S(1)}, bf16[640,128]{1,0:T(8,128)(2,1)S(1)}, u32[]{:S(2)}, u32[]{:S(2)}) collective-permute-start(bf16[640,128]{1,0:T(8,128)(2,1)S(1)} %slice_select_fusion.mix), channel_id=1, source_target_pairs={{0,1},{1,0},{2,3},{3,2},{4,5},{5,4},{6,7},{7,6},{8,9},{9,8},{10,11... | collective-permute-start | bytes 491528 | tf_op jit(solution)/shard_map/ppermute | solution.py:29
  17.2 1.7 %collective-permute-start.4 = (bf16[1280,128]{1,0:T(8,128)(2,1)S(1)}, bf16[1280,128]{1,0:T(8,128)(2,1)S(1)}, u32[]{:S(2)}, u32[]{:S(2)}) collective-permute-start(bf16[1280,128]{1,0:T(8,128)(2,1)S(1)} %shard_map.84.own), channel_id=1, source_target_pairs={{0,1},{1,0},{2,3},{3,2},{4,5},{5,4},{6,7},{7,6},{8,9},{9,8},{10,11... | collective-permute-start | bytes 983048 | tf_op jit(solution)/shard_map/ppermute | solution.py:29
  20.8 10.5 %collective-permute-start.8 = (bf16[328,128]{1,0:T(8,128)(2,1)S(1)}, bf16[328,128]{1,0:T(8,128)(2,1)S(1)}, u32[]{:S(2)}, u32[]{:S(2)}) collective-permute-start(bf16[328,128]{1,0:T(8,128)(2,1)S(1)} %get-tuple-element.31), channel_id=1, source_target_pairs={{0,2},{1,3},{2,0},{3,1},{4,6},{5,7},{6,4},{7,5},{8,10},{9,11},{10,... | collective-permute-start | bytes 251912 | tf_op jit(solution)/shard_map/ppermute | solution.py:29
  20.8 10.5 %collective-permute-start.6 = (bf16[328,128]{1,0:T(8,128)(2,1)S(1)}, bf16[328,128]{1,0:T(8,128)(2,1)S(1)}, u32[]{:S(2)}, u32[]{:S(2)}) collective-permute-start(bf16[328,128]{1,0:T(8,128)(2,1)S(1)} %get-tuple-element.29.mix_own), channel_id=1, source_target_pairs={{0,4},{1,5},{2,14},{3,15},{4,8},{5,9},{6,2},{7,3},{8,12},{9,13},{1... | collective-permute-start | bytes 251912 | tf_op jit(solution)/shard_map/ppermute | solution.py:29
  20.9 6.9 %collective-permute-start.9 = (bf16[320,128]{1,0:T(8,128)(2,1)S(1)}, bf16[320,128]{1,0:T(8,128)(2,1)S(1)}, u32[]{:S(2)}, u32[]{:S(2)}) collective-permute-start(bf16[320,128]{1,0:T(8,128)(2,1)S(1)} %get-tuple-element.32), channel_id=1, source_target_pairs={{0,3},{1,2},{2,1},{3,0},{4,7},{5,6},{6,5},{7,4},{8,11},{9,10},{10,... | collective-permute-start | bytes 245768 | tf_op jit(solution)/shard_map/ppermute | solution.py:29
  25.6 5.7 %collective-permute-start.7 = (bf16[320,128]{1,0:T(8,128)(2,1)S(1)}, bf16[320,128]{1,0:T(8,128)(2,1)S(1)}, u32[]{:S(2)}, u32[]{:S(2)}) collective-permute-start(bf16[320,128]{1,0:T(8,128)(2,1)S(1)} %get-tuple-element.30), channel_id=1, source_target_pairs={{0,5},{1,4},{2,15},{3,14},{4,9},{5,8},{6,3},{7,2},{8,13},{9,12},{1... | collective-permute-start | bytes 245768 | tf_op jit(solution)/shard_map/ppermute | solution.py:29
  25.6 5.7 %collective-permute-start.5 = (bf16[320,128]{1,0:T(8,128)(2,1)S(1)}, bf16[320,128]{1,0:T(8,128)(2,1)S(1)}, u32[]{:S(2)}, u32[]{:S(2)}) collective-permute-start(bf16[320,128]{1,0:T(8,128)(2,1)S(1)} %get-tuple-element.30), channel_id=1, source_target_pairs={{0,1},{1,0},{2,3},{3,2},{4,5},{5,4},{6,7},{7,6},{8,9},{9,8},{10,11... | collective-permute-start | bytes 245768 | tf_op jit(solution)/shard_map/ppermute | solution.py:29

commit v7 on v6

--- a/solution.py
+++ b/solution.py
@@ -178,7 +178,7 @@
     put_counts(load, counted[...].astype(F32))
 
 
-def ready_kernel(size, held, w_one, w_two, gain_one, gain_two, time_bias, w, w_next, table, gather, spread, base, one_in, two_in, bias_in, small_sems, sems):
+def ready_kernel(size, anchor_ref, held, w_one, w_two, gain_one, gain_two, time_bias, w, w_next, table, gather, spread, base, edges, one_in, two_in, bias_in, small_sems, sems):
     small = [
         pltpu.make_async_copy(source, target, small_sems.at[i])
         for i, (source, target) in enumerate(((gain_one, one_in), (gain_two, two_in), (time_bias, bias_in)))
@@ -188,6 +188,10 @@
     for copy in small + copies:
         copy.start()
     group_tables(size, gather, spread)
+    anchor, (columns, lanes) = anchor_ref[0], edges.shape[1:]
+    col = lax.broadcasted_iota(jnp.int32, (columns, lanes), 0)
+    for i, cut in enumerate((anchor, jnp.where(anchor == 0, columns, anchor) - 1)):
+        edges[i] = jnp.where(col == cut, 0.0, 1.0)
     for row in range(held.shape[0]):
         value = held[local_row(core, row, held.shape[0])]
         base[row] = OWN_SCALE * value + JOIN_SCALE * value.astype(BF16).astype(F32)
@@ -360,7 +364,7 @@
     )(in_hbm(latent), in_hbm(counts))
     weights = jax.ShapeDtypeStruct((3, 3 * outs, channels), BF16)
     vector = pltpu.VMEM((channels,), F32)
-    w_first, w_next, table, gather, spread, base = pl.pallas_call(
+    w_first, w_next, table, gather, spread, base, edges = pl.pallas_call(
         functools.partial(ready_kernel, size),
         out_shape=(
             weights,
@@ -369,21 +373,17 @@
             jax.ShapeDtypeStruct((channels, 128), BF16),
             jax.ShapeDtypeStruct((128, channels), BF16),
             jax.ShapeDtypeStruct(latent.shape, F32),
+            jax.ShapeDtypeStruct((2, columns, LANES), F32),
         ),
-        in_specs=[VMEM] + [HBM] * 5,
-        out_specs=(VMEM,) * 6,
+        in_specs=[SMEM, VMEM] + [HBM] * 5,
+        out_specs=(VMEM,) * 7,
         scratch_shapes=[vector] * 3 + [pltpu.SemaphoreType.DMA((3,)), pltpu.SemaphoreType.DMA((2, 18))],
         compiler_params=PARAMS,
-    )(held, *[in_hbm(v) for v in (conv_one, conv_two, gain_one, gain_two, time_bias)])
+    )(offset, held, *[in_hbm(v) for v in (conv_one, conv_two, gain_one, gain_two, time_bias)])
     full = moved(lowered, lambda b: b ^ 1, 0)
     load = moved(load, lambda b: b + 2 if b % 2 else b - 2, 0)
     beyond = load[: lowered.shape[0]]
     blocks = (-1, stride, LANES)
-    spot = lax.broadcasted_iota(jnp.int32, (3, columns, 128), 1)
-    kind = lax.broadcasted_iota(jnp.int32, (3, columns, 128), 0)
-    cut = jnp.where(kind == 0, spot == anchor, spot == jnp.where(anchor == 0, columns, anchor) - 1)
-    edges = jnp.where(jnp.where(kind == 2, spot < anchor, cut), 0.0, 1.0)
-
     full_other = moved(full, lambda b: b, 1)
     lowered_blocks, beyond = lowered.reshape(blocks), beyond.reshape(blocks)
     col = lax.broadcasted_iota(jnp.int32, beyond.shape, 1)

time: 32.4 us -> 33.5 us (1.034)
  waiting for transfers between devices: 7.12 us -> 9.39 us
  starting transfers between devices: 11.9 us -> 10.8 us
    ppermute x10, waiting for transfers between devices: 7.12 us -> 9.39 us  [moved(): return lax.ppermute(value, ('blk', 'rows'), pairs)]
    ppermute x10, starting transfers between devices: 11.9 us -> 10.8 us  [moved(): return lax.ppermute(value, ('blk', 'rows'), pairs)]
  transfers between devices with their start and end apart: 10 -> 10, of which waited for: 5 -> 3; matrix products, arithmetic and copies ran while one was open for 1% -> 1% of each run, Pallas kernels for 15% -> 14%
where the time goes in v7:
time: 33.5 us; the launch traced here: 33.3 us
  Pallas kernels  12.2 us (36%)
  starting transfers between devices  10.8 us (32%)
  waiting for transfers between devices  9.39 us (28%)
  between operations  0.75 us (2%)
    ppermute x10, starting transfers between devices, moved(): return lax.ppermute(value, ('blk', 'rows'), pairs)  10.8 us
    ppermute x10, waiting for transfers between devices, moved(): return lax.ppermute(value, ('blk', 'rows'), pairs)  9.39 us
    pallas_call x1, Pallas kernels, per_device(): pl.pallas_call(functools.partial(first_kernel, size, rows), out_shape=pac...  3.55 us
    pallas_call x1, Pallas kernels, per_device(): pl.pallas_call(functools.partial(ready_kernel, size), out_shape=(weights,...  3.43 us
    pallas_call x1, Pallas kernels, per_device(): pl.pallas_call(second_kernel, out_shape=(marked, plain, marked, plain), i...  1.87 us
    pallas_call x1, Pallas kernels, per_device(): pl.pallas_call(near_kernel, out_shape=jax.ShapeDtypeStruct((height, colum...  1.31 us
    pallas_call x1, Pallas kernels, per_device(): pl.pallas_call(lower_kernel, out_shape=(stacked(rows * stride, channels),...  1.06 us
    pallas_call x1, Pallas kernels, per_device(): pl.pallas_call(last_kernel, out_shape=jax.ShapeDtypeStruct(latent.shape,...  0.95 us
  transfers between devices with their start and end apart: 10, of which 3 were waited for; matrix products, arithmetic and copies ran while one was open for 1% of the time, Pallas kernels for 14%

profile of v7, /device:TPU:1, one launch (start us, length us, event | category | flops | bytes accessed | tf_op | source)
XLA Modules:
  0.0 33.3 jit_solution(17177146803692518086)
XLA Ops:
  0.0 1.1 %shard_map.82 = (bf16[640,128]{1,0:T(8,128)(2,1)S(1)}, bf16[648,128]{1,0:T(8,128)(2,1)S(1)}, f32[4,32,640]{2,1,0:T(8,128)S(1)}, s32[1,64]{1,0:T(1,128)S(1)}) custom-call(f32[4,32,640]{2,1,0:T(8,128)} %latent.1, s32[1,64]{1,0:T(1,128)} %counts.1), custom_call_target="tpu_custom_call" | custom-call | tf_op jit(solution)/shard_map/pallas_call | solution.py:352
  1.1 4.2 %collective-permute-start = (bf16[648,128]{1,0:T(8,128)(2,1)S(1)}, bf16[648,128]{1,0:T(8,128)(2,1)S(1)}, u32[]{:S(2)}, u32[]{:S(2)}) collective-permute-start(bf16[648,128]{1,0:T(8,128)(2,1)S(1)} %get-tuple-element.23), channel_id=1, source_target_pairs={{0,12},{1,13},{2,6},{3,7},{4,0},{5,1},{6,10},{7,11},{8,4},{9,5},{1... | collective-permute-start | bytes 497672 | tf_op jit(solution)/shard_map/ppermute | solution.py:29
  5.3 0.0 collective-permute-start.2
  5.9 0.1 xor.14
  6.0 4.0 %collective-permute-done.2.full = bf16[640,128]{1,0:T(8,128)(2,1)S(1)} collective-permute-done((bf16[640,128]{1,0:T(8,128)(2,1)S(1)}, bf16[640,128]{1,0:T(8,128)(2,1)S(1)}, u32[]{:S(2)}, u32[]{:S(2)}) %collective-permute-start.2) | collective-permute-done | bytes 163872 | tf_op jit(solution)/shard_map/ppermute | solution.py:29
  10.1 1.8 %collective-permute-start.3 = (bf16[640,128]{1,0:T(8,128)(2,1)S(1)}, bf16[640,128]{1,0:T(8,128)(2,1)S(1)}, u32[]{:S(2)}, u32[]{:S(2)}) collective-permute-start(bf16[640,128]{1,0:T(8,128)(2,1)S(1)} %collective-permute-done.2.full), channel_id=1, source_target_pairs={{0,1},{1,0},{2,3},{3,2},{4,5},{5,4},{6,7},{7,6},{8,9},{9,8},{10,11... | collective-permute-start | bytes 491528 | tf_op jit(solution)/shard_map/ppermute | solution.py:29
  11.9 0.0 collective-permute-done.load
  11.9 0.2 slice_select_fusion.mix
  12.0 0.1 collective-permute-start.1
  12.1 3.4 %shard_map.83 = (bf16[3,960,640]{2,1,0:T(8,128)(2,1)S(1)}, bf16[3,960,640]{2,1,0:T(8,128)(2,1)S(1)}, f32[8,640]{1,0:T(8,128)S(1)}, bf16[640,128]{1,0:T(8,128)(2,...) custom-call(s32[1]{0:T(128)} %copy.9.anchor_ref, ...), custom_call_target="tpu_custom_call" | custom-call | tf_op jit(solution)/shard_map/pallas_call | solution.py:367
  15.6 0.0 collective-permute-done.3.full_other
  15.6 0.0 collective-permute-done.1.mix_other
  15.6 3.6 %shard_map.84.own = bf16[1280,128]{1,0:T(8,128)(2,1)S(1)} custom-call(bf16[640,128]{1,0:T(8,128)(2,1)S(1)} %slice_select_fusion.mix, bf16[640,128]{1,0:T(8,128)(2,1)S(1)} %collective-permute-done.1.mix_other, bf16[640,128]{1,0:T(8,128)(2,1)S(1)} %collective-permute-done.2.full, bf16[640,128]{1,0:T(8,128)(2,1)S(1)} %collective-permute-done.3.full_other, ...), custom_call_target="tpu_custom_call" | custom-call | tf_op jit(solution)/shard_map/pallas_call | solution.py:396
  19.1 0.6 %collective-permute-start.4 = (bf16[1280,128]{1,0:T(8,128)(2,1)S(1)}, bf16[1280,128]{1,0:T(8,128)(2,1)S(1)}, u32[]{:S(2)}, u32[]{:S(2)}) collective-permute-start(bf16[1280,128]{1,0:T(8,128)(2,1)S(1)} %shard_map.84.own), channel_id=1, source_target_pairs={{0,1},{1,0},{2,3},{3,2},{4,5},{5,4},{6,7},{7,6},{8,9},{9,8},{10,11... | collective-permute-start | bytes 983048 | tf_op jit(solution)/shard_map/ppermute | solution.py:29
  19.7 1.3 %shard_map.85.near_part = f32[8,64,320]{2,1,0:T(8,128)S(1)} custom-call(bf16[1280,128]{1,0:T(8,128)(2,1)S(1)} %shard_map.84.own, bf16[3,960,640]{2,1,0:T(8,128)(2,1)S(1)} %get-tuple-element.30.w, f32[2,64,128]{2,1,0:T(8,128)S(1)} %get-tuple-element.25.edges), custom_call_target="tpu_custom_call" | custom-call | tf_op jit(solution)/shard_map/pallas_call | solution.py:406
  21.0 0.0 collective-permute-done.4.other
  21.0 1.9 %shard_map.86 = (bf16[328,128]{1,0:T(8,128)(2,1)S(1)}, bf16[320,128]{1,0:T(8,128)(2,1)S(1)}, bf16[328,128]{1,0:T(8,128)(2,1)S(1)}, bf16[320,128]{1,0:T(8,128)(2,1)S(1)}) custom-call(s32[1]{0:T(128)} %copy.9.anchor_ref, bf16[1280,128]{1,0:T(8,128)(2,1)S(1)} %shard_map.84.own, bf16[1280,128]{1,0:T(8,128)(2,1)S(1)} %collective-permute-done.4.other, ...), custom_call_target="tpu_custom_call" | custom-call | tf_op jit(solution)/shard_map/pallas_call | solution.py:415
  22.9 0.1 collective-permute-start.8
  23.0 0.5 %collective-permute-start.6 = (bf16[328,128]{1,0:T(8,128)(2,1)S(1)}, bf16[328,128]{1,0:T(8,128)(2,1)S(1)}, u32[]{:S(2)}, u32[]{:S(2)}) collective-permute-start(bf16[328,128]{1,0:T(8,128)(2,1)S(1)} %get-tuple-element.31.mix_own), channel_id=1, source_target_pairs={{0,4},{1,5},{2,14},{3,15},{4,8},{5,9},{6,2},{7,3},{8,12},{9,13},{1... | collective-permute-start | bytes 251912 | tf_op jit(solution)/shard_map/ppermute | solution.py:29
  23.4 3.3 %collective-permute-start.9 = (bf16[320,128]{1,0:T(8,128)(2,1)S(1)}, bf16[320,128]{1,0:T(8,128)(2,1)S(1)}, u32[]{:S(2)}, u32[]{:S(2)}) collective-permute-start(bf16[320,128]{1,0:T(8,128)(2,1)S(1)} %get-tuple-element.34), channel_id=1, source_target_pairs={{0,3},{1,2},{2,1},{3,0},{4,7},{5,6},{6,5},{7,4},{8,11},{9,10},{10,... | collective-permute-start | bytes 245768 | tf_op jit(solution)/shard_map/ppermute | solution.py:29
  26.7 0.0 collective-permute-start.7
  26.7 0.3 collective-permute-start.5
  27.0 2.2 %collective-permute-done.9.full_cross = bf16[320,128]{1,0:T(8,128)(2,1)S(1)} collective-permute-done((bf16[320,128]{1,0:T(8,128)(2,1)S(1)}, bf16[320,128]{1,0:T(8,128)(2,1)S(1)}, u32[]{:S(2)}, u32[]{:S(2)}) %collective-permute-start.9) | collective-permute-done | bytes 81952 | tf_op jit(solution)/shard_map/ppermute | solution.py:29
  29.2 3.1 %collective-permute-done.7.mix_cross = bf16[320,128]{1,0:T(8,128)(2,1)S(1)} collective-permute-done((bf16[320,128]{1,0:T(8,128)(2,1)S(1)}, bf16[320,128]{1,0:T(8,128)(2,1)S(1)}, u32[]{:S(2)}, u32[]{:S(2)}) %collective-permute-start.7) | collective-permute-done | bytes 81952 | tf_op jit(solution)/shard_map/ppermute | solution.py:29
  32.3 0.0 collective-permute-done.5.mix_core
  32.3 0.0 collective-permute-done.8.full_same
  32.3 0.0 collective-permute-done.6.mix_same
  32.4 1.0 %shard_map.87 = f32[4,32,640]{2,1,0:T(8,128)} custom-call(s32[1]{0:T(128)} %copy.9.anchor_ref, f32[4,32,640]{2,1,0:T(8,128)S(1)} %get-tuple-element.21.base, s32[1,64]{1,0:T(1,128)S(1)} %get-tuple-element.22.counts, bf16[648,128]{1,0:T(8,128)(2,1)S(1)} %collective-permute-done.load, bf16[328,128]{1,0:T(8,128)(2,1)S(1)} %get-tuple-element.31.mix_own, ...), custom_call_target="tpu_custom_call" | custom-call | tf_op jit(solution)/shard_map/pallas_call | solution.py:432
  (2 shorter events, 0.0 us)
Async XLA Ops:
  1.1 10.8 %collective-permute-start = (bf16[648,128]{1,0:T(8,128)(2,1)S(1)}, bf16[648,128]{1,0:T(8,128)(2,1)S(1)}, u32[]{:S(2)}, u32[]{:S(2)}) collective-permute-start(bf16[648,128]{1,0:T(8,128)(2,1)S(1)} %get-tuple-element.23), channel_id=1, source_target_pairs={{0,12},{1,13},{2,6},{3,7},{4,0},{5,1},{6,10},{7,11},{8,4},{9,5},{1... | collective-permute-start | bytes 497672 | tf_op jit(solution)/shard_map/ppermute | solution.py:29
  5.3 4.8 %collective-permute-start.2 = (bf16[640,128]{1,0:T(8,128)(2,1)S(1)}, bf16[640,128]{1,0:T(8,128)(2,1)S(1)}, u32[]{:S(2)}, u32[]{:S(2)}) collective-permute-start(bf16[640,128]{1,0:T(8,128)(2,1)S(1)} %get-tuple-element.24), channel_id=1, source_target_pairs={{0,2},{1,3},{2,0},{3,1},{4,6},{5,7},{6,4},{7,5},{8,10},{9,11},{10,... | collective-permute-start | bytes 491528 | tf_op jit(solution)/shard_map/ppermute | solution.py:29
  10.1 5.5 %collective-permute-start.3 = (bf16[640,128]{1,0:T(8,128)(2,1)S(1)}, bf16[640,128]{1,0:T(8,128)(2,1)S(1)}, u32[]{:S(2)}, u32[]{:S(2)}) collective-permute-start(bf16[640,128]{1,0:T(8,128)(2,1)S(1)} %collective-permute-done.2.full), channel_id=1, source_target_pairs={{0,1},{1,0},{2,3},{3,2},{4,5},{5,4},{6,7},{7,6},{8,9},{9,8},{10,11... | collective-permute-start | bytes 491528 | tf_op jit(solution)/shard_map/ppermute | solution.py:29
  12.0 3.5 %collective-permute-start.1 = (bf16[640,128]{1,0:T(8,128)(2,1)S(1)}, bf16[640,128]{1,0:T(8,128)(2,1)S(1)}, u32[]{:S(2)}, u32[]{:S(2)}) collective-permute-start(bf16[640,128]{1,0:T(8,128)(2,1)S(1)} %slice_select_fusion.mix), channel_id=1, source_target_pairs={{0,1},{1,0},{2,3},{3,2},{4,5},{5,4},{6,7},{7,6},{8,9},{9,8},{10,11... | collective-permute-start | bytes 491528 | tf_op jit(solution)/shard_map/ppermute | solution.py:29
  19.1 1.9 %collective-permute-start.4 = (bf16[1280,128]{1,0:T(8,128)(2,1)S(1)}, bf16[1280,128]{1,0:T(8,128)(2,1)S(1)}, u32[]{:S(2)}, u32[]{:S(2)}) collective-permute-start(bf16[1280,128]{1,0:T(8,128)(2,1)S(1)} %shard_map.84.own), channel_id=1, source_target_pairs={{0,1},{1,0},{2,3},{3,2},{4,5},{5,4},{6,7},{7,6},{8,9},{9,8},{10,11... | collective-permute-start | bytes 983048 | tf_op jit(solution)/shard_map/ppermute | solution.py:29
  22.9 9.5 %collective-permute-start.8 = (bf16[328,128]{1,0:T(8,128)(2,1)S(1)}, bf16[328,128]{1,0:T(8,128)(2,1)S(1)}, u32[]{:S(2)}, u32[]{:S(2)}) collective-permute-start(bf16[328,128]{1,0:T(8,128)(2,1)S(1)} %get-tuple-element.33), channel_id=1, source_target_pairs={{0,2},{1,3},{2,0},{3,1},{4,6},{5,7},{6,4},{7,5},{8,10},{9,11},{10,... | collective-permute-start | bytes 251912 | tf_op jit(solution)/shard_map/ppermute | solution.py:29
  23.0 9.4 %collective-permute-start.6 = (bf16[328,128]{1,0:T(8,128)(2,1)S(1)}, bf16[328,128]{1,0:T(8,128)(2,1)S(1)}, u32[]{:S(2)}, u32[]{:S(2)}) collective-permute-start(bf16[328,128]{1,0:T(8,128)(2,1)S(1)} %get-tuple-element.31.mix_own), channel_id=1, source_target_pairs={{0,4},{1,5},{2,14},{3,15},{4,8},{5,9},{6,2},{7,3},{8,12},{9,13},{1... | collective-permute-start | bytes 251912 | tf_op jit(solution)/shard_map/ppermute | solution.py:29
  23.4 5.8 %collective-permute-start.9 = (bf16[320,128]{1,0:T(8,128)(2,1)S(1)}, bf16[320,128]{1,0:T(8,128)(2,1)S(1)}, u32[]{:S(2)}, u32[]{:S(2)}) collective-permute-start(bf16[320,128]{1,0:T(8,128)(2,1)S(1)} %get-tuple-element.34), channel_id=1, source_target_pairs={{0,3},{1,2},{2,1},{3,0},{4,7},{5,6},{6,5},{7,4},{8,11},{9,10},{10,... | collective-permute-start | bytes 245768 | tf_op jit(solution)/shard_map/ppermute | solution.py:29
  26.7 5.7 %collective-permute-start.7 = (bf16[320,128]{1,0:T(8,128)(2,1)S(1)}, bf16[320,128]{1,0:T(8,128)(2,1)S(1)}, u32[]{:S(2)}, u32[]{:S(2)}) collective-permute-start(bf16[320,128]{1,0:T(8,128)(2,1)S(1)} %get-tuple-element.32), channel_id=1, source_target_pairs={{0,5},{1,4},{2,15},{3,14},{4,9},{5,8},{6,3},{7,2},{8,13},{9,12},{1... | collective-permute-start | bytes 245768 | tf_op jit(solution)/shard_map/ppermute | solution.py:29
  26.7 5.7 %collective-permute-start.5 = (bf16[320,128]{1,0:T(8,128)(2,1)S(1)}, bf16[320,128]{1,0:T(8,128)(2,1)S(1)}, u32[]{:S(2)}, u32[]{:S(2)}) collective-permute-start(bf16[320,128]{1,0:T(8,128)(2,1)S(1)} %get-tuple-element.32), channel_id=1, source_target_pairs={{0,1},{1,0},{2,3},{3,2},{4,5},{5,4},{6,7},{7,6},{8,9},{9,8},{10,11... | collective-permute-start | bytes 245768 | tf_op jit(solution)/shard_map/ppermute | solution.py:29
